TPU v7x, 32 devices: a whole 2x2x4 slice. The times are simulated.
32 devices in a mesh: row: 4 (over y, x), col: 8 (over z, core).
Axes of the slice: x: 2, y: 2, z: 4, core: 2. Of those that a mesh axis runs over, the one named last changes fastest.
Arguments:
- currents: float32 [2, 64, 16384], P(None, None, ('row', 'col')), may hold values from -6 to 6
- projection: bfloat16 [64, 64, 16384], P(None, None, ('row', 'col')), may hold values from -0.75 to 0.75
- near_blocks: bfloat16 [4, 64, 64, 16384], P(None, None, None, ('row', 'col')), may hold values from -0.375 to 0.375
- partners: int32 [4, 16384], P(None, ('row', 'col')), may hold values from 0 to 8, as said below
- shifts: int32 [2, 16384], P(None, ('row', 'col')), may hold values from -2 to 2, as said below
- green: float32 [2048, 2048], P(('row', 'col')), may hold values from 0.5 to 2.5, as said below
Outputs:
- product: float32 [2, 64, 16384], P(None, None, ('row', 'col'))
Inputs may be any that keep to these rules, and one draw needn't show every extreme that they name: shifts[0, n] is 0 or more for elements of the first element row and 0 or less for those of the last; shifts[1, n] likewise for the first and last element columns, so that every stencil lies inside the grid. partners[0, n] is 4, the element itself; for k of 1 or more the codes of one element are distinct, each 3 (dr + 1) + (dc + 1) for offsets dr, dc in -1, 0, 1, not both 0, of an element that lies inside the array. green is the spectrum of a real even kernel: green[ky, kx] = green[(2048 - ky) % 2048, kx] = green[ky, (2048 - kx) % 2048].
All inputs are finite; a program needn't handle non-finite values.
Results may differ from a plain program's by a relative error of at most 0.0038.
Values may be sent and summed in bfloat16 or wider, within the bound.
No kernel may reach another device: no remote copies, remote signals or barrier semaphores. Data moves between devices by JAX's collectives and lax.ppermute only.
A program may use at most 192 MiB of HBM per device.

v0:
```python
import functools
import math

import jax
import jax.numpy as jnp
import numpy as np
from jax import lax
from jax.experimental import pallas as pl
from jax.experimental.pallas import tpu as pltpu
from jax.sharding import PartitionSpec as P

BASIS = 64
STEN = 8
PITCH = 8
HALO = 2
NEIGH = 4
RHS = 2
ER = 32
EC = 16


def extended_2(block, sides, width):
    for axis, dim in sides:
        count = lax.axis_size(axis)
        forward = [(i, i + 1) for i in range(count - 1)]
        backward = [(target, source) for source, target in forward]
        low = lax.ppermute(
            lax.slice_in_dim(block, block.shape[dim] - width, None, axis=dim), axis, forward
        )
        high = lax.ppermute(lax.slice_in_dim(block, 0, width, axis=dim), axis, backward)
        block = jnp.concatenate([low, block, high], axis=dim)
    return block


def angle_table(first_size, second_size, modulus, direction):
    left_index = jnp.arange(first_size, dtype=jnp.int32)
    right_index = jnp.arange(second_size, dtype=jnp.int32)
    turn_count = left_index[:, None] * right_index[None, :] % modulus
    angles = turn_count.astype(jnp.float32) * (2.0 * math.pi / modulus)
    return (jnp.cos(angles), direction * jnp.sin(angles))


def complex_apply(real_part, imag_part, cosine, sine_table, pattern):
    highest = lax.Precision.HIGHEST
    out_real = jnp.einsum(pattern, real_part, cosine, precision=highest)
    out_imag = jnp.einsum(pattern, real_part, sine_table, precision=highest)
    if imag_part is not None:
        out_real = out_real - jnp.einsum(pattern, imag_part, sine_table, precision=highest)
        out_imag = out_imag + jnp.einsum(pattern, imag_part, cosine, precision=highest)
    return (out_real, out_imag)


def transform_last(real_part, imag_part, length, count_in, count_out, direction):
    leading = real_part.shape[:-1]
    inner_size = 128
    outer_size = length // inner_size
    rows_in = count_in // inner_size
    kept_count = count_out // outer_size
    shaped_real = real_part.reshape(leading + (rows_in, inner_size))
    shaped_imag = None
    if imag_part is not None:
        shaped_imag = imag_part.reshape(leading + (rows_in, inner_size))
    cosine, sine_table = angle_table(rows_in, outer_size, outer_size, direction)
    first_real, first_imag = complex_apply(
        shaped_real, shaped_imag, cosine, sine_table, "...ab,ak->...kb"
    )
    twist_cos, twist_sin = angle_table(outer_size, inner_size, length, direction)
    turned_real = first_real * twist_cos - first_imag * twist_sin
    turned_imag = first_real * twist_sin + first_imag * twist_cos
    cosine, sine_table = angle_table(inner_size, kept_count, inner_size, direction)
    last_real, last_imag = complex_apply(
        turned_real, turned_imag, cosine, sine_table, "...kb,bj->...jk"
    )
    out_shape = leading + (kept_count * outer_size,)
    return (last_real.reshape(out_shape), last_imag.reshape(out_shape))


def place_shifted(blocks, amount, dim_index):
    new_shape = list(blocks.shape)
    new_shape[dim_index] = new_shape[dim_index] + 2 * HALO
    result = jnp.zeros(tuple(new_shape), blocks.dtype)
    for offset in range(-HALO, HALO + 1):
        widths = [(0, 0)] * blocks.ndim
        widths[dim_index] = (HALO + offset, HALO - offset)
        result = jnp.where(amount == offset, jnp.pad(blocks, widths), result)
    return result


def pick_shifted(windows, amount, dim_index):
    new_shape = list(windows.shape)
    new_shape[dim_index] = STEN
    result = jnp.zeros(tuple(new_shape), windows.dtype)
    for offset in range(-HALO, HALO + 1):
        piece = lax.slice_in_dim(windows, HALO + offset, HALO + offset + STEN, axis=dim_index)
        result = jnp.where(amount == offset, piece, result)
    return result


def intersection_add(framed, dim_index):
    element_count = framed.shape[dim_index]
    window_size = framed.shape[dim_index + 1]
    head_part = lax.slice_in_dim(framed, 0, PITCH, axis=dim_index + 1)
    tail_part = lax.slice_in_dim(framed, PITCH, window_size, axis=dim_index + 1)
    widths = [(0, 0)] * framed.ndim
    widths[dim_index + 1] = (0, 2 * PITCH - window_size)
    tail_part = jnp.pad(tail_part, widths)
    merged = framed.shape[:dim_index] + (element_count * PITCH,) + framed.shape[dim_index + 2 :]
    head_part = head_part.reshape(merged)
    tail_part = tail_part.reshape(merged)
    front_pad = [(0, 0)] * len(merged)
    front_pad[dim_index] = (0, PITCH)
    back_pad = [(0, 0)] * len(merged)
    back_pad[dim_index] = (PITCH, 0)
    summed = jnp.pad(head_part, front_pad) + jnp.pad(tail_part, back_pad)
    return lax.slice_in_dim(summed, 0, element_count * PITCH + 2 * HALO, axis=dim_index)


def cut_windows(field, dim_index):
    element_count = (field.shape[dim_index] - 2 * HALO) // PITCH
    widths = [(0, 0)] * field.ndim
    widths[dim_index] = (0, PITCH - 2 * HALO)
    extended = jnp.pad(field, widths)
    split_shape = field.shape[:dim_index] + (element_count, PITCH) + field.shape[dim_index + 1 :]
    head_part = lax.slice_in_dim(extended, 0, element_count * PITCH, axis=dim_index).reshape(
        split_shape
    )
    tail_part = lax.slice_in_dim(
        extended, PITCH, PITCH + element_count * PITCH, axis=dim_index
    ).reshape(split_shape)
    tail_part = lax.slice_in_dim(tail_part, 0, 2 * HALO, axis=dim_index + 1)
    return jnp.concatenate([head_part, tail_part], axis=dim_index + 1)


def fold_margin(padded, dim_index):
    full_size = padded.shape[dim_index]
    inner_size = full_size - 4 * HALO
    core_part = lax.slice_in_dim(padded, 2 * HALO, 2 * HALO + inner_size, axis=dim_index)
    upper_part = lax.slice_in_dim(padded, 0, HALO, axis=dim_index)
    lower_part = lax.slice_in_dim(padded, full_size - HALO, full_size, axis=dim_index)
    upper_pad = [(0, 0)] * padded.ndim
    upper_pad[dim_index] = (0, inner_size - HALO)
    lower_pad = [(0, 0)] * padded.ndim
    lower_pad[dim_index] = (inner_size - HALO, 0)
    return core_part + jnp.pad(upper_part, upper_pad) + jnp.pad(lower_part, lower_pad)


def shards_general(currents, projection, near_blocks, partners, shifts, green):
    row_count = lax.axis_size("row")
    col_count = lax.axis_size("col")
    device_count = row_count * col_count
    elements = ER * EC
    cur_half = currents.astype(jnp.bfloat16)
    spread = extended_2(cur_half.reshape(RHS, BASIS, ER, EC), (("row", 2), ("col", 3)), 1)
    views = []
    for symbol in range(9):
        row_start = symbol // 3
        col_start = symbol % 3
        views.append(
            spread[:, :, row_start : row_start + ER, col_start : col_start + EC].reshape(
                RHS, BASIS, elements
            )
        )
    picked = []
    for neighbour_slot in range(NEIGH):
        chosen = jnp.zeros((RHS, BASIS, elements), jnp.bfloat16)
        for symbol in range(9):
            chosen = jnp.where(partners[neighbour_slot] == symbol, views[symbol], chosen)
        picked.append(chosen)
    near_term = jnp.einsum(
        "kabn,kqbn->qan", near_blocks, jnp.stack(picked), preferred_element_type=jnp.float32
    )
    stencil = jnp.einsum("sbn,qbn->qsn", projection, cur_half, preferred_element_type=jnp.float32)
    blocks = stencil.reshape(RHS, STEN, STEN, elements)
    framed = place_shifted(place_shifted(blocks, shifts[0], 1), shifts[1], 2)
    window_size = STEN + 2 * HALO
    framed = framed.reshape(RHS, window_size, window_size, ER, EC).transpose(0, 3, 1, 4, 2)
    extended = intersection_add(intersection_add(framed, 1), 2)
    padded = extended_2(extended, (("row", 1), ("col", 2)), HALO)
    charges = fold_margin(fold_margin(padded, 1), 2)
    slab = lax.all_to_all(charges, "col", split_axis=1, concat_axis=2, tiled=True)
    slab_rows = slab.shape[1]
    width_cols = slab.shape[2]
    length_cols = 2 * width_cols
    block_cols = length_cols // device_count
    grid_rows = slab_rows * device_count
    length_rows = 2 * grid_rows
    fwd_real, fwd_imag = transform_last(slab, None, length_cols, width_cols, length_cols, -1.0)
    out_real = fwd_real.reshape(RHS, slab_rows, device_count, block_cols)
    out_imag = fwd_imag.reshape(RHS, slab_rows, device_count, block_cols)
    arrived = (
        lax.all_to_all(out_real, ("row", "col"), split_axis=2, concat_axis=2, tiled=True),
        lax.all_to_all(out_imag, ("row", "col"), split_axis=2, concat_axis=2, tiled=True),
    )
    col_real = arrived[0].transpose(0, 3, 2, 1).reshape(RHS, block_cols, grid_rows)
    col_imag = arrived[1].transpose(0, 3, 2, 1).reshape(RHS, block_cols, grid_rows)
    spec_real, spec_imag = transform_last(
        col_real, col_imag, length_rows, grid_rows, length_rows, -1.0
    )
    spec_real = spec_real * green
    spec_imag = spec_imag * green
    back_real, back_imag = transform_last(
        spec_real, spec_imag, length_rows, length_rows, grid_rows, 1.0
    )
    send_real = back_real.reshape(RHS, block_cols, device_count, slab_rows)
    send_imag = back_imag.reshape(RHS, block_cols, device_count, slab_rows)
    returned = (
        lax.all_to_all(send_real, ("row", "col"), split_axis=2, concat_axis=2, tiled=True),
        lax.all_to_all(send_imag, ("row", "col"), split_axis=2, concat_axis=2, tiled=True),
    )
    rows_real = returned[0].transpose(0, 3, 2, 1).reshape(RHS, slab_rows, length_cols)
    rows_imag = returned[1].transpose(0, 3, 2, 1).reshape(RHS, slab_rows, length_cols)
    final_real, final_imag = transform_last(
        rows_real, rows_imag, length_cols, length_cols, width_cols, 1.0
    )
    potential_slab = final_real * (1.0 / (length_rows * length_cols))
    potential = lax.all_to_all(potential_slab, "col", split_axis=2, concat_axis=1, tiled=True)
    rimmed = extended_2(potential, (("row", 1), ("col", 2)), HALO)
    windows = cut_windows(cut_windows(rimmed, 1), 3)
    windows = windows.transpose(0, 2, 4, 1, 3).reshape(RHS, window_size, window_size, elements)
    samples = pick_shifted(pick_shifted(windows, shifts[0], 1), shifts[1], 2).reshape(
        RHS, STEN * STEN, elements
    )
    sample_high = samples.astype(jnp.bfloat16)
    sample_low = (samples - sample_high.astype(jnp.float32)).astype(jnp.bfloat16)
    far_term = jnp.einsum(
        "sbn,qsn->qbn", projection, sample_high, preferred_element_type=jnp.float32
    )
    far_term = far_term + jnp.einsum(
        "sbn,qsn->qbn", projection, sample_low, preferred_element_type=jnp.float32
    )
    return far_term + near_term


LANES = 128
SUB = 8
TILES = 4
GROUPS = 9
PARITY_ORDER = (0, 2, 4, 6, 1, 3, 5, 7)


def roll(value, amount, dim):
    return pltpu.roll(value, amount % value.shape[dim], dim)


def lane_index(shape):
    return lax.broadcasted_iota(jnp.int32, shape, len(shape) - 1)


def sub_index(shape):
    return lax.broadcasted_iota(jnp.int32, shape, len(shape) - 2)


def sum_rows(parts):
    sub = sub_index(parts[0].shape)
    top = sub < 4
    level = []
    for i in range(4):
        a, b = parts[i], parts[i + 4]
        level.append(jnp.where(top, a, b) + roll(jnp.where(top, b, a), 4, 0))
    mask = (sub & 2) == 0
    level = [
        jnp.where(mask, level[i], level[i + 2])
        + jnp.where(mask, roll(level[i], -2, 0), roll(level[i + 2], 2, 0))
        for i in range(2)
    ]
    mask = (sub & 1) == 0
    a, b = level
    return jnp.where(mask, a, b) + jnp.where(mask, roll(a, -1, 0), roll(b, 1, 0))


def next_row(value):
    lane = lane_index(value.shape)
    sub = sub_index(value.shape)
    turned = roll(value, EC, 1)
    carried = jnp.where((sub & 3) == 0, 0.0, roll(turned, 1, 0))
    return jnp.where(lane < EC, carried, turned)


def previous_row(value):
    lane = lane_index(value.shape)
    sub = sub_index(value.shape)
    turned = roll(value, -EC, 1)
    carried = jnp.where((sub & 3) == 3, 0.0, roll(turned, -1, 0))
    return jnp.where(lane >= LANES - EC, carried, turned)


def place_charges(stencil, row_shift, col_shift):
    shape = row_shift.shape
    lane = lane_index(shape)
    sub = sub_index(shape)
    window = STEN + 2 * HALO
    row_mask = {o: row_shift == o for o in range(-HALO, HALO + 1)}
    col_mask = {o: col_shift == o for o in range(-HALO, HALO + 1)}
    first = []
    for rr in range(window):
        line = []
        for c in range(STEN):
            value = jnp.zeros(shape, jnp.float32)
            for o in range(-HALO, HALO + 1):
                source = rr - HALO - o
                if 0 <= source < STEN:
                    value = jnp.where(row_mask[o], stencil(source * STEN + c), value)
            line.append(value)
        first.append(line)
    framed = []
    for rr in range(window):
        line = []
        for cc in range(window):
            value = jnp.zeros(shape, jnp.float32)
            for o in range(-HALO, HALO + 1):
                source = cc - HALO - o
                if 0 <= source < STEN:
                    value = jnp.where(col_mask[o], first[rr][source], value)
            line.append(value)
        framed.append(line)
    grid = []
    for r in range(PITCH):
        line = []
        for cc in range(window):
            value = framed[r + HALO][cc]
            if r < HALO:
                value = value + next_row(framed[r + HALO + PITCH][cc])
            if r >= PITCH - HALO:
                value = value + previous_row(framed[r + HALO - PITCH][cc])
            line.append(value)
        grid.append(line)
    slot = sub & 3
    low_lanes = lane < EC
    high_lanes = lane >= LANES - EC
    line = []
    for cc in range(window):
        value = jnp.where(low_lanes & (slot == 0), roll(roll(framed[10][cc], EC, 1), -3, 0), 0.0)
        value = jnp.where(low_lanes & (slot == 1), roll(roll(framed[11][cc], EC, 1), -2, 0), value)
        value = jnp.where(high_lanes & (slot == 3), roll(roll(framed[0][cc], -EC, 1), 3, 0), value)
        value = jnp.where(high_lanes & (slot == 2), roll(roll(framed[1][cc], -EC, 1), 2, 0), value)
        line.append(value)
    grid.append(line)
    elem_col = lane & (EC - 1)
    parts = [[] for _ in range(SUB)]
    edges = [jnp.zeros(shape, jnp.float32) for _ in range(SUB)]
    for r in range(GROUPS):
        cells = []
        for c in range(PITCH):
            value = grid[r][c + HALO]
            if c < HALO:
                value = value + jnp.where(elem_col == 0, 0.0, roll(grid[r][c + HALO + PITCH], 1, 1))
            if c >= PITCH - HALO:
                value = value + jnp.where(
                    elem_col == EC - 1, 0.0, roll(grid[r][c + HALO - PITCH], -1, 1)
                )
            cells.append(value)
        turned = transpose_blocks([cells[c] for c in PARITY_ORDER], lane)
        for e in range(SUB):
            parts[e].append(turned[e])
            start = EC * e
            edge = edges[e]
            edge = jnp.where(lane == r, roll(grid[r][10], r - start - (EC - 1), 1), edge)
            edge = jnp.where(lane == 64 + r, roll(grid[r][11], 64 + r - start - (EC - 1), 1), edge)
            edge = jnp.where(lane == 63 - r, roll(grid[r][0], 63 - r - start, 1), edge)
            edge = jnp.where(lane == 127 - r, roll(grid[r][1], 127 - r - start, 1), edge)
            edges[e] = edge
    return [parts[e] + [edges[e]] for e in range(SUB)]


def transpose_blocks(values, lane):
    block = lane // EC
    for step in (4, 2, 1):
        mask = (block & step) == 0
        result = list(values)
        for i in range(SUB):
            if i & step:
                continue
            a, b = values[i], values[i + step]
            result[i] = jnp.where(mask, a, roll(b, EC * step, 1))
            result[i + step] = jnp.where(mask, roll(a, -EC * step, 1), b)
        values = result
    return values


def halves(a, b):
    low = lane_index(a.shape) < 64
    return jnp.where(low, a, roll(b, 64, 1)), jnp.where(low, roll(a, 64, 1), b)


def half_rows(a, b):
    top = sub_index(a.shape) < 4
    return jnp.where(top, a, roll(b, 4, 0)), jnp.where(top, roll(a, 4, 0), b)


def gather_rows(part, edge, count):
    sample = edge(0)
    lane = lane_index(sample.shape)
    from_low = (lane == 0) | (lane == 64)
    from_high = (lane == 63) | (lane == 127)
    rows = []
    for j in range(count):
        groups = []
        for r in range(GROUPS):
            value = part(j, r)
            if j > 0:
                value = value + jnp.where(from_low, roll(edge(j - 1), -r, 1), 0.0)
            if j < count - 1:
                value = value + jnp.where(from_high, roll(edge(j + 1), r, 1), 0.0)
            groups.append(value)
        first, second = [], []
        for parity in range(2):
            for b in range(2):
                low, high = half_rows(groups[parity + 4 * b], groups[parity + 4 * b + 2])
                first.append(low)
                second.append(high)
        low, high = half_rows(groups[8], groups[8])
        first.append(low)
        second.append(high)
        rows.append(jnp.concatenate(first + second, axis=0))
    even, odd = [], []
    for j in range(0, count, 2):
        low, high = halves(rows[j], rows[j + 1])
        even.append(low)
        odd.append(high)
    return jnp.concatenate(even, axis=1), jnp.concatenate(odd, axis=1)


def join_spectrum(even, odd):
    quarter = even.shape[1] // 2
    ec, es = even[:, :quarter], even[:, quarter:]
    oc, os = odd[:, :quarter], odd[:, quarter:]
    return [ec + oc, es - os, ec - oc, es + os]


def split_spectrum(blocks):
    a, b, c, d = blocks
    return (
        jnp.concatenate([a + c, d + b], axis=1),
        jnp.concatenate([a - c, d - b], axis=1),
    )


def scatter_rows(even, odd, count, put):
    rows = []
    for j in range(0, count, 2):
        tile = slice(64 * j, 64 * j + LANES)
        rows.extend(halves(even[:, tile], odd[:, tile]))
    blocks = []
    for j in range(count):
        first = [rows[j][8 * i : 8 * i + 8] for i in range(5)]
        second = [rows[j][40 + 8 * i : 48 + 8 * i] for i in range(5)]
        groups = [None] * GROUPS
        for parity in range(2):
            for b in range(2):
                low, high = half_rows(first[2 * parity + b], second[2 * parity + b])
                groups[parity + 4 * b] = low
                groups[parity + 4 * b + 2] = high
        sub = sub_index(first[4].shape)
        tail = jnp.where(sub < 4, roll(first[4], 4, 0), second[4])
        head = jnp.where(sub < 4, first[4], roll(second[4], 4, 0))
        groups[8] = jnp.where((sub & 2) == 0, head, tail)
        blocks.append(groups)
    lane = lane_index(blocks[0][0].shape)
    for j in range(count):
        edge = jnp.zeros(blocks[0][0].shape, jnp.float32)
        for r in range(GROUPS):
            if j < count - 1:
                edge = jnp.where(
                    (lane == r) | (lane == 64 + r), roll(blocks[j + 1][r], r, 1), edge
                )
            if j > 0:
                edge = jnp.where(
                    (lane == 63 - r) | (lane == 127 - r), roll(blocks[j - 1][r], -r, 1), edge
                )
        put(j, blocks[j] + [edge])


def read_samples(part, edge, row_shift, col_shift, put):
    shape = row_shift.shape
    lane = lane_index(shape)
    sub = sub_index(shape)
    elem_col = lane & (EC - 1)
    window = STEN + 2 * HALO
    grid = []
    for r in range(GROUPS):
        turned = transpose_blocks([part(e, r) for e in range(SUB)], lane)
        cells = [None] * PITCH
        for place, c in enumerate(PARITY_ORDER):
            cells[c] = turned[place]
        line = [None] * window
        for c in range(PITCH):
            line[c + HALO] = cells[c]
        after = [roll(cells[c], -1, 1) for c in range(HALO)]
        before = [roll(cells[PITCH - HALO + c], 1, 1) for c in range(HALO)]
        for e in range(SUB):
            start = EC * e
            last = lane == start + EC - 1
            zero = lane == start
            after[0] = jnp.where(last, roll(edge(e), start + EC - 1 - r, 1), after[0])
            after[1] = jnp.where(last, roll(edge(e), start + EC - 1 - 64 - r, 1), after[1])
            before[0] = jnp.where(zero, roll(edge(e), start - 63 + r, 1), before[0])
            before[1] = jnp.where(zero, roll(edge(e), start - 127 + r, 1), before[1])
        line[0], line[1] = before
        line[10], line[11] = after
        grid.append(line)
    slot = sub & 3
    first_row = (slot == 0) & (lane < EC)
    last_row = (slot == 3) & (lane >= LANES - EC)
    framed = [[None] * window for _ in range(window)]
    for cc in range(window):
        for r in range(PITCH):
            framed[r + HALO][cc] = grid[r][cc]
        outer = grid[8][cc]
        below = roll(outer, -EC, 1)
        above = roll(outer, EC, 1)
        framed[10][cc] = jnp.where(last_row, roll(below, 3, 0), previous_row(grid[0][cc]))
        framed[11][cc] = jnp.where(last_row, roll(below, 2, 0), previous_row(grid[1][cc]))
        framed[0][cc] = jnp.where(first_row, roll(above, -3, 0), next_row(grid[6][cc]))
        framed[1][cc] = jnp.where(first_row, roll(above, -2, 0), next_row(grid[7][cc]))
    for a in range(STEN):
        line = []
        for cc in range(window):
            value = framed[a + HALO][cc]
            for o in range(-HALO, HALO + 1):
                if o:
                    value = jnp.where(row_shift == o, framed[a + HALO + o][cc], value)
            line.append(value)
        for b in range(STEN):
            value = line[b + HALO]
            for o in range(-HALO, HALO + 1):
                if o:
                    value = jnp.where(col_shift == o, line[b + HALO + o], value)
            put(a * STEN + b, value)


def add_outer_rows(chunk, row_count, col_count):
    sub = sub_index((SUB, LANES))
    even, odd = [], []
    for i in range(row_count):
        for j in range(col_count):
            rows = [chunk(i, j)[8 * k : 8 * k + 8] for k in range(4)]
            if j == 0 and i > 0:
                outer = chunk(i - 1, 0)[32:40]
                rows[0] = rows[0] + jnp.where(sub == 0, outer, 0.0)
                rows[2] = rows[2] + jnp.where(sub == 0, roll(outer, -1, 0), 0.0)
            if j == col_count - 1 and i < row_count - 1:
                outer = chunk(i + 1, j)[32:40]
                rows[1] = rows[1] + jnp.where(sub == 7, outer, 0.0)
                rows[3] = rows[3] + jnp.where(sub == 7, roll(outer, 1, 0), 0.0)
            even.extend(rows[:2])
            odd.extend(rows[2:])
    return jnp.concatenate(even, axis=0), jnp.concatenate(odd, axis=0)


def spread_outer_rows(even, odd, row_count, col_count, put):
    sub = sub_index((SUB, LANES))

    def block(i, j):
        start = 16 * (i * col_count + j)
        return [even[start : start + 8], even[start + 8 : start + 16],
                odd[start : start + 8], odd[start + 8 : start + 16]]

    for i in range(row_count):
        for j in range(col_count):
            outer = jnp.zeros((SUB, LANES), jnp.float32)
            if j == 0 and i < row_count - 1:
                rows = block(i + 1, 0)
                outer = jnp.where(sub == 0, rows[0], jnp.where(sub == 1, roll(rows[2], 1, 0), outer))
            if j == col_count - 1 and i > 0:
                rows = block(i - 1, j)
                outer = jnp.where(sub == 7, rows[1], jnp.where(sub == 6, roll(rows[3], -1, 0), outer))
            put(i, j, block(i, j) + [outer])


def two_terms(value):
    high = value.astype(jnp.bfloat16)
    return high, (value - high.astype(jnp.float32)).astype(jnp.bfloat16)


def dot(left, right, dims=((1,), (0,))):
    return lax.dot_general(left, right, (dims, ((), ())), preferred_element_type=jnp.float32)


def even_positions(row_count, col_count):
    j, c, e = np.meshgrid(np.arange(col_count), np.arange(4), np.arange(EC), indexing="ij")
    columns = (LANES * j + PITCH * e + 2 * c).reshape(-1)
    i, j, b, h, t = np.meshgrid(
        np.arange(row_count), np.arange(col_count), np.arange(2), np.arange(2), np.arange(TILES),
        indexing="ij",
    )
    rows = (ER * PITCH * i + SUB * PITCH * t + PITCH * j + 2 * h + 4 * b).reshape(-1)
    return columns, rows


def basis_tables(positions, length, lane_major):
    quarter = length // 4
    outer = np.arange(quarter // LANES) * LANES
    inner = np.arange(LANES)
    tables = []
    for parity in range(2):
        x = positions + parity
        coarse = 2.0 * np.pi * (x[:, None] * outer[None, :] % length) / length
        fine = 2.0 * np.pi * (x[:, None] * inner[None, :] % length) / length
        sign = np.where(positions % 4 == 0, 1.0, -1.0)
        if lane_major:
            shape_c, shape_f, shape_s = (1, 2), (0, 2), (0, 1)
        parts = [np.cos(coarse), np.sin(coarse), np.cos(fine), np.sin(fine)]
        parts = [np.asarray(p, np.float32) for p in parts]
        sign = np.asarray(sign, np.float32)
        if lane_major:
            cc, cs = (jnp.asarray(np.ascontiguousarray(p.T))[:, None, :] for p in parts[:2])
            fc, fs = (jnp.asarray(np.ascontiguousarray(p.T))[None, :, :] for p in parts[2:])
            sg = jnp.asarray(sign)[None, :]
            shape = (quarter, x.shape[0])
            axis, order = 0, lax.broadcasted_iota(jnp.int32, shape, 0)
        else:
            cc, cs = (jnp.asarray(p)[:, :, None] for p in parts[:2])
            fc, fs = (jnp.asarray(p)[:, None, :] for p in parts[2:])
            sg = jnp.asarray(sign)[:, None]
            shape = (x.shape[0], quarter)
            axis, order = 1, lax.broadcasted_iota(jnp.int32, shape, 1)
        cosine = (cc * fc - cs * fs).reshape(shape)
        if parity == 0:
            sine = (cs * fc + cc * fs).reshape(shape)
            second = jnp.where(order == 0, 1.0, -sine) * sg
        else:
            second = cosine * sg
        full = jnp.concatenate([cosine, second], axis=axis)
        high = lax.reduce_precision(full, 8, 7)
        tables.append(high.astype(jnp.bfloat16))
        tables.append((full - high).astype(jnp.bfloat16))
    return tables


def tiled_shifts(shifts_ref, which):
    rows = [shifts_ref[which : which + 1, LANES * t : LANES * (t + 1)] for t in range(TILES)]
    return jnp.concatenate(rows * RHS, axis=0)


def charge_kernel(currents_ref, projection_ref, shifts_ref, out_ref, current, partial, stencil):
    step = pl.program_id(0)

    @pl.when(step == 0)
    def _():
        current[...] = currents_ref[...].astype(jnp.bfloat16).astype(jnp.float32)

    for t in range(TILES):
        lanes = slice(LANES * t, LANES * (t + 1))
        totals = [[None] * RHS for _ in range(STEN)]
        for b in range(0, BASIS, 16):
            values = [
                [current[q, b + 8 * h : b + 8 * h + 8, lanes] for h in range(2)] for q in range(RHS)
            ]
            for s in range(STEN):
                weight = projection_ref[s, b : b + 16, lanes].astype(jnp.float32)
                for q in range(RHS):
                    term = weight[:8] * values[q][0] + weight[8:] * values[q][1]
                    totals[s][q] = term if totals[s][q] is None else totals[s][q] + term
        for s in range(STEN):
            for q in range(RHS):
                partial[s, q * TILES + t] = totals[s][q]
    for s in range(STEN):
        stencil[step * STEN + s] = sum_rows([partial[s, i] for i in range(SUB)])

    @pl.when(step == pl.num_programs(0) - 1)
    def _():
        chunks = place_charges(
            lambda s: stencil[s], tiled_shifts(shifts_ref, 0), tiled_shifts(shifts_ref, 1)
        )
        for e in range(SUB):
            out_ref[e] = jnp.concatenate(chunks[e], axis=0).astype(out_ref.dtype)


def column_kernel(count, rows_ref, eh, el, oh, ol, out_ref):
    def part(j, r):
        return rows_ref[j, 8 * r : 8 * r + 8, :].astype(jnp.float32)

    even, odd = gather_rows(part, lambda j: part(j, GROUPS), count)
    even = even.astype(jnp.bfloat16)
    odd = odd.astype(jnp.bfloat16)
    blocks = join_spectrum(
        dot(even, eh[...]) + dot(even, el[...]), dot(odd, oh[...]) + dot(odd, ol[...])
    )
    half = out_ref.shape[1]
    device = 0
    for block in blocks:
        for t in range(0, block.shape[1], LANES):
            for chunk in halves(block[:half, t : t + LANES], block[half:, t : t + LANES]):
                out_ref[device] = chunk.astype(out_ref.dtype)
                device += 1


def row_kernel(row_count, col_count, in_ref, eh, el, oh, ol, teh, tel, toh, tol, sum_ref, diff_ref, out_ref):
    even, odd = add_outer_rows(
        lambda i, j: in_ref[i * col_count + j].astype(jnp.float32), row_count, col_count
    )
    even = even.astype(jnp.bfloat16)
    odd = odd.astype(jnp.bfloat16)
    a = dot(eh[...], even) + dot(el[...], even)
    b = dot(oh[...], odd) + dot(ol[...], odd)
    plus, minus = sum_ref[...], diff_ref[...]

    def back(value, high_ref, low_ref):
        high, low = two_terms(value)
        both = dot(high_ref[...], jnp.concatenate([high, low], axis=1))
        return both[:, :LANES] + both[:, LANES:] + dot(low_ref[...], high)

    def put(i, j, parts):
        out_ref[i * col_count + j] = jnp.concatenate(parts, axis=0).astype(out_ref.dtype)

    spread_outer_rows(
        back(a * plus + b * minus, teh, tel),
        back(a * minus + b * plus, toh, tol),
        row_count,
        col_count,
        put,
    )


def grid_kernel(count, in_ref, eh, el, oh, ol, out_ref):
    devices = in_ref.shape[0]
    first, second = [], []
    for d in range(0, devices, 2):
        low, high = halves(in_ref[d].astype(jnp.float32), in_ref[d + 1].astype(jnp.float32))
        first.append(low)
        second.append(high)
    per_block = devices // 8
    blocks = []
    for k in range(4):
        span = slice(per_block * k, per_block * (k + 1))
        blocks.append(
            jnp.concatenate(
                [jnp.concatenate(first[span], axis=1), jnp.concatenate(second[span], axis=1)], axis=0
            )
        )
    contract = ((1,), (1,))

    def back(value, high_ref, low_ref):
        high, low = two_terms(value)
        both = dot(jnp.concatenate([high, low], axis=0), high_ref[...], contract)
        half = high.shape[0]
        return both[:half] + both[half:] + dot(high, low_ref[...], contract)

    even, odd = split_spectrum(blocks)

    def put(j, parts):
        out_ref[j] = jnp.concatenate(parts, axis=0).astype(out_ref.dtype)

    scatter_rows(back(even, eh, el), back(odd, oh, ol), count, put)


def far_kernel(grid_ref, projection_ref, shifts_ref, near_ref, out_ref, samples):
    @pl.when(pl.program_id(0) == 0)
    def _():
        def part(e, r):
            return grid_ref[e, 8 * r : 8 * r + 8, :].astype(jnp.float32)

        def put(s, value):
            samples[s] = value

        read_samples(
            part,
            lambda e: part(e, GROUPS),
            tiled_shifts(shifts_ref, 0),
            tiled_shifts(shifts_ref, 1),
            put,
        )

    depth = out_ref.shape[1]

    def add_row(a, totals):
        totals = list(totals)
        for b in range(STEN):
            s = a * STEN + b
            for t in range(TILES):
                weight = projection_ref[s, :, LANES * t : LANES * (t + 1)].astype(jnp.float32)
                for q in range(RHS):
                    index = q * TILES + t
                    totals[index] = totals[index] + weight * samples[s, index : index + 1, :]
        return tuple(totals)

    start = tuple(
        near_ref[q, :, LANES * t : LANES * (t + 1)] for q in range(RHS) for t in range(TILES)
    )
    totals = lax.fori_loop(0, STEN, add_row, start)
    for q in range(RHS):
        for t in range(TILES):
            out_ref[q, :, LANES * t : LANES * (t + 1)] = totals[q * TILES + t]


def near_kernel(own_ref, left_ref, right_ref, above_ref, below_ref, partners_ref, blocks_ref, out_ref, picked):
    @pl.when(pl.program_id(0) == 0)
    def _():
        lane = lane_index((BASIS, LANES))
        elem_col = lane & (EC - 1)

        def three(own, left, right):
            own, left, right = (v.astype(jnp.float32) for v in (own, left, right))
            return (
                jnp.where(elem_col == 0, roll(left, 1 - EC, 1), roll(own, 1, 1)),
                own,
                jnp.where(elem_col == EC - 1, roll(right, EC - 1, 1), roll(own, -1, 1)),
            )

        for q in range(RHS):
            tiles = [three(above_ref[0, q], above_ref[1, q], above_ref[2, q])]
            for t in range(TILES):
                lanes = slice(LANES * t, LANES * (t + 1))
                tiles.append(three(own_ref[q, :, lanes], left_ref[q, :, lanes], right_ref[q, :, lanes]))
            tiles.append(three(below_ref[0, q], below_ref[1, q], below_ref[2, q]))
            for t in range(TILES):
                lanes = slice(LANES * t, LANES * (t + 1))
                before, here, after = tiles[t : t + 3]
                codes = [partners_ref[k : k + 1, lanes] for k in range(NEIGH)]
                chosen = [here[1]] * NEIGH
                for c in range(3):
                    views = (
                        jnp.where(lane < EC, roll(before[c], EC, 1), roll(here[c], EC, 1)),
                        here[c],
                        jnp.where(lane >= LANES - EC, roll(after[c], -EC, 1), roll(here[c], -EC, 1)),
                    )
                    for r in range(3):
                        if r == 1 and c == 1:
                            continue
                        for k in range(1, NEIGH):
                            chosen[k] = jnp.where(codes[k] == 3 * r + c, views[r], chosen[k])
                for k in range(NEIGH):
                    picked[k, q, :, lanes] = chosen[k]

    def one_tile(t, carry):
        lanes = pl.ds(pl.multiple_of(t * LANES, LANES), LANES)
        totals = [[None] * RHS for _ in range(SUB)]
        for k in range(NEIGH):
            for b in range(0, BASIS, 16):
                values = [
                    [picked[k, q, b + 8 * h : b + 8 * h + 8, lanes] for h in range(2)]
                    for q in range(RHS)
                ]
                for a in range(SUB):
                    weight = blocks_ref[k, a, b : b + 16, lanes].astype(jnp.float32)
                    for q in range(RHS):
                        term = weight[:8] * values[q][0] + weight[8:] * values[q][1]
                        totals[a][q] = term if totals[a][q] is None else totals[a][q] + term
        for q in range(RHS):
            out_ref[q, :, lanes] = sum_rows([totals[a][q] for a in range(SUB)])
        return carry

    lax.fori_loop(0, TILES, one_tile, 0)


def neighbours(value, axis):
    count = lax.axis_size(axis)
    forward = [(i, i + 1) for i in range(count - 1)]
    backward = [(i + 1, i) for i in range(count - 1)]
    return forward, backward


def whole(shape):
    return pl.BlockSpec(shape, lambda *_: (0,) * len(shape))


def shards_real(currents, projection, near_blocks, partners, shifts, green):
    row_count = lax.axis_size("row")
    col_count = lax.axis_size("col")
    elements = currents.shape[2]
    width = col_count * LANES
    length = 2 * width
    quarter = length // 4
    f32, b16 = jnp.float32, jnp.bfloat16
    struct = jax.ShapeDtypeStruct
    devices = row_count * col_count

    charges = pl.pallas_call(
        charge_kernel,
        grid=(STEN,),
        in_specs=[
            whole((RHS, BASIS, elements)),
            pl.BlockSpec((STEN, BASIS, elements), lambda i: (i, 0, 0)),
            whole((2, elements)),
        ],
        out_specs=whole((SUB, 80, LANES)),
        out_shape=struct((SUB, 80, LANES), b16),
        scratch_shapes=[
            pltpu.VMEM((RHS, BASIS, elements), f32),
            pltpu.VMEM((STEN, SUB, SUB, LANES), f32),
            pltpu.VMEM((STEN * STEN, SUB, LANES), f32),
        ],
        name="charges",
    )(currents, projection, shifts)
    slab = lax.all_to_all(charges, "col", 0, 0, tiled=True)

    columns, rows = even_positions(row_count, col_count)
    col_tables = basis_tables(columns, length, False)
    row_tables = basis_tables(rows, length, True)
    back_tables = basis_tables(rows, length, False)
    weight_k = jnp.where(jnp.arange(length) % quarter == 0, 1.0, 2.0).astype(f32)
    mine = lax.axis_index("row") * col_count + lax.axis_index("col")
    depth = green.shape[0]
    weight_m = jnp.where((mine * depth + jnp.arange(depth)) % quarter == 0, 1.0, 2.0).astype(f32)
    scaled = green * (weight_m * (1.0 / (length * length)))[:, None] * weight_k[None, :]
    scaled = jnp.concatenate([scaled, scaled], axis=0).T
    upper = jnp.concatenate([scaled[:quarter], scaled[3 * quarter :]], axis=0)
    lower = jnp.concatenate([scaled[2 * quarter : 3 * quarter], scaled[quarter : 2 * quarter]], axis=0)

    spectrum = pl.pallas_call(
        functools.partial(column_kernel, col_count),
        out_shape=struct((devices, 40, LANES), b16),
        name="columns",
    )(slab, *col_tables)
    arrived = lax.all_to_all(spectrum, ("row", "col"), 0, 0, tiled=True)
    rows_back = pl.pallas_call(
        functools.partial(row_kernel, row_count, col_count),
        out_shape=struct((devices, 40, LANES), b16),
        name="rows",
    )(arrived, *row_tables, *back_tables, upper + lower, upper - lower)
    returned = lax.all_to_all(rows_back, ("row", "col"), 0, 0, tiled=True)
    potential = pl.pallas_call(
        functools.partial(grid_kernel, col_count),
        out_shape=struct((SUB, 80, LANES), b16),
        name="grid",
    )(returned, *col_tables)
    pieces = lax.all_to_all(potential, "col", 0, 0, tiled=True)

    half = currents.astype(b16)
    forward, backward = neighbours(half, "col")
    left = lax.ppermute(half, "col", forward)
    right = lax.ppermute(half, "col", backward)
    three = jnp.stack([half, left, right])
    forward, backward = neighbours(half, "row")
    above = lax.ppermute(three[..., elements - LANES :], "row", forward)
    below = lax.ppermute(three[..., :LANES], "row", backward)
    near = pl.pallas_call(
        near_kernel,
        grid=(BASIS // SUB,),
        in_specs=[
            whole((RHS, BASIS, elements)),
            whole((RHS, BASIS, elements)),
            whole((RHS, BASIS, elements)),
            whole((3, RHS, BASIS, LANES)),
            whole((3, RHS, BASIS, LANES)),
            whole((NEIGH, elements)),
            pl.BlockSpec((NEIGH, SUB, BASIS, elements), lambda i: (0, i, 0, 0)),
        ],
        out_specs=pl.BlockSpec((RHS, SUB, elements), lambda i: (0, i, 0)),
        out_shape=struct((RHS, BASIS, elements), f32),
        scratch_shapes=[pltpu.VMEM((NEIGH, RHS, BASIS, elements), f32)],
        name="near",
    )(half, left, right, above, below, partners, near_blocks)

    depth = 16
    return pl.pallas_call(
        far_kernel,
        grid=(BASIS // depth,),
        in_specs=[
            whole((SUB, 80, LANES)),
            pl.BlockSpec((STEN * STEN, depth, elements), lambda i: (0, i, 0)),
            whole((2, elements)),
            pl.BlockSpec((RHS, depth, elements), lambda i: (0, i, 0)),
        ],
        out_specs=pl.BlockSpec((RHS, depth, elements), lambda i: (0, i, 0)),
        out_shape=struct((RHS, BASIS, elements), f32),
        scratch_shapes=[pltpu.VMEM((STEN * STEN, SUB, LANES), f32)],
        name="far",
    )(pieces, projection, shifts, near)


def shards(currents, projection, near_blocks, partners, shifts, green):
    row_count = lax.axis_size("row")
    col_count = lax.axis_size("col")
    fits = col_count == SUB and green.shape[0] == 64 and 2 * row_count * col_count == green.shape[0]
    if fits and currents.shape[2] == TILES * LANES and row_count * ER == col_count * EC:
        return shards_real(currents, projection, near_blocks, partners, shifts, green)
    return shards_general(currents, projection, near_blocks, partners, shifts, green)


def solution(mesh):
    in_specs = (
        P(None, None, ("row", "col")),
        P(None, None, ("row", "col")),
        P(None, None, None, ("row", "col")),
        P(None, ("row", "col")),
        P(None, ("row", "col")),
        P(("row", "col"), None),
    )
    out_specs = P(None, None, ("row", "col"))
    return jax.shard_map(shards, mesh=mesh, in_specs=in_specs, out_specs=out_specs, check_vma=False)
```

profile of v0, /device:TPU:0, one launch (start us, length us, event | category | flops | bytes accessed | tf_op | source)
XLA Modules:
  0.0 122.8 jit_solution(8248292244678679663)
XLA Ops:
  0.0 7.7 %charges.1 = bf16[8,80,128]{2,1,0:T(8,128)(2,1)} custom-call(f32[2,64,512]{2,1,0:T(8,128)} %currents_ref.1, bf16[64,64,512]{2,1,0:T(8,128)(2,1)} %projection_ref.3, s32[2,512]{1,0:T(2,128)} %shifts_ref.3), custom_call_target="tpu_custom_call" | custom-call | tf_op jit(solution)/shard_map/charges/pallas_call | solution.py:868
  7.7 6.4 %all-to-all-start = ((bf16[8,80,128]{2,1,0:T(8,128)(2,1)}), bf16[8,80,128]{2,1,0:T(8,128)(2,1)}, u32[]{:S(2)}, u32[]{:S(2)}) async-start(bf16[8,80,128]{2,1,0:T(8,128)(2,1)} %charges.1), calls=%async_computation | async-start | bytes 327680 | tf_op jit(solution)/shard_map/all_to_all | solution.py:885
  14.1 0.0 copy-start.36
  14.1 0.0 copy-start.37
  14.1 0.0 copy-start.38
  14.1 0.0 copy-start.39
  14.1 3.4 %multiply_subtract_fusion.5 = (f32[512,4,128]{2,1,0:T(4,128)S(1)}, f32[512,4,128]{2,1,0:T(4,128)}) fusion(f32[512,128]{1,0:T(8,128)S(1)} %copy-done.28, f32[512,4]{1,0:T(8,128)S(1)} %copy-done.29, f32[512,128]{1,0:T(8,128)S(1)} %copy-done.30, f32[512,4]{1,0:T(8,128)S(1)} %copy-done.31), kind=kLoop, calls=%fused_computation.44 | loop fusion | flops 1835008 | bytes 2637824 | tf_op jit(solution)/shard_map/sub | solution.py:617
  17.5 1.0 copy.59
  18.6 2.5 %multiply_subtract_fusion.4 = f32[512,4,128]{2,1,0:T(4,128)S(1)} fusion(f32[512,128]{1,0:T(8,128)S(1)} %copy-done.36, f32[512,4]{1,0:T(8,128)S(1)} %copy-done.37, f32[512,128]{1,0:T(8,128)S(1)} %copy-done.38, f32[512,4]{1,0:T(8,128)S(1)} %copy-done.39), kind=kLoop, calls=%fused_computation.42 | loop fusion | flops 786432 | bytes 1589248 | tf_op jit(solution)/shard_map/sub | solution.py:617
  21.1 1.1 copy.58
  22.1 0.3 copy.38
  22.5 0.0 copy-start.32
  22.5 0.0 copy-start.34
  22.5 0.0 copy-start.35
  22.5 0.3 multiply_multiply_fusion
  22.9 0.0 copy-start.26
  22.9 0.0 copy-start.45
  22.9 0.0 copy-start.46
  22.9 0.3 maximum_bitcast_fusion
  23.3 0.2 copy-done.32
  23.4 0.1 copy-done.33
  23.5 0.1 copy-done.34
  23.6 0.1 copy-done.35
  23.7 2.5 %multiply_subtract_fusion = f32[512,4,128]{2,1,0:T(4,128)S(1)} fusion(f32[512,128]{1,0:T(8,128)S(1)} %copy-done.32, f32[512,4]{1,0:T(8,128)S(1)} %copy-done.33, f32[512,128]{1,0:T(8,128)S(1)} %copy-done.34, f32[512,4]{1,0:T(8,128)S(1)} %copy-done.35), kind=kLoop, calls=%fused_computation.36 | loop fusion | flops 786432 | bytes 1589248 | tf_op jit(solution)/shard_map/sub | solution.py:617
  26.2 0.0 copy-start.20
  26.3 0.0 copy-start.21
  26.3 0.2 multiply_subtract_fusion.2
  26.5 1.3 %multiply_subtract_fusion.3 = (f32[4,128,512]{2,1,0:T(8,128)}, f32[4,128,512]{2,1,0:T(8,128)S(1)}) fusion(f32[128,512]{1,0:T(8,128)S(1)} %copy-done.24, f32[4,512]{1,0:T(4,128)S(1)} %copy-done.43, f32[128,512]{1,0:T(8,128)S(1)} %copy-done.25, f32[4,512]{1,0:T(4,128)S(1)} %copy-done.44), kind=kLoop, calls=%fused_computation.41 | loop fusion | flops 1835008 | bytes 2637824 | tf_op jit(solution)/shard_map/sub | solution.py:617
  27.9 3.4 %multiply_subtract_fusion.1 = (f32[512,4,128]{2,1,0:T(4,128)}, f32[512,4,128]{2,1,0:T(4,128)S(1)}) fusion(f32[512,128]{1,0:T(8,128)S(1)} %copy-done.20, f32[512,4]{1,0:T(8,128)S(1)} %copy-done.21, f32[512,128]{1,0:T(8,128)S(1)} %copy-done.22, f32[512,4]{1,0:T(8,128)S(1)} %copy-done.23), kind=kLoop, calls=%fused_computation.38 | loop fusion | flops 1835008 | bytes 2637824 | tf_op jit(solution)/shard_map/sub | solution.py:617
  31.2 2.6 %broadcast_multiply_fusion = (f32[512,512]{1,0:T(8,128)}, f32[512,512]{1,0:T(8,128)}, f32[512,512]{1,0:T(8,128)}, f32[512,512]{1,0:T(8,128)}, f32[512,512]{1,0:T(8,128)S(1)}, /*index=5*/f32[512,512]{1,0:T(8,128)S(1)}) fusion(f32[512]{0:T(512)S(1)} %copy-done.42, f32[64,8,4,128]{3,2,1,0:T(4,128)S(1)} %bitcast.43, ...), kind=kLoop, calls=%fused_computation.47 | loop fusion | flops 2359296 | bytes 12587520 | tf_op jit(solution)/shard_map/mul | solution.py:622
  33.8 1.8 %fusion = (bf16[512,1024]{1,0:T(8,128)(2,1)}, bf16[512,1024]{1,0:T(8,128)(2,1)}) fusion(f32[512,512]{1,0:T(8,128)S(1)} %get-tuple-element.39, f32[512,512]{1,0:T(8,128)S(1)} %bitcast.52), kind=kLoop, calls=%fused_computation.12 | loop fusion | flops 2621440 | bytes 4194304 | tf_op jit(solution)/shard_map/convert_element_type | solution.py:626
  35.6 1.8 %fusion.1 = (bf16[512,1024]{1,0:T(8,128)(2,1)}, bf16[512,1024]{1,0:T(8,128)(2,1)}) fusion(f32[512,512]{1,0:T(8,128)S(1)} %get-tuple-element.40, f32[512,512]{1,0:T(8,128)S(1)} %bitcast.53), kind=kLoop, calls=%fused_computation.13 | loop fusion | flops 2621440 | bytes 4194304 | tf_op jit(solution)/shard_map/convert_element_type | solution.py:626
  37.4 1.0 fusion.18
  38.4 4.1 %columns.1 = bf16[32,40,128]{2,1,0:T(8,128)(2,1)} custom-call(bf16[8,80,128]{2,1,0:T(8,128)(2,1)} %all-to-all-done.rows_ref, bf16[512,1024]{1,0:T(8,128)(2,1)} %get-tuple-element.16.eh, bf16[512,1024]{1,0:T(8,128)(2,1)} %get-tuple-element.15.el, bf16[512,1024]{1,0:T(8,128)(2,1)} %get-tuple-element.14.oh, bf16[512,1024]{1,0:T(8,128)(2,1)} %get-tuple-element.13.ol), custom_call_target="tpu_custom_call" | custom-call | tf_op jit(solution)/shard_map/columns/pallas_call | solution.py:900
  42.5 6.2 %all-to-all-start.1 = ((bf16[32,40,128]{2,1,0:T(8,128)(2,1)}), bf16[32,40,128]{2,1,0:T(8,128)(2,1)S(1)}, u32[]{:S(2)}, u32[]{:S(2)}) async-start(bf16[32,40,128]{2,1,0:T(8,128)(2,1)} %columns.1), calls=%async_computation.1 | async-start | bytes 655360 | tf_op jit(solution)/shard_map/all_to_all | solution.py:905
  48.8 2.8 %fusion.2 = (bf16[1024,512]{1,0:T(8,128)(2,1)}, bf16[1024,512]{1,0:T(8,128)(2,1)}) fusion(f32[512,512]{1,0:T(8,128)S(1)} %copy-done.5, f32[512,512]{1,0:T(8,128)} %bitcast.54), kind=kLoop, calls=%fused_computation.14 | loop fusion | flops 2621440 | bytes 4194304 | tf_op jit(solution)/shard_map/convert_element_type | solution.py:626
  51.7 0.1 copy.56
  51.7 1.1 copy-done.1
  52.9 0.1 copy.57
  52.9 0.0 copy-done.12
  53.0 0.1 copy-done.13
  53.1 0.1 copy-done.14
  53.1 1.1 fusion.9
  54.2 1.7 %fusion.3 = (bf16[1024,512]{1,0:T(8,128)(2,1)}, bf16[1024,512]{1,0:T(8,128)(2,1)}) fusion(f32[512,512]{1,0:T(8,128)S(1)} %copy-done.4, f32[512,512]{1,0:T(8,128)S(1)} %bitcast.47), kind=kLoop, calls=%fused_computation.15 | loop fusion | flops 2621440 | bytes 4194304 | tf_op jit(solution)/shard_map/convert_element_type | solution.py:626
  55.9 1.8 %fusion.4 = (bf16[512,1024]{1,0:T(8,128)(2,1)}, bf16[512,1024]{1,0:T(8,128)(2,1)}) fusion(f32[512,512]{1,0:T(8,128)S(1)} %copy-done.3, f32[512,512]{1,0:T(8,128)S(1)} %bitcast.56), kind=kLoop, calls=%fused_computation.16 | loop fusion | flops 2621440 | bytes 4194304 | tf_op jit(solution)/shard_map/convert_element_type | solution.py:626
  57.7 1.8 %fusion.5 = (bf16[512,1024]{1,0:T(8,128)(2,1)}, bf16[512,1024]{1,0:T(8,128)(2,1)}) fusion(f32[512,512]{1,0:T(8,128)S(1)} %copy-done.2, f32[512,512]{1,0:T(8,128)S(1)} %bitcast.55), kind=kLoop, calls=%fused_computation.17 | loop fusion | flops 2621440 | bytes 4194304 | tf_op jit(solution)/shard_map/convert_element_type | solution.py:626
  59.5 1.1 all-to-all-done.1.in_ref
  60.6 0.7 copy-done.9
  61.4 6.9 %rows.1 = bf16[32,40,128]{2,1,0:T(8,128)(2,1)} custom-call(bf16[32,40,128]{2,1,0:T(8,128)(2,1)} %copy-done.9, bf16[1024,512]{1,0:T(8,128)(2,1)} %get-tuple-element.12.eh, bf16[1024,512]{1,0:T(8,128)(2,1)} %get-tuple-element.11.el, bf16[1024,512]{1,0:T(8,128)(2,1)} %get-tuple-element.10.oh, bf16[1024,512]{1,0:T(8,128)(2,1)} %get-tuple-element.9.ol, ...), custom_call_target="tpu_custom_call" | custom-call | tf_op jit(solution)/shard_map/rows/pallas_call | solution.py:906
  68.2 4.6 %all-to-all-start.2 = ((bf16[32,40,128]{2,1,0:T(8,128)(2,1)}), bf16[32,40,128]{2,1,0:T(8,128)(2,1)S(1)}, u32[]{:S(2)}, u32[]{:S(2)}) async-start(bf16[32,40,128]{2,1,0:T(8,128)(2,1)} %rows.1), calls=%async_computation.2 | async-start | bytes 655360 | tf_op jit(solution)/shard_map/all_to_all | solution.py:911
  72.8 2.2 %collective-permute-start = (bf16[2,64,512]{2,1,0:T(8,128)(2,1)S(1)}, bf16[2,64,512]{2,1,0:T(8,128)(2,1)S(1)}, u32[]{:S(2)}, u32[]{:S(2)}) collective-permute-start(bf16[2,64,512]{2,1,0:T(8,128)(2,1)S(1)} %convert_element_type.51.own_ref), channel_id=1, source_target_pairs={{0,1},{1,2},{2,3},{3,4},{4,5},{5,6},{6,7},{8,9},{9,10},{10,11},{11... | collective-permute-start | bytes 393224 | tf_op jit(solution)/shard_map/ppermute | solution.py:921
  75.0 1.3 %collective-permute-start.1 = (bf16[2,64,512]{2,1,0:T(8,128)(2,1)S(1)}, bf16[2,64,512]{2,1,0:T(8,128)(2,1)S(1)}, u32[]{:S(2)}, u32[]{:S(2)}) collective-permute-start(bf16[2,64,512]{2,1,0:T(8,128)(2,1)S(1)} %convert_element_type.51.own_ref), channel_id=1, source_target_pairs={{1,0},{2,1},{3,2},{4,3},{5,4},{6,5},{7,6},{9,8},{10,9},{11,10},{12... | collective-permute-start | bytes 393224 | tf_op jit(solution)/shard_map/ppermute | solution.py:922
  76.3 8.5 %all-to-all-done.2.in_ref = bf16[32,40,128]{2,1,0:T(8,128)(2,1)S(1)} async-done(((bf16[32,40,128]{2,1,0:T(8,128)(2,1)}), bf16[32,40,128]{2,1,0:T(8,128)(2,1)S(1)}, u32[]{:S(2)}, u32[]{:S(2)}) %all-to-all-start.2) | async-done | bytes 327712 | tf_op jit(solution)/shard_map/all_to_all | solution.py:911
  84.8 0.7 copy-done.10
  85.6 4.6 %grid.1 = bf16[8,80,128]{2,1,0:T(8,128)(2,1)} custom-call(bf16[32,40,128]{2,1,0:T(8,128)(2,1)} %copy-done.10, bf16[512,1024]{1,0:T(8,128)(2,1)} %get-tuple-element.16.eh, bf16[512,1024]{1,0:T(8,128)(2,1)} %get-tuple-element.15.el, bf16[512,1024]{1,0:T(8,128)(2,1)} %get-tuple-element.14.oh, bf16[512,1024]{1,0:T(8,128)(2,1)} %get-tuple-element.13.ol), custom_call_target="tpu_custom_call" | custom-call | tf_op jit(solution)/shard_map/grid/pallas_call | solution.py:912
  90.2 3.4 %all-to-all-start.3 = ((bf16[8,80,128]{2,1,0:T(8,128)(2,1)}), bf16[8,80,128]{2,1,0:T(8,128)(2,1)S(1)}, u32[]{:S(2)}, u32[]{:S(2)}) async-start(bf16[8,80,128]{2,1,0:T(8,128)(2,1)} %grid.1), calls=%async_computation.3 | async-start | bytes 327680 | tf_op jit(solution)/shard_map/all_to_all | solution.py:917
  93.7 1.7 %collective-permute-start.2 = (bf16[3,2,64,128]{3,2,1,0:T(8,128)(2,1)S(1)}, bf16[3,2,64,128]{3,2,1,0:T(8,128)(2,1)S(1)}, u32[]{:S(2)}, u32[]{:S(2)}) collective-permute-start(bf16[3,2,64,128]{3,2,1,0:T(8,128)(2,1)S(1)} %get-tuple-element.30), channel_id=1, source_target_pairs={{0,8},{8,16},{16,24},{1,9},{9,17},{17,25},{2,10},{10,18},{18,26},{... | collective-permute-start | bytes 294920 | tf_op jit(solution)/shard_map/ppermute | solution.py:925
  95.4 1.3 %collective-permute-start.3 = (bf16[3,2,64,128]{3,2,1,0:T(8,128)(2,1)S(1)}, bf16[3,2,64,128]{3,2,1,0:T(8,128)(2,1)S(1)}, u32[]{:S(2)}, u32[]{:S(2)}) collective-permute-start(bf16[3,2,64,128]{3,2,1,0:T(8,128)(2,1)S(1)} %get-tuple-element.29), channel_id=1, source_target_pairs={{8,0},{16,8},{24,16},{9,1},{17,9},{25,17},{10,2},{18,10},{26,18},{... | collective-permute-start | bytes 294920 | tf_op jit(solution)/shard_map/ppermute | solution.py:926
  96.7 1.7 %collective-permute-done.2.above_ref = bf16[3,2,64,128]{3,2,1,0:T(8,128)(2,1)S(1)} collective-permute-done((bf16[3,2,64,128]{3,2,1,0:T(8,128)(2,1)S(1)}, bf16[3,2,64,128]{3,2,1,0:T(8,128)(2,1)S(1)}, u32[]{:S(2)}, u32[]{:S(2)}) %collective-permute-start.2) | collective-permute-done | bytes 98336 | tf_op jit(solution)/shard_map/ppermute | solution.py:925
  98.4 4.4 %collective-permute-done.3.below_ref = bf16[3,2,64,128]{3,2,1,0:T(8,128)(2,1)S(1)} collective-permute-done((bf16[3,2,64,128]{3,2,1,0:T(8,128)(2,1)S(1)}, bf16[3,2,64,128]{3,2,1,0:T(8,128)(2,1)S(1)}, u32[]{:S(2)}, u32[]{:S(2)}) %collective-permute-start.3) | collective-permute-done | bytes 98336 | tf_op jit(solution)/shard_map/ppermute | solution.py:926
  102.9 0.6 copy-done.41
  103.5 12.8 %near.1.near_ref = f32[2,64,512]{2,1,0:T(8,128)} custom-call(bf16[2,64,512]{2,1,0:T(8,128)(2,1)} %copy-done.16, bf16[2,64,512]{2,1,0:T(8,128)(2,1)} %copy-done.17, bf16[2,64,512]{2,1,0:T(8,128)(2,1)} %copy-done.18, bf16[3,2,64,128]{3,2,1,0:T(8,128)(2,1)} %copy-done.40, bf16[3,2,64,128]{3,2,1,0:T(8,128)(2,1)} %copy-done.41, s32[4,512]{1,0:T(4,128)} %partners_ref.1, ...), custom_call_target="tpu_custom_call" | custom-call | tf_op jit(solution)/shard_map/near/pallas_call | solution.py:927
  116.3 0.7 copy-done.15
  116.9 5.8 %far.1 = f32[2,64,512]{2,1,0:T(8,128)} custom-call(bf16[8,80,128]{2,1,0:T(8,128)(2,1)} %copy-done.15, bf16[64,64,512]{2,1,0:T(8,128)(2,1)} %projection_ref.3, s32[2,512]{1,0:T(2,128)} %shifts_ref.3, f32[2,64,512]{2,1,0:T(8,128)} %near.1.near_ref), custom_call_target="tpu_custom_call" | custom-call | tf_op jit(solution)/shard_map/far/pallas_call | solution.py:946
  (82 shorter events, 0.3 us)
Async XLA Ops:
  0.0 14.1 %copy-start.28 = (f32[512,128]{1,0:T(8,128)S(1)}, f32[512,128]{1,0:T(8,128)}, u32[]{:S(2)}) copy-start(f32[512,128]{1,0:T(8,128)} %constant.100.clone) | copy-start | bytes 786436
  0.0 14.1 %copy-start.29 = (f32[512,4]{1,0:T(8,128)S(1)}, f32[512,4]{1,0:T(8,128)}, u32[]{:S(2)}) copy-start(f32[512,4]{1,0:T(8,128)} %constant.98.clone) | copy-start | bytes 24580
  0.0 14.1 %copy-start.30 = (f32[512,128]{1,0:T(8,128)S(1)}, f32[512,128]{1,0:T(8,128)}, u32[]{:S(2)}) copy-start(f32[512,128]{1,0:T(8,128)} %constant.99.clone) | copy-start | bytes 786436
  0.0 14.1 %copy-start.31 = (f32[512,4]{1,0:T(8,128)S(1)}, f32[512,4]{1,0:T(8,128)}, u32[]{:S(2)}) copy-start(f32[512,4]{1,0:T(8,128)} %constant.97.clone) | copy-start | bytes 24580
  7.7 30.7 %all-to-all-start = ((bf16[8,80,128]{2,1,0:T(8,128)(2,1)}), bf16[8,80,128]{2,1,0:T(8,128)(2,1)}, u32[]{:S(2)}, u32[]{:S(2)}) async-start(bf16[8,80,128]{2,1,0:T(8,128)(2,1)} %charges.1), calls=%async_computation | async-start | bytes 327680 | tf_op jit(solution)/shard_map/all_to_all | solution.py:885
  14.1 4.5 %copy-start.36 = (f32[512,128]{1,0:T(8,128)S(1)}, f32[512,128]{1,0:T(8,128)}, u32[]{:S(2)}) copy-start(f32[512,128]{1,0:T(8,128)} %constant.105.clone) | copy-start | bytes 786436
  14.1 4.4 %copy-start.37 = (f32[512,4]{1,0:T(8,128)S(1)}, f32[512,4]{1,0:T(8,128)}, u32[]{:S(2)}) copy-start(f32[512,4]{1,0:T(8,128)} %constant.103.clone) | copy-start | bytes 24580
  14.1 4.4 %copy-start.38 = (f32[512,128]{1,0:T(8,128)S(1)}, f32[512,128]{1,0:T(8,128)}, u32[]{:S(2)}) copy-start(f32[512,128]{1,0:T(8,128)} %constant.104.clone) | copy-start | bytes 786436
  14.1 4.4 %copy-start.39 = (f32[512,4]{1,0:T(8,128)S(1)}, f32[512,4]{1,0:T(8,128)}, u32[]{:S(2)}) copy-start(f32[512,4]{1,0:T(8,128)} %constant.102.clone) | copy-start | bytes 24580
  18.6 3.6 %copy-start.19 = (f32[64,2048]{1,0:T(8,128)S(1)}, f32[64,2048]{1,0:T(8,128)}, u32[]{:S(2)}) copy-start(f32[64,2048]{1,0:T(8,128)} %param.41) | copy-start | bytes 1572868
  22.5 1.0 copy-start.32
  22.5 1.0 copy-start.33
  22.5 1.1 copy-start.34
  22.5 1.2 copy-start.35
  22.9 3.3 %copy-start.26 = (f32[128,512]{1,0:T(8,128)S(1)}, f32[128,512]{1,0:T(8,128)}, u32[]{:S(2)}) copy-start(f32[128,512]{1,0:T(8,128)} %constant.114.clone) | copy-start | bytes 786436
  22.9 3.3 %copy-start.27 = (f32[128,512]{1,0:T(8,128)S(1)}, f32[128,512]{1,0:T(8,128)}, u32[]{:S(2)}) copy-start(f32[128,512]{1,0:T(8,128)} %constant.113.clone) | copy-start | bytes 786436
  22.9 3.3 %copy-start.45 = (f32[4,512]{1,0:T(4,128)S(1)}, f32[4,512]{1,0:T(4,128)}, u32[]{:S(2)}) copy-start(f32[4,512]{1,0:T(4,128)} %constant.112.clone) | copy-start | bytes 24580
  22.9 3.3 %copy-start.46 = (f32[4,512]{1,0:T(4,128)S(1)}, f32[4,512]{1,0:T(4,128)}, u32[]{:S(2)}) copy-start(f32[4,512]{1,0:T(4,128)} %constant.111.clone) | copy-start | bytes 24580
  23.7 2.8 %copy-start.24 = (f32[128,512]{1,0:T(8,128)S(1)}, f32[128,512]{1,0:T(8,128)}, u32[]{:S(2)}) copy-start(f32[128,512]{1,0:T(8,128)} %constant.109.clone) | copy-start | bytes 786436
  23.7 2.8 %copy-start.25 = (f32[128,512]{1,0:T(8,128)S(1)}, f32[128,512]{1,0:T(8,128)}, u32[]{:S(2)}) copy-start(f32[128,512]{1,0:T(8,128)} %constant.108.clone) | copy-start | bytes 786436
  23.7 2.8 %copy-start.43 = (f32[4,512]{1,0:T(4,128)S(1)}, f32[4,512]{1,0:T(4,128)}, u32[]{:S(2)}) copy-start(f32[4,512]{1,0:T(4,128)} %constant.107.clone) | copy-start | bytes 24580
  23.7 2.8 %copy-start.44 = (f32[4,512]{1,0:T(4,128)S(1)}, f32[4,512]{1,0:T(4,128)}, u32[]{:S(2)}) copy-start(f32[4,512]{1,0:T(4,128)} %constant.106.clone) | copy-start | bytes 24580
  26.2 1.6 %copy-start.20 = (f32[512,128]{1,0:T(8,128)S(1)}, f32[512,128]{1,0:T(8,128)}, u32[]{:S(2)}) copy-start(f32[512,128]{1,0:T(8,128)} %constant.118.clone) | copy-start | bytes 786436
  26.3 1.5 %copy-start.21 = (f32[512,4]{1,0:T(8,128)S(1)}, f32[512,4]{1,0:T(8,128)}, u32[]{:S(2)}) copy-start(f32[512,4]{1,0:T(8,128)} %constant.116.clone) | copy-start | bytes 24580
  26.3 1.5 %copy-start.22 = (f32[512,128]{1,0:T(8,128)S(1)}, f32[512,128]{1,0:T(8,128)}, u32[]{:S(2)}) copy-start(f32[512,128]{1,0:T(8,128)} %constant.117.clone) | copy-start | bytes 786436
  26.3 1.5 %copy-start.23 = (f32[512,4]{1,0:T(8,128)S(1)}, f32[512,4]{1,0:T(8,128)}, u32[]{:S(2)}) copy-start(f32[512,4]{1,0:T(8,128)} %constant.115.clone) | copy-start | bytes 24580
  27.8 3.4 %copy-start = (f32[512,4,128]{2,1,0:T(4,128)S(1)}, f32[512,4,128]{2,1,0:T(4,128)}, u32[]{:S(2)}) copy-start(f32[512,4,128]{2,1,0:T(4,128)} %get-tuple-element.26) | copy-start | bytes 3145732
  27.8 3.4 %copy-start.42 = (f32[512]{0:T(512)S(1)}, f32[512]{0:T(512)}, u32[]{:S(2)}) copy-start(f32[512]{0:T(512)} %constant.110.clone) | copy-start | bytes 6148
  27.8 3.4 %copy-start.47 = (f32[512]{0:T(512)S(1)}, f32[512]{0:T(512)}, u32[]{:S(2)}) copy-start(f32[512]{0:T(512)} %constant.101.clone) | copy-start | bytes 6148
  31.2 2.6 %copy-start.6 = (f32[64,8,4,128]{3,1,2,0:T(8,128)S(1)}, f32[64,8,4,128]{3,1,2,0:T(8,128)}, u32[]{:S(2)}) copy-start(f32[64,8,4,128]{3,1,2,0:T(8,128)} %copy.59) | copy-start | bytes 3145732
  33.8 1.8 %copy-start.7 = (f32[64,8,4,128]{3,1,2,0:T(8,128)S(1)}, f32[64,8,4,128]{3,1,2,0:T(8,128)}, u32[]{:S(2)}) copy-start(f32[64,8,4,128]{3,1,2,0:T(8,128)} %copy.58) | copy-start | bytes 3145732
  38.4 10.4 %copy-start.5 = (f32[512,512]{1,0:T(8,128)S(1)}, f32[512,512]{1,0:T(8,128)}, u32[]{:S(2)}) copy-start(f32[512,512]{1,0:T(8,128)} %get-tuple-element.35) | copy-start | bytes 3145732
  42.5 18.1 %all-to-all-start.1 = ((bf16[32,40,128]{2,1,0:T(8,128)(2,1)}), bf16[32,40,128]{2,1,0:T(8,128)(2,1)S(1)}, u32[]{:S(2)}, u32[]{:S(2)}) async-start(bf16[32,40,128]{2,1,0:T(8,128)(2,1)} %columns.1), calls=%async_computation.1 | async-start | bytes 655360 | tf_op jit(solution)/shard_map/all_to_all | solution.py:905
  51.6 1.2 copy-start.1
  51.6 1.3 %copy-start.11 = (f32[512,128]{1,0:T(8,128)S(1)}, f32[512,128]{1,0:T(8,128)}, u32[]{:S(2)}) copy-start(f32[512,128]{1,0:T(8,128)} %get-tuple-element.19) | copy-start | bytes 786436
  51.6 1.3 %copy-start.12 = (f32[512,128]{1,0:T(8,128)S(1)}, f32[512,128]{1,0:T(8,128)}, u32[]{:S(2)}) copy-start(f32[512,128]{1,0:T(8,128)} %get-tuple-element.20) | copy-start | bytes 786436
  51.6 1.4 %copy-start.13 = (f32[512,128]{1,0:T(8,128)S(1)}, f32[512,128]{1,0:T(8,128)}, u32[]{:S(2)}) copy-start(f32[512,128]{1,0:T(8,128)} %get-tuple-element.21) | copy-start | bytes 786436
  51.7 1.5 %copy-start.14 = (f32[512,128]{1,0:T(8,128)S(1)}, f32[512,128]{1,0:T(8,128)}, u32[]{:S(2)}) copy-start(f32[512,128]{1,0:T(8,128)} %get-tuple-element.22) | copy-start | bytes 786436
  52.9 1.3 %copy-start.4 = (f32[512,512]{1,0:T(8,128)S(1)}, f32[512,512]{1,0:T(8,128)}, u32[]{:S(2)}) copy-start(f32[512,512]{1,0:T(8,128)} %get-tuple-element.34) | copy-start | bytes 3145732
  54.2 1.7 %copy-start.3 = (f32[512,512]{1,0:T(8,128)S(1)}, f32[512,512]{1,0:T(8,128)}, u32[]{:S(2)}) copy-start(f32[512,512]{1,0:T(8,128)} %get-tuple-element.36) | copy-start | bytes 3145732
  55.9 1.8 %copy-start.2 = (f32[512,512]{1,0:T(8,128)S(1)}, f32[512,512]{1,0:T(8,128)}, u32[]{:S(2)}) copy-start(f32[512,512]{1,0:T(8,128)} %get-tuple-element.33) | copy-start | bytes 3145732
  60.6 0.7 copy-start.9
  61.4 11.4 %copy-start.8 = (f32[2,64,512]{2,1,0:T(8,128)S(1)}, f32[2,64,512]{2,1,0:T(8,128)}, u32[]{:S(2)}) copy-start(f32[2,64,512]{2,1,0:T(8,128)} %currents_ref.1) | copy-start | bytes 786436
  68.2 16.6 %all-to-all-start.2 = ((bf16[32,40,128]{2,1,0:T(8,128)(2,1)}), bf16[32,40,128]{2,1,0:T(8,128)(2,1)S(1)}, u32[]{:S(2)}, u32[]{:S(2)}) async-start(bf16[32,40,128]{2,1,0:T(8,128)(2,1)} %rows.1), calls=%async_computation.2 | async-start | bytes 655360 | tf_op jit(solution)/shard_map/all_to_all | solution.py:911
  72.8 30.0 %copy-start.16 = (bf16[2,64,512]{2,1,0:T(8,128)(2,1)}, bf16[2,64,512]{2,1,0:T(8,128)(2,1)S(1)}, u32[]{:S(2)}) copy-start(bf16[2,64,512]{2,1,0:T(8,128)(2,1)S(1)} %convert_element_type.51.own_ref) | copy-start | bytes 393220
  72.8 20.8 %collective-permute-start = (bf16[2,64,512]{2,1,0:T(8,128)(2,1)S(1)}, bf16[2,64,512]{2,1,0:T(8,128)(2,1)S(1)}, u32[]{:S(2)}, u32[]{:S(2)}) collective-permute-start(bf16[2,64,512]{2,1,0:T(8,128)(2,1)S(1)} %convert_element_type.51.own_ref), channel_id=1, source_target_pairs={{0,1},{1,2},{2,3},{3,4},{4,5},{5,6},{6,7},{8,9},{9,10},{10,11},{11... | collective-permute-start | bytes 393224 | tf_op jit(solution)/shard_map/ppermute | solution.py:921
  75.0 18.6 %collective-permute-start.1 = (bf16[2,64,512]{2,1,0:T(8,128)(2,1)S(1)}, bf16[2,64,512]{2,1,0:T(8,128)(2,1)S(1)}, u32[]{:S(2)}, u32[]{:S(2)}) collective-permute-start(bf16[2,64,512]{2,1,0:T(8,128)(2,1)S(1)} %convert_element_type.51.own_ref), channel_id=1, source_target_pairs={{1,0},{2,1},{3,2},{4,3},{5,4},{6,5},{7,6},{9,8},{10,9},{11,10},{12... | collective-permute-start | bytes 393224 | tf_op jit(solution)/shard_map/ppermute | solution.py:922
  84.8 0.7 copy-start.10
  90.2 26.1 %all-to-all-start.3 = ((bf16[8,80,128]{2,1,0:T(8,128)(2,1)}), bf16[8,80,128]{2,1,0:T(8,128)(2,1)S(1)}, u32[]{:S(2)}, u32[]{:S(2)}) async-start(bf16[8,80,128]{2,1,0:T(8,128)(2,1)} %grid.1), calls=%async_computation.3 | async-start | bytes 327680 | tf_op jit(solution)/shard_map/all_to_all | solution.py:917
  93.6 9.2 %copy-start.17 = (bf16[2,64,512]{2,1,0:T(8,128)(2,1)}, bf16[2,64,512]{2,1,0:T(8,128)(2,1)S(1)}, u32[]{:S(2)}) copy-start(bf16[2,64,512]{2,1,0:T(8,128)(2,1)S(1)} %collective-permute-done.left_ref) | copy-start | bytes 393220
  93.6 9.2 %copy-start.18 = (bf16[2,64,512]{2,1,0:T(8,128)(2,1)}, bf16[2,64,512]{2,1,0:T(8,128)(2,1)S(1)}, u32[]{:S(2)}) copy-start(bf16[2,64,512]{2,1,0:T(8,128)(2,1)S(1)} %collective-permute-done.1.right_ref) | copy-start | bytes 393220
  93.7 4.7 %collective-permute-start.2 = (bf16[3,2,64,128]{3,2,1,0:T(8,128)(2,1)S(1)}, bf16[3,2,64,128]{3,2,1,0:T(8,128)(2,1)S(1)}, u32[]{:S(2)}, u32[]{:S(2)}) collective-permute-start(bf16[3,2,64,128]{3,2,1,0:T(8,128)(2,1)S(1)} %get-tuple-element.30), channel_id=1, source_target_pairs={{0,8},{8,16},{16,24},{1,9},{9,17},{17,25},{2,10},{10,18},{18,26},{... | collective-permute-start | bytes 294920 | tf_op jit(solution)/shard_map/ppermute | solution.py:925
  95.4 7.4 %collective-permute-start.3 = (bf16[3,2,64,128]{3,2,1,0:T(8,128)(2,1)S(1)}, bf16[3,2,64,128]{3,2,1,0:T(8,128)(2,1)S(1)}, u32[]{:S(2)}, u32[]{:S(2)}) collective-permute-start(bf16[3,2,64,128]{3,2,1,0:T(8,128)(2,1)S(1)} %get-tuple-element.29), channel_id=1, source_target_pairs={{8,0},{16,8},{24,16},{9,1},{17,9},{25,17},{10,2},{18,10},{26,18},{... | collective-permute-start | bytes 294920 | tf_op jit(solution)/shard_map/ppermute | solution.py:926
  98.4 4.4 %copy-start.40 = (bf16[3,2,64,128]{3,2,1,0:T(8,128)(2,1)}, bf16[3,2,64,128]{3,2,1,0:T(8,128)(2,1)S(1)}, u32[]{:S(2)}) copy-start(bf16[3,2,64,128]{3,2,1,0:T(8,128)(2,1)S(1)} %collective-permute-done.2.above_ref) | copy-start | bytes 294916
  102.8 0.6 copy-start.41
  116.3 0.7 copy-start.15
where the time goes:
time: 124 us; the launch traced here: 123 us
  Pallas kernels  41.9 us (34%)
  other arithmetic  29.3 us (24%)
  starting transfers between devices  27 us (22%)
  waiting for transfers between devices  15.8 us (13%)
  local copies, waits for them, and re-layouts  8.23 us (7%)
    sub x6, other arithmetic, basis_tables(): cosine = (cc * fc - cs * fs).reshape(shape)  13.2 us
    pallas_call x1, Pallas kernels, shards_real(): pl.pallas_call(near_kernel, grid=(BASIS // SUB,), in_specs=[whole((RHS, B...  12.8 us
    convert_element_type x6, other arithmetic, basis_tables(): tables.append((full - high).astype(jnp.bfloat16))  11.7 us
    all_to_all x1, waiting for transfers between devices, shards_real(): returned = lax.all_to_all(rows_back, ('row', 'col'), 0, 0, tiled=True)  8.51 us
    pallas_call x1, Pallas kernels, shards_real(): pl.pallas_call(charge_kernel, grid=(STEN,), in_specs=[whole((RHS, BASIS,...  7.65 us
    unnamed x101, local copies, waits for them, and re-layouts  7.24 us
    pallas_call x1, Pallas kernels, shards_real(): pl.pallas_call(functools.partial(row_kernel, row_count, col_count), out_s...  6.87 us
    all_to_all x1, starting transfers between devices, shards_real(): slab = lax.all_to_all(charges, 'col', 0, 0, tiled=True)  6.37 us
  transfers between devices with their start and end apart: 8, of which 4 were waited for; matrix products, arithmetic and copies ran while one was open for 27% of the time, Pallas kernels for 14%

commit v1 on v0

--- a/solution.py
+++ b/solution.py
@@ -420,21 +420,6 @@
     return jnp.concatenate(even, axis=1), jnp.concatenate(odd, axis=1)
 
 
-def join_spectrum(even, odd):
-    quarter = even.shape[1] // 2
-    ec, es = even[:, :quarter], even[:, quarter:]
-    oc, os = odd[:, :quarter], odd[:, quarter:]
-    return [ec + oc, es - os, ec - oc, es + os]
-
-
-def split_spectrum(blocks):
-    a, b, c, d = blocks
-    return (
-        jnp.concatenate([a + c, d + b], axis=1),
-        jnp.concatenate([a - c, d - b], axis=1),
-    )
-
-
 def scatter_rows(even, odd, count, put):
     rows = []
     for j in range(0, count, 2):
@@ -587,44 +572,109 @@
     return columns, rows
 
 
-def basis_tables(positions, length, lane_major):
-    quarter = length // 4
-    outer = np.arange(quarter // LANES) * LANES
-    inner = np.arange(LANES)
-    tables = []
+def angle_pair(left, right, length):
+    angles = 2.0 * np.pi * (np.asarray(left)[:, None] * np.asarray(right)[None, :] % length) / length
+    return np.asarray(np.cos(angles), np.float32), np.asarray(np.sin(angles), np.float32)
+
+
+def position_bases(positions, length):
+    orders = np.arange(length // 4)
+    grouped = positions.reshape(-1, SUB)
+    offsets = grouped[0] - grouped[0, 0]
+    assert (grouped == grouped[:, :1] + offsets[None, :]).all()
+    return (
+        *angle_pair(grouped[:, 0], orders, length),
+        *angle_pair(offsets, orders, length),
+        *angle_pair(offsets + 1, orders, length),
+    )
+
+
+def order_bases(positions, length):
+    bases = np.arange(0, length // 4, SUB)
+    result = []
     for parity in range(2):
-        x = positions + parity
-        coarse = 2.0 * np.pi * (x[:, None] * outer[None, :] % length) / length
-        fine = 2.0 * np.pi * (x[:, None] * inner[None, :] % length) / length
-        sign = np.where(positions % 4 == 0, 1.0, -1.0)
-        if lane_major:
-            shape_c, shape_f, shape_s = (1, 2), (0, 2), (0, 1)
-        parts = [np.cos(coarse), np.sin(coarse), np.cos(fine), np.sin(fine)]
-        parts = [np.asarray(p, np.float32) for p in parts]
-        sign = np.asarray(sign, np.float32)
-        if lane_major:
-            cc, cs = (jnp.asarray(np.ascontiguousarray(p.T))[:, None, :] for p in parts[:2])
-            fc, fs = (jnp.asarray(np.ascontiguousarray(p.T))[None, :, :] for p in parts[2:])
-            sg = jnp.asarray(sign)[None, :]
-            shape = (quarter, x.shape[0])
-            axis, order = 0, lax.broadcasted_iota(jnp.int32, shape, 0)
+        result.extend(angle_pair(bases, positions + parity, length))
+        result.extend(angle_pair(np.arange(SUB), positions + parity, length))
+    return tuple(result)
+
+
+def fill_by_position(sign_of, bases, out_refs):
+    base_cos, base_sin, even_cos, even_sin, odd_cos, odd_sin = bases
+    ec, es, oc, os = (ref[...] for ref in (even_cos, even_sin, odd_cos, odd_sin))
+    start = lane_index(ec.shape) == 0
+
+    def pair(i, carry):
+        parts = [[], [], []]
+        for h in range(2):
+            row = 2 * i + h
+            bc, bs = base_cos[pl.ds(row, 1), :], base_sin[pl.ds(row, 1), :]
+            parts[0].append(bc * ec - bs * es)
+            parts[1].append(jnp.where(start, 1.0, -(bs * ec + bc * es)) * sign_of(row))
+            parts[2].append(bc * oc - bs * os)
+        rows = pl.ds(pl.multiple_of(16 * i, 16), 16)
+        for ref, part in zip(out_refs, parts):
+            ref[rows, :] = jnp.concatenate(part, axis=0).astype(ref.dtype)
+        return carry
+
+    lax.fori_loop(0, base_cos.shape[0] // 2, pair, 0)
+
+
+def column_table_kernel(*refs):
+    fill_by_position(lambda row: (1 - 2 * ((row // 2) & 1)).astype(jnp.float32), refs[:6], refs[6:])
+
+
+def row_table_kernel(green_ref, *refs):
+    position, order, outs = refs[:6], refs[6:14], refs[14:]
+    quarter = position[0].shape[1]
+    tiles = quarter // LANES
+    sub = sub_index((SUB, quarter))
+    flip = jnp.where(sub < 4, 1.0, -1.0)
+    fill_by_position(lambda row: flip, position, outs[3:6])
+    ebc, ebs, ec, es, obc, obs, oc, os = order
+    ec, es, oc, os = (ref[...] for ref in (ec, es, oc, os))
+    lanes = jnp.where((lane_index((SUB, quarter)) & 4) == 0, 1.0, -1.0)
+
+    def pair(i, carry):
+        parts = [[], [], []]
+        for h in range(2):
+            row = 2 * i + h
+            one = (pl.ds(row, 1), slice(None))
+            bc, bs = ebc[one], ebs[one]
+            parts[0].append(bc * ec - bs * es)
+            first = (sub + row) == 0
+            parts[1].append(jnp.where(first, 1.0, -(bs * ec + bc * es)) * lanes)
+            parts[2].append(obc[one] * oc - obs[one] * os)
+        rows = pl.ds(pl.multiple_of(16 * i, 16), 16)
+        for ref, part in zip(outs[:3], parts):
+            ref[rows, :] = jnp.concatenate(part, axis=0).astype(ref.dtype)
+        return carry
+
+    lax.fori_loop(0, ebc.shape[0] // 2, pair, 0)
+
+    depth = green_ref.shape[0]
+    device = lax.axis_index("row") * lax.axis_size("col") + lax.axis_index("col")
+    number = sub_index((depth, LANES)) + device * depth
+    length = 4 * quarter
+    weight = jnp.where(number % quarter == 0, 1.0, 2.0) * (1.0 / (length * length))
+    lane = lane_index((depth, LANES))
+
+    def scaled(tile):
+        value = green_ref[:, LANES * tile : LANES * (tile + 1)] * weight
+        if tile % tiles == 0:
+            value = value * jnp.where(lane == 0, 1.0, 2.0)
         else:
-            cc, cs = (jnp.asarray(p)[:, :, None] for p in parts[:2])
-            fc, fs = (jnp.asarray(p)[:, None, :] for p in parts[2:])
-            sg = jnp.asarray(sign)[:, None]
-            shape = (x.shape[0], quarter)
-            axis, order = 1, lax.broadcasted_iota(jnp.int32, shape, 1)
-        cosine = (cc * fc - cs * fs).reshape(shape)
-        if parity == 0:
-            sine = (cs * fc + cc * fs).reshape(shape)
-            second = jnp.where(order == 0, 1.0, -sine) * sg
-        else:
-            second = cosine * sg
-        full = jnp.concatenate([cosine, second], axis=axis)
-        high = lax.reduce_precision(full, 8, 7)
-        tables.append(high.astype(jnp.bfloat16))
-        tables.append((full - high).astype(jnp.bfloat16))
-    return tables
+            value = value * 2.0
+        return jnp.concatenate([value, value], axis=0)
+
+    for t in range(tiles):
+        cos_plus, cos_minus = scaled(t), scaled(2 * tiles + t)
+        sin_minus, sin_plus = scaled(tiles + t), scaled(3 * tiles + t)
+        first = slice(LANES * t, LANES * (t + 1))
+        second = slice(quarter + LANES * t, quarter + LANES * (t + 1))
+        outs[6][first, :] = (cos_plus + cos_minus).T
+        outs[7][first, :] = (cos_plus - cos_minus).T
+        outs[6][second, :] = (sin_plus + sin_minus).T
+        outs[7][second, :] = (sin_plus - sin_minus).T
 
 
 def tiled_shifts(shifts_ref, which):
@@ -666,53 +716,66 @@
             out_ref[e] = jnp.concatenate(chunks[e], axis=0).astype(out_ref.dtype)
 
 
-def column_kernel(count, rows_ref, eh, el, oh, ol, out_ref):
+def column_sign(shape):
+    return jnp.where((lane_index(shape) & EC) == 0, 1.0, -1.0)
+
+
+def column_kernel(count, rows_ref, even_cos, even_sin, odd_cos, out_ref):
     def part(j, r):
         return rows_ref[j, 8 * r : 8 * r + 8, :].astype(jnp.float32)
 
     even, odd = gather_rows(part, lambda j: part(j, GROUPS), count)
+    both = jnp.concatenate([odd, odd * column_sign(odd.shape)], axis=0).astype(jnp.bfloat16)
     even = even.astype(jnp.bfloat16)
-    odd = odd.astype(jnp.bfloat16)
-    blocks = join_spectrum(
-        dot(even, eh[...]) + dot(even, el[...]), dot(odd, oh[...]) + dot(odd, ol[...])
-    )
+    ec, es = dot(even, even_cos[...]), dot(even, even_sin[...])
+    both = dot(both, odd_cos[...])
+    oc, os = both[: odd.shape[0]], both[odd.shape[0] :]
     half = out_ref.shape[1]
     device = 0
-    for block in blocks:
+    for block in (ec + oc, es - os, ec - oc, es + os):
         for t in range(0, block.shape[1], LANES):
             for chunk in halves(block[:half, t : t + LANES], block[half:, t : t + LANES]):
                 out_ref[device] = chunk.astype(out_ref.dtype)
                 device += 1
 
 
-def row_kernel(row_count, col_count, in_ref, eh, el, oh, ol, teh, tel, toh, tol, sum_ref, diff_ref, out_ref):
+def row_kernel(row_count, col_count, in_ref, even_cos, even_sin, odd_cos, back_cos, back_sin, back_odd,
+               sum_ref, diff_ref, out_ref):
     even, odd = add_outer_rows(
         lambda i, j: in_ref[i * col_count + j].astype(jnp.float32), row_count, col_count
     )
+    flip = jnp.where((sub_index(odd.shape) & 4) == 0, 1.0, -1.0)
+    both = jnp.concatenate([odd, odd * flip], axis=1).astype(jnp.bfloat16)
     even = even.astype(jnp.bfloat16)
-    odd = odd.astype(jnp.bfloat16)
-    a = dot(eh[...], even) + dot(el[...], even)
-    b = dot(oh[...], odd) + dot(ol[...], odd)
-    plus, minus = sum_ref[...], diff_ref[...]
-
-    def back(value, high_ref, low_ref):
-        high, low = two_terms(value)
-        both = dot(high_ref[...], jnp.concatenate([high, low], axis=1))
-        return both[:, :LANES] + both[:, LANES:] + dot(low_ref[...], high)
+    a = [dot(even_cos[...], even), dot(even_sin[...], even)]
+    both = dot(odd_cos[...], both)
+    b = [both[:, :LANES], both[:, LANES:]]
+    quarter = odd.shape[0]
+
+    def pieces(left, right):
+        for k in range(2):
+            span = slice(quarter * k, quarter * (k + 1))
+            yield two_terms(left[k] * sum_ref[span, :] + right[k] * diff_ref[span, :])
+
+    def fold(value):
+        return value[:, :LANES] + value[:, LANES:]
+
+    (ch, cl), (sh, sl) = pieces(a, b)
+    even = fold(
+        dot(back_cos[...], jnp.concatenate([ch, cl], axis=1))
+        + dot(back_sin[...], jnp.concatenate([sh, sl], axis=1))
+    )
+    (ch, cl), (sh, sl) = pieces(b, a)
+    both = dot(back_odd[...], jnp.concatenate([ch, cl, sh, sl], axis=1))
+    odd = fold(both[:, : 2 * LANES]) + fold(both[:, 2 * LANES :]) * flip
 
     def put(i, j, parts):
         out_ref[i * col_count + j] = jnp.concatenate(parts, axis=0).astype(out_ref.dtype)
 
-    spread_outer_rows(
-        back(a * plus + b * minus, teh, tel),
-        back(a * minus + b * plus, toh, tol),
-        row_count,
-        col_count,
-        put,
-    )
-
-
-def grid_kernel(count, in_ref, eh, el, oh, ol, out_ref):
+    spread_outer_rows(even, odd, row_count, col_count, put)
+
+
+def grid_kernel(count, in_ref, even_cos, even_sin, odd_cos, out_ref):
     devices = in_ref.shape[0]
     first, second = [], []
     for d in range(0, devices, 2):
@@ -728,20 +791,25 @@
                 [jnp.concatenate(first[span], axis=1), jnp.concatenate(second[span], axis=1)], axis=0
             )
         )
-    contract = ((1,), (1,))
-
-    def back(value, high_ref, low_ref):
-        high, low = two_terms(value)
-        both = dot(jnp.concatenate([high, low], axis=0), high_ref[...], contract)
-        half = high.shape[0]
-        return both[:half] + both[half:] + dot(high, low_ref[...], contract)
-
-    even, odd = split_spectrum(blocks)
+    cos_plus, sin_minus, cos_minus, sin_plus = blocks
+    half = cos_plus.shape[0]
+
+    def back(values, table):
+        terms = [term for value in values for term in two_terms(value)]
+        result = dot(jnp.concatenate(terms, axis=0), table[...], ((1,), (1,)))
+        return [
+            result[2 * half * i : 2 * half * i + half] + result[2 * half * i + half : 2 * half * (i + 1)]
+            for i in range(len(values))
+        ]
+
+    even = back([cos_plus + cos_minus], even_cos)[0] + back([sin_plus + sin_minus], even_sin)[0]
+    odd, turned = back([cos_plus - cos_minus, sin_plus - sin_minus], odd_cos)
+    odd = odd + turned * column_sign(odd.shape)
 
     def put(j, parts):
         out_ref[j] = jnp.concatenate(parts, axis=0).astype(out_ref.dtype)
 
-    scatter_rows(back(even, eh, el), back(odd, oh, ol), count, put)
+    scatter_rows(even, odd, count, put)
 
 
 def far_kernel(grid_ref, projection_ref, shifts_ref, near_ref, out_ref, samples):
@@ -885,17 +953,14 @@
     slab = lax.all_to_all(charges, "col", 0, 0, tiled=True)
 
     columns, rows = even_positions(row_count, col_count)
-    col_tables = basis_tables(columns, length, False)
-    row_tables = basis_tables(rows, length, True)
-    back_tables = basis_tables(rows, length, False)
-    weight_k = jnp.where(jnp.arange(length) % quarter == 0, 1.0, 2.0).astype(f32)
-    mine = lax.axis_index("row") * col_count + lax.axis_index("col")
-    depth = green.shape[0]
-    weight_m = jnp.where((mine * depth + jnp.arange(depth)) % quarter == 0, 1.0, 2.0).astype(f32)
-    scaled = green * (weight_m * (1.0 / (length * length)))[:, None] * weight_k[None, :]
-    scaled = jnp.concatenate([scaled, scaled], axis=0).T
-    upper = jnp.concatenate([scaled[:quarter], scaled[3 * quarter :]], axis=0)
-    lower = jnp.concatenate([scaled[2 * quarter : 3 * quarter], scaled[quarter : 2 * quarter]], axis=0)
+    table = struct((quarter, quarter), b16)
+    col_tables = pl.pallas_call(column_table_kernel, out_shape=[table] * 3, name="column_tables")(
+        *position_bases(columns, length)
+    )
+    spread = struct((2 * quarter, LANES), f32)
+    row_tables = pl.pallas_call(
+        row_table_kernel, out_shape=[table] * 6 + [spread] * 2, name="row_tables"
+    )(green, *position_bases(rows, length), *order_bases(rows, length))
 
     spectrum = pl.pallas_call(
         functools.partial(column_kernel, col_count),
@@ -907,7 +972,7 @@
         functools.partial(row_kernel, row_count, col_count),
         out_shape=struct((devices, 40, LANES), b16),
         name="rows",
-    )(arrived, *row_tables, *back_tables, upper + lower, upper - lower)
+    )(arrived, *row_tables)
     returned = lax.all_to_all(rows_back, ("row", "col"), 0, 0, tiled=True)
     potential = pl.pallas_call(
         functools.partial(grid_kernel, col_count),

time: 124 us -> 97.6 us (0.79)
  other arithmetic: 29.3 us -> 1.03 us
  waiting for transfers between devices: 15.8 us -> 25.5 us
  local copies, waits for them, and re-layouts: 8.23 us -> 3.45 us
  starting transfers between devices: 27 us -> 22.6 us
  Pallas kernels: 41.9 us -> 43.9 us
    sub x7 -> x0, other arithmetic: 14.3 us -> none  [the longest x6 13.2 us: basis_tables(): cosine = (cc * fc - cs * fs).reshape(shape)]
    convert_element_type x6 -> x0, other arithmetic: 11.7 us -> none  [basis_tables(): tables.append((full - high).astype(jnp.bfloat16))]
    pallas_call x0 -> x2, Pallas kernels: none -> 7.6 us  [the longest x1 4.72 us: shards_real(): pl.pallas_call(row_table_kernel, out_shape=[table] * 6 + [spread] * 2, na...]
    all_to_all x1, waiting for transfers between devices: 1.11 us -> 7.3 us  [shards_real(): arrived = lax.all_to_all(spectrum, ('row', 'col'), 0, 0, tiled=True)]
    all_to_all x1, waiting for transfers between devices: 0.01 us -> 4.3 us  [shards_real(): slab = lax.all_to_all(charges, 'col', 0, 0, tiled=True)]
    unnamed x101 -> x20, local copies, waits for them, and re-layouts: 7.24 us -> 3.45 us
    mul x3 -> x0, other arithmetic: 2.94 us -> none  [the longest x1 2.59 us: basis_tables(): second = cosine * sg]
    pallas_call x1, Pallas kernels: 6.87 us -> 4.19 us  [shards_real(): pl.pallas_call(functools.partial(row_kernel, row_count, col_count), out_s...]
  transfers between devices with their start and end apart: 8 -> 8, of which waited for: 4 -> 5; matrix products, arithmetic and copies ran while one was open for 27% -> 1% of each run, Pallas kernels for 14% -> 24%
where the time goes in v1:
time: 97.6 us; the launch traced here: 96.6 us
  Pallas kernels  43.9 us (45%)
  waiting for transfers between devices  25.5 us (26%)
  starting transfers between devices  22.6 us (23%)
  local copies, waits for them, and re-layouts  3.45 us (4%)
  other arithmetic  1.03 us (1%)
    pallas_call x1, Pallas kernels, shards_real(): pl.pallas_call(near_kernel, grid=(BASIS // SUB,), in_specs=[whole((RHS, B...  12.8 us
    all_to_all x1, waiting for transfers between devices, shards_real(): returned = lax.all_to_all(rows_back, ('row', 'col'), 0, 0, tiled=True)  7.71 us
    pallas_call x1, Pallas kernels, shards_real(): pl.pallas_call(charge_kernel, grid=(STEN,), in_specs=[whole((RHS, BASIS,...  7.61 us
    all_to_all x1, waiting for transfers between devices, shards_real(): arrived = lax.all_to_all(spectrum, ('row', 'col'), 0, 0, tiled=True)  7.3 us
    all_to_all x1, starting transfers between devices, shards_real(): slab = lax.all_to_all(charges, 'col', 0, 0, tiled=True)  6.35 us
    pallas_call x1, Pallas kernels, shards_real(): pl.pallas_call(far_kernel, grid=(BASIS // depth,), in_specs=[whole((SUB,...  5.84 us
    pallas_call x1, Pallas kernels, shards_real(): pl.pallas_call(row_table_kernel, out_shape=[table] * 6 + [spread] * 2, na...  4.72 us
    ppermute x1, waiting for transfers between devices, shards_real(): below = lax.ppermute(three[..., :LANES], 'row', backward)  4.43 us
  transfers between devices with their start and end apart: 8, of which 5 were waited for; matrix products, arithmetic and copies ran while one was open for 1% of the time, Pallas kernels for 24%

profile of v1, /device:TPU:0, one launch (start us, length us, event | category | flops | bytes accessed | tf_op | source)
XLA Modules:
  0.0 96.6 jit_solution(5443140144012565215)
XLA Ops:
  0.0 0.0 copy-start
  0.0 7.6 %charges.1 = bf16[8,80,128]{2,1,0:T(8,128)(2,1)} custom-call(f32[2,64,512]{2,1,0:T(8,128)} %currents_ref.1, bf16[64,64,512]{2,1,0:T(8,128)(2,1)} %projection_ref.3, s32[2,512]{1,0:T(2,128)} %shifts_ref.3), custom_call_target="tpu_custom_call" | custom-call | tf_op jit(solution)/shard_map/charges/pallas_call | solution.py:936
  7.6 6.4 %all-to-all-start = ((bf16[8,80,128]{2,1,0:T(8,128)(2,1)}), bf16[8,80,128]{2,1,0:T(8,128)(2,1)S(1)}, u32[]{:S(2)}, u32[]{:S(2)}) async-start(bf16[8,80,128]{2,1,0:T(8,128)(2,1)} %charges.1), calls=%async_computation | async-start | bytes 327680 | tf_op jit(solution)/shard_map/all_to_all | solution.py:953
  14.0 2.9 %column_tables.1 = (bf16[512,512]{1,0:T(8,128)(2,1)}, bf16[512,512]{1,0:T(8,128)(2,1)}, bf16[512,512]{1,0:T(8,128)(2,1)}) custom-call(f32[64,512]{1,0:T(8,128)} %constant.40.clone.refs_0_, f32[64,512]{1,0:T(8,128)} %constant.41.clone.refs_1_, f32[8,512]{1,0:T(8,128)} %constant.42.clone.refs_2_, f32[8,512]{1,0:T(8,128)} %constant.43.clone.refs_3_, ...), custom_call_target="tpu_custom_call" | custom-call | tf_op jit(solution)/shard_map/column_tables/pallas_call | solution.py:957
  16.8 4.3 %all-to-all-done.rows_ref = bf16[8,80,128]{2,1,0:T(8,128)(2,1)S(1)} async-done(((bf16[8,80,128]{2,1,0:T(8,128)(2,1)}), bf16[8,80,128]{2,1,0:T(8,128)(2,1)S(1)}, u32[]{:S(2)}, u32[]{:S(2)}) %all-to-all-start) | async-done | bytes 163872 | tf_op jit(solution)/shard_map/all_to_all | solution.py:953
  21.1 0.0 copy-start.4
  21.2 0.7 copy-done.4
  21.8 2.8 %columns.1 = bf16[32,40,128]{2,1,0:T(8,128)(2,1)} custom-call(bf16[8,80,128]{2,1,0:T(8,128)(2,1)} %copy-done.4, bf16[512,512]{1,0:T(8,128)(2,1)} %get-tuple-element.16.even_cos, bf16[512,512]{1,0:T(8,128)(2,1)} %get-tuple-element.17.even_sin, bf16[512,512]{1,0:T(8,128)(2,1)} %get-tuple-element.18.odd_cos), custom_call_target="tpu_custom_call" | custom-call | tf_op jit(solution)/shard_map/columns/pallas_call | solution.py:965
  24.6 4.0 %all-to-all-start.1 = ((bf16[32,40,128]{2,1,0:T(8,128)(2,1)}), bf16[32,40,128]{2,1,0:T(8,128)(2,1)S(1)}, u32[]{:S(2)}, u32[]{:S(2)}) async-start(bf16[32,40,128]{2,1,0:T(8,128)(2,1)} %columns.1), calls=%async_computation.1 | async-start | bytes 655360 | tf_op jit(solution)/shard_map/all_to_all | solution.py:970
  28.6 4.7 %row_tables.1 = (bf16[512,512]{1,0:T(8,128)(2,1)}, bf16[512,512]{1,0:T(8,128)(2,1)}, bf16[512,512]{1,0:T(8,128)(2,1)}, bf16[512,512]{1,0:T(8,128)(2,1)}, bf16[51...) custom-call(f32[64,2048]{1,0:T(8,128)} %green_ref.1, ...), custom_call_target="tpu_custom_call" | custom-call | tf_op jit(solution)/shard_map/row_tables/pallas_call | solution.py:961
  33.3 7.3 %all-to-all-done.1.in_ref = bf16[32,40,128]{2,1,0:T(8,128)(2,1)S(1)} async-done(((bf16[32,40,128]{2,1,0:T(8,128)(2,1)}), bf16[32,40,128]{2,1,0:T(8,128)(2,1)S(1)}, u32[]{:S(2)}, u32[]{:S(2)}) %all-to-all-start.1) | async-done | bytes 327712 | tf_op jit(solution)/shard_map/all_to_all | solution.py:970
  40.6 0.0 copy-start.1
  40.6 0.7 copy-done.1
  41.3 4.2 %rows.1 = bf16[32,40,128]{2,1,0:T(8,128)(2,1)} custom-call(bf16[32,40,128]{2,1,0:T(8,128)(2,1)} %copy-done.1, bf16[512,512]{1,0:T(8,128)(2,1)} %get-tuple-element.19.even_cos, bf16[512,512]{1,0:T(8,128)(2,1)} %get-tuple-element.20.even_sin, bf16[512,512]{1,0:T(8,128)(2,1)} %get-tuple-element.21.odd_cos, bf16[512,512]{1,0:T(8,128)(2,1)} %get-tuple-element.22.back_cos, ...), custom_call_target="tpu_custom_call" | custom-call | tf_op jit(solution)/shard_map/rows/pallas_call | solution.py:971
  45.5 2.6 %all-to-all-start.2 = ((bf16[32,40,128]{2,1,0:T(8,128)(2,1)}), bf16[32,40,128]{2,1,0:T(8,128)(2,1)S(1)}, u32[]{:S(2)}, u32[]{:S(2)}) async-start(bf16[32,40,128]{2,1,0:T(8,128)(2,1)} %rows.1), calls=%async_computation.2 | async-start | bytes 655360 | tf_op jit(solution)/shard_map/all_to_all | solution.py:976
  48.1 1.0 %convert_element_type.3.own_ref = bf16[2,64,512]{2,1,0:T(8,128)(2,1)S(1)} convert(f32[2,64,512]{2,1,0:T(8,128)} %currents_ref.1) | non-fusion elementwise | flops 65536 | bytes 393216 | tf_op jit(solution)/shard_map/convert_element_type | solution.py:984
  49.1 0.0 copy-start.5
  49.1 2.0 %collective-permute-start = (bf16[2,64,512]{2,1,0:T(8,128)(2,1)S(1)}, bf16[2,64,512]{2,1,0:T(8,128)(2,1)S(1)}, u32[]{:S(2)}, u32[]{:S(2)}) collective-permute-start(bf16[2,64,512]{2,1,0:T(8,128)(2,1)S(1)} %convert_element_type.3.own_ref), channel_id=1, source_target_pairs={{0,1},{1,2},{2,3},{3,4},{4,5},{5,6},{6,7},{8,9},{9,10},{10,11},{11... | collective-permute-start | bytes 393224 | tf_op jit(solution)/shard_map/ppermute | solution.py:986
  51.1 1.3 %collective-permute-start.1 = (bf16[2,64,512]{2,1,0:T(8,128)(2,1)S(1)}, bf16[2,64,512]{2,1,0:T(8,128)(2,1)S(1)}, u32[]{:S(2)}, u32[]{:S(2)}) collective-permute-start(bf16[2,64,512]{2,1,0:T(8,128)(2,1)S(1)} %convert_element_type.3.own_ref), channel_id=1, source_target_pairs={{1,0},{2,1},{3,2},{4,3},{5,4},{6,5},{7,6},{9,8},{10,9},{11,10},{12... | collective-permute-start | bytes 393224 | tf_op jit(solution)/shard_map/ppermute | solution.py:987
  52.4 7.7 %all-to-all-done.2.in_ref = bf16[32,40,128]{2,1,0:T(8,128)(2,1)S(1)} async-done(((bf16[32,40,128]{2,1,0:T(8,128)(2,1)}), bf16[32,40,128]{2,1,0:T(8,128)(2,1)S(1)}, u32[]{:S(2)}, u32[]{:S(2)}) %all-to-all-start.2) | async-done | bytes 327712 | tf_op jit(solution)/shard_map/all_to_all | solution.py:976
  60.1 0.0 copy-start.2
  60.1 0.7 copy-done.2
  60.9 3.1 %grid.1 = bf16[8,80,128]{2,1,0:T(8,128)(2,1)} custom-call(bf16[32,40,128]{2,1,0:T(8,128)(2,1)} %copy-done.2, bf16[512,512]{1,0:T(8,128)(2,1)} %get-tuple-element.16.even_cos, bf16[512,512]{1,0:T(8,128)(2,1)} %get-tuple-element.17.even_sin, bf16[512,512]{1,0:T(8,128)(2,1)} %get-tuple-element.18.odd_cos), custom_call_target="tpu_custom_call" | custom-call | tf_op jit(solution)/shard_map/grid/pallas_call | solution.py:977
  64.0 3.4 %all-to-all-start.3 = ((bf16[8,80,128]{2,1,0:T(8,128)(2,1)}), bf16[8,80,128]{2,1,0:T(8,128)(2,1)S(1)}, u32[]{:S(2)}, u32[]{:S(2)}) async-start(bf16[8,80,128]{2,1,0:T(8,128)(2,1)} %grid.1), calls=%async_computation.3 | async-start | bytes 327680 | tf_op jit(solution)/shard_map/all_to_all | solution.py:982
  67.4 0.0 copy-done
  67.4 0.0 collective-permute-done.left_ref
  67.4 0.0 copy-start.6
  67.4 0.0 collective-permute-done.1.right_ref
  67.4 0.0 copy-start.7
  67.5 1.7 %collective-permute-start.2 = (bf16[3,2,64,128]{3,2,1,0:T(8,128)(2,1)S(1)}, bf16[3,2,64,128]{3,2,1,0:T(8,128)(2,1)S(1)}, u32[]{:S(2)}, u32[]{:S(2)}) collective-permute-start(bf16[3,2,64,128]{3,2,1,0:T(8,128)(2,1)S(1)} %get-tuple-element.28), channel_id=1, source_target_pairs={{0,8},{8,16},{16,24},{1,9},{9,17},{17,25},{2,10},{10,18},{18,26},{... | collective-permute-start | bytes 294920 | tf_op jit(solution)/shard_map/ppermute | solution.py:990
  69.2 1.3 %collective-permute-start.3 = (bf16[3,2,64,128]{3,2,1,0:T(8,128)(2,1)S(1)}, bf16[3,2,64,128]{3,2,1,0:T(8,128)(2,1)S(1)}, u32[]{:S(2)}, u32[]{:S(2)}) collective-permute-start(bf16[3,2,64,128]{3,2,1,0:T(8,128)(2,1)S(1)} %get-tuple-element.27), channel_id=1, source_target_pairs={{8,0},{16,8},{24,16},{9,1},{17,9},{25,17},{10,2},{18,10},{26,18},{... | collective-permute-start | bytes 294920 | tf_op jit(solution)/shard_map/ppermute | solution.py:991
  70.5 1.7 %collective-permute-done.2.above_ref = bf16[3,2,64,128]{3,2,1,0:T(8,128)(2,1)S(1)} collective-permute-done((bf16[3,2,64,128]{3,2,1,0:T(8,128)(2,1)S(1)}, bf16[3,2,64,128]{3,2,1,0:T(8,128)(2,1)S(1)}, u32[]{:S(2)}, u32[]{:S(2)}) %collective-permute-start.2) | collective-permute-done | bytes 98336 | tf_op jit(solution)/shard_map/ppermute | solution.py:990
  72.2 0.0 copy-start.8
  72.2 4.4 %collective-permute-done.3.below_ref = bf16[3,2,64,128]{3,2,1,0:T(8,128)(2,1)S(1)} collective-permute-done((bf16[3,2,64,128]{3,2,1,0:T(8,128)(2,1)S(1)}, bf16[3,2,64,128]{3,2,1,0:T(8,128)(2,1)S(1)}, u32[]{:S(2)}, u32[]{:S(2)}) %collective-permute-start.3) | collective-permute-done | bytes 98336 | tf_op jit(solution)/shard_map/ppermute | solution.py:991
  76.6 0.0 copy-done.5
  76.6 0.0 copy-done.6
  76.6 0.0 copy-done.7
  76.6 0.0 copy-done.8
  76.6 0.0 copy-start.9
  76.7 0.6 copy-done.9
  77.3 12.8 %near.1.near_ref = f32[2,64,512]{2,1,0:T(8,128)} custom-call(bf16[2,64,512]{2,1,0:T(8,128)(2,1)} %copy-done.5, bf16[2,64,512]{2,1,0:T(8,128)(2,1)} %copy-done.6, bf16[2,64,512]{2,1,0:T(8,128)(2,1)} %copy-done.7, bf16[3,2,64,128]{3,2,1,0:T(8,128)(2,1)} %copy-done.8, bf16[3,2,64,128]{3,2,1,0:T(8,128)(2,1)} %copy-done.9, s32[4,512]{1,0:T(4,128)} %partners_ref.1, ...), custom_call_target="tpu_custom_call" | custom-call | tf_op jit(solution)/shard_map/near/pallas_call | solution.py:992
  90.1 0.0 all-to-all-done.3.grid_ref
  90.1 0.0 copy-start.3
  90.1 0.6 copy-done.3
  90.8 5.8 %far.1 = f32[2,64,512]{2,1,0:T(8,128)} custom-call(bf16[8,80,128]{2,1,0:T(8,128)(2,1)} %copy-done.3, bf16[64,64,512]{2,1,0:T(8,128)(2,1)} %projection_ref.3, s32[2,512]{1,0:T(2,128)} %shifts_ref.3, f32[2,64,512]{2,1,0:T(8,128)} %near.1.near_ref), custom_call_target="tpu_custom_call" | custom-call | tf_op jit(solution)/shard_map/far/pallas_call | solution.py:1011
  (2 shorter events, 0.1 us)
Async XLA Ops:
  0.0 67.4 %copy-start = (f32[2,64,512]{2,1,0:T(8,128)S(1)}, f32[2,64,512]{2,1,0:T(8,128)}, u32[]{:S(2)}) copy-start(f32[2,64,512]{2,1,0:T(8,128)} %currents_ref.1) | copy-start | bytes 786436
  7.6 13.5 %all-to-all-start = ((bf16[8,80,128]{2,1,0:T(8,128)(2,1)}), bf16[8,80,128]{2,1,0:T(8,128)(2,1)S(1)}, u32[]{:S(2)}, u32[]{:S(2)}) async-start(bf16[8,80,128]{2,1,0:T(8,128)(2,1)} %charges.1), calls=%async_computation | async-start | bytes 327680 | tf_op jit(solution)/shard_map/all_to_all | solution.py:953
  21.1 0.7 copy-start.4
  24.6 16.0 %all-to-all-start.1 = ((bf16[32,40,128]{2,1,0:T(8,128)(2,1)}), bf16[32,40,128]{2,1,0:T(8,128)(2,1)S(1)}, u32[]{:S(2)}, u32[]{:S(2)}) async-start(bf16[32,40,128]{2,1,0:T(8,128)(2,1)} %columns.1), calls=%async_computation.1 | async-start | bytes 655360 | tf_op jit(solution)/shard_map/all_to_all | solution.py:970
  40.6 0.7 copy-start.1
  45.5 14.6 %all-to-all-start.2 = ((bf16[32,40,128]{2,1,0:T(8,128)(2,1)}), bf16[32,40,128]{2,1,0:T(8,128)(2,1)S(1)}, u32[]{:S(2)}, u32[]{:S(2)}) async-start(bf16[32,40,128]{2,1,0:T(8,128)(2,1)} %rows.1), calls=%async_computation.2 | async-start | bytes 655360 | tf_op jit(solution)/shard_map/all_to_all | solution.py:976
  49.1 27.5 %copy-start.5 = (bf16[2,64,512]{2,1,0:T(8,128)(2,1)}, bf16[2,64,512]{2,1,0:T(8,128)(2,1)S(1)}, u32[]{:S(2)}) copy-start(bf16[2,64,512]{2,1,0:T(8,128)(2,1)S(1)} %convert_element_type.3.own_ref) | copy-start | bytes 393220
  49.1 18.3 %collective-permute-start = (bf16[2,64,512]{2,1,0:T(8,128)(2,1)S(1)}, bf16[2,64,512]{2,1,0:T(8,128)(2,1)S(1)}, u32[]{:S(2)}, u32[]{:S(2)}) collective-permute-start(bf16[2,64,512]{2,1,0:T(8,128)(2,1)S(1)} %convert_element_type.3.own_ref), channel_id=1, source_target_pairs={{0,1},{1,2},{2,3},{3,4},{4,5},{5,6},{6,7},{8,9},{9,10},{10,11},{11... | collective-permute-start | bytes 393224 | tf_op jit(solution)/shard_map/ppermute | solution.py:986
  51.1 16.3 %collective-permute-start.1 = (bf16[2,64,512]{2,1,0:T(8,128)(2,1)S(1)}, bf16[2,64,512]{2,1,0:T(8,128)(2,1)S(1)}, u32[]{:S(2)}, u32[]{:S(2)}) collective-permute-start(bf16[2,64,512]{2,1,0:T(8,128)(2,1)S(1)} %convert_element_type.3.own_ref), channel_id=1, source_target_pairs={{1,0},{2,1},{3,2},{4,3},{5,4},{6,5},{7,6},{9,8},{10,9},{11,10},{12... | collective-permute-start | bytes 393224 | tf_op jit(solution)/shard_map/ppermute | solution.py:987
  60.1 0.7 copy-start.2
  64.0 26.1 %all-to-all-start.3 = ((bf16[8,80,128]{2,1,0:T(8,128)(2,1)}), bf16[8,80,128]{2,1,0:T(8,128)(2,1)S(1)}, u32[]{:S(2)}, u32[]{:S(2)}) async-start(bf16[8,80,128]{2,1,0:T(8,128)(2,1)} %grid.1), calls=%async_computation.3 | async-start | bytes 327680 | tf_op jit(solution)/shard_map/all_to_all | solution.py:982
  67.4 9.2 %copy-start.6 = (bf16[2,64,512]{2,1,0:T(8,128)(2,1)}, bf16[2,64,512]{2,1,0:T(8,128)(2,1)S(1)}, u32[]{:S(2)}) copy-start(bf16[2,64,512]{2,1,0:T(8,128)(2,1)S(1)} %collective-permute-done.left_ref) | copy-start | bytes 393220
  67.4 9.2 %copy-start.7 = (bf16[2,64,512]{2,1,0:T(8,128)(2,1)}, bf16[2,64,512]{2,1,0:T(8,128)(2,1)S(1)}, u32[]{:S(2)}) copy-start(bf16[2,64,512]{2,1,0:T(8,128)(2,1)S(1)} %collective-permute-done.1.right_ref) | copy-start | bytes 393220
  67.5 4.7 %collective-permute-start.2 = (bf16[3,2,64,128]{3,2,1,0:T(8,128)(2,1)S(1)}, bf16[3,2,64,128]{3,2,1,0:T(8,128)(2,1)S(1)}, u32[]{:S(2)}, u32[]{:S(2)}) collective-permute-start(bf16[3,2,64,128]{3,2,1,0:T(8,128)(2,1)S(1)} %get-tuple-element.28), channel_id=1, source_target_pairs={{0,8},{8,16},{16,24},{1,9},{9,17},{17,25},{2,10},{10,18},{18,26},{... | collective-permute-start | bytes 294920 | tf_op jit(solution)/shard_map/ppermute | solution.py:990
  69.2 7.4 %collective-permute-start.3 = (bf16[3,2,64,128]{3,2,1,0:T(8,128)(2,1)S(1)}, bf16[3,2,64,128]{3,2,1,0:T(8,128)(2,1)S(1)}, u32[]{:S(2)}, u32[]{:S(2)}) collective-permute-start(bf16[3,2,64,128]{3,2,1,0:T(8,128)(2,1)S(1)} %get-tuple-element.27), channel_id=1, source_target_pairs={{8,0},{16,8},{24,16},{9,1},{17,9},{25,17},{10,2},{18,10},{26,18},{... | collective-permute-start | bytes 294920 | tf_op jit(solution)/shard_map/ppermute | solution.py:991
  72.2 4.4 %copy-start.8 = (bf16[3,2,64,128]{3,2,1,0:T(8,128)(2,1)}, bf16[3,2,64,128]{3,2,1,0:T(8,128)(2,1)S(1)}, u32[]{:S(2)}) copy-start(bf16[3,2,64,128]{3,2,1,0:T(8,128)(2,1)S(1)} %collective-permute-done.2.above_ref) | copy-start | bytes 294916
  76.6 0.6 copy-start.9
  90.1 0.7 copy-start.3

commit v2 on v1

--- a/solution.py
+++ b/solution.py
@@ -712,8 +712,59 @@
         chunks = place_charges(
             lambda s: stencil[s], tiled_shifts(shifts_ref, 0), tiled_shifts(shifts_ref, 1)
         )
+        to_next, to_previous, to_rows = pack_currents(
+            lambda q, t: current[q, :, LANES * t : LANES * (t + 1)]
+        )
+        mine = lax.axis_index("col")
+        blank = jnp.zeros((SUB, LANES), jnp.float32)
         for e in range(SUB):
-            out_ref[e] = jnp.concatenate(chunks[e], axis=0).astype(out_ref.dtype)
+            after = (mine == e - 1).astype(jnp.float32)
+            before = (mine == e + 1).astype(jnp.float32)
+            rows = chunks[e] + [to_next * after + to_previous * before, to_rows[e], blank]
+            out_ref[e] = jnp.concatenate(rows, axis=0).astype(out_ref.dtype)
+
+
+def pack_currents(tile):
+    half = BASIS // 2
+    lane = lane_index((half, LANES))
+    elem_col = lane & (EC - 1)
+    to_next = jnp.zeros((half, LANES), jnp.float32)
+    to_previous = jnp.zeros((half, LANES), jnp.float32)
+    for q in range(RHS):
+        for t in range(TILES):
+            value = tile(q, t)
+            for h in range(2):
+                place = q * TILES + t + SUB * h
+                part = value[half * h : half * (h + 1)]
+                here = elem_col == place
+                to_next = jnp.where(here, roll(part, place - (EC - 1), 1), to_next)
+                to_previous = jnp.where(here, roll(part, place, 1), to_previous)
+    lane = lane_index((SUB, LANES))
+    to_rows = []
+    for e in range(SUB):
+        rows = jnp.zeros((SUB, LANES), jnp.float32)
+        for q in range(RHS):
+            span = slice(SUB * e, SUB * (e + 1))
+            last = roll(tile(q, TILES - 1)[span], EC * q - (LANES - EC), 1)
+            first = roll(tile(q, 0)[span], 2 * EC + EC * q, 1)
+            rows = jnp.where(lane // EC == q, last, jnp.where(lane // EC == 2 + q, first, rows))
+        to_rows.append(rows)
+    return to_next, to_previous, to_rows
+
+
+def forward_rows(edge_row, j, count, which):
+    lane = lane_index((SUB, LANES))
+    start = 2 * EC * which
+    value = roll(edge_row(j), -start, 1)
+    for q in range(RHS):
+        place = 2 * EC + 2 * q
+        if j > 0:
+            corner = roll(edge_row(j - 1), place - start - EC * q - (EC - 1), 1)
+            value = jnp.where(lane == place, corner, value)
+        if j < count - 1:
+            corner = roll(edge_row(j + 1), place + 1 - start - EC * q, 1)
+            value = jnp.where(lane == place + 1, corner, value)
+    return jnp.where(lane < 64, roll(value, 2, 0), roll(roll(value, 64, 1), -2, 0))
 
 
 def column_sign(shape):
@@ -731,10 +782,24 @@
     both = dot(both, odd_cos[...])
     oc, os = both[: odd.shape[0]], both[odd.shape[0] :]
     half = out_ref.shape[1]
+    mine = lax.axis_index("row")
+    ends = [
+        [forward_rows(lambda k: part(k, GROUPS + 5), j, count, which) for which in range(2)]
+        for j in range(count)
+    ]
+    sub = sub_index((SUB, LANES))
+    middle = (sub >= 2) & (sub < 6)
     device = 0
     for block in (ec + oc, es - os, ec - oc, es + os):
         for t in range(0, block.shape[1], LANES):
             for chunk in halves(block[:half, t : t + LANES], block[half:, t : t + LANES]):
+                i, j = device // count, device % count
+                below = (mine == i - 1).astype(jnp.float32)
+                above = (mine == i + 1).astype(jnp.float32)
+                tail = jnp.where(
+                    middle, ends[j][0] * below + ends[j][1] * above, chunk[half - SUB :]
+                )
+                chunk = jnp.concatenate([chunk[: half - SUB], tail], axis=0)
                 out_ref[device] = chunk.astype(out_ref.dtype)
                 device += 1
 
@@ -851,71 +916,132 @@
             out_ref[q, :, LANES * t : LANES * (t + 1)] = totals[q * TILES + t]
 
 
-def near_kernel(own_ref, left_ref, right_ref, above_ref, below_ref, partners_ref, blocks_ref, out_ref, picked):
+def pick_kernel(currents_ref, slab_ref, arrived_ref, partners_ref, out_ref):
+    lane = lane_index((BASIS, LANES))
+    elem_col = lane & (EC - 1)
+    row, col = lax.axis_index("row"), lax.axis_index("col")
+    col_count = lax.axis_size("col")
+    devices = arrived_ref.shape[0]
+
+    def column_edge(source):
+        source = jnp.clip(source, 0, col_count - 1)
+        return slab_ref[source, 80:112, :].astype(jnp.float32)
+
+    from_left, from_right = column_edge(col - 1), column_edge(col + 1)
+
+    def beside(edge, q, t, end):
+        place = q * TILES + t
+        return jnp.concatenate([roll(edge, end - place, 1), roll(edge, end - place - SUB, 1)], axis=0)
+
+    def three(own, left, right):
+        return (
+            jnp.where(elem_col == 0, left, roll(own, 1, 1)),
+            own,
+            jnp.where(elem_col == EC - 1, right, roll(own, -1, 1)),
+        )
+
+    sub = sub_index((SUB, LANES))
+
+    def outer_row(source):
+        parts = []
+        for j in range(col_count):
+            index = jnp.clip(source * col_count + j, 0, devices - 1)
+            value = arrived_ref[index, 32:40, :].astype(jnp.float32)
+            parts.append(jnp.where(sub < 4, roll(value, -2, 0), roll(roll(value, 2, 0), -64, 1)))
+        return jnp.concatenate(parts, axis=0)
+
+    rows = outer_row(row - 1), outer_row(row + 1)
+
+    def outer_three(value, q, start):
+        own = roll(value, start - EC * q, 1)
+        left = roll(value, start - 2 * EC - 2 * q, 1)
+        right = roll(value, start + EC - 1 - 2 * EC - 2 * q - 1, 1)
+        return three(own, left, right)
+
+    for q in range(RHS):
+        tiles = []
+        for t in range(TILES):
+            own = currents_ref[q, :, LANES * t : LANES * (t + 1)]
+            own = own.astype(jnp.bfloat16).astype(jnp.float32)
+            tiles.append(three(own, beside(from_left, q, t, 0), beside(from_right, q, t, EC - 1)))
+        above = outer_three(rows[0], q, 0)
+        below = outer_three(rows[1], q, LANES - EC)
+        for t in range(TILES):
+            lanes = slice(LANES * t, LANES * (t + 1))
+            codes = [partners_ref[k : k + 1, lanes] for k in range(1, NEIGH)]
+            chosen = [tiles[t][1]] * (NEIGH - 1)
+            for c in range(3):
+                here = tiles[t][c]
+                before = roll(tiles[t - 1][c], EC, 1) if t else above[c]
+                after = roll(tiles[t + 1][c], -EC, 1) if t < TILES - 1 else below[c]
+                views = (
+                    jnp.where(lane < EC, before, roll(here, EC, 1)),
+                    here,
+                    jnp.where(lane >= LANES - EC, after, roll(here, -EC, 1)),
+                )
+                for r in range(3):
+                    if r == 1 and c == 1:
+                        continue
+                    for k in range(NEIGH - 1):
+                        chosen[k] = jnp.where(codes[k] == 3 * r + c, views[r], chosen[k])
+            for k in range(NEIGH - 1):
+                out_ref[k, q, :, lanes] = chosen[k].astype(out_ref.dtype)
+
+
+def near_kernel(has_total, *refs):
+    values_ref, refs = refs[0], refs[1:]
+    total_ref = None
+    if has_total:
+        total_ref, refs = refs[0], refs[1:]
+    blocks, out_ref, picked = refs[:-2], refs[-2], refs[-1]
+
     @pl.when(pl.program_id(0) == 0)
     def _():
-        lane = lane_index((BASIS, LANES))
-        elem_col = lane & (EC - 1)
-
-        def three(own, left, right):
-            own, left, right = (v.astype(jnp.float32) for v in (own, left, right))
-            return (
-                jnp.where(elem_col == 0, roll(left, 1 - EC, 1), roll(own, 1, 1)),
-                own,
-                jnp.where(elem_col == EC - 1, roll(right, EC - 1, 1), roll(own, -1, 1)),
-            )
-
-        for q in range(RHS):
-            tiles = [three(above_ref[0, q], above_ref[1, q], above_ref[2, q])]
-            for t in range(TILES):
-                lanes = slice(LANES * t, LANES * (t + 1))
-                tiles.append(three(own_ref[q, :, lanes], left_ref[q, :, lanes], right_ref[q, :, lanes]))
-            tiles.append(three(below_ref[0, q], below_ref[1, q], below_ref[2, q]))
-            for t in range(TILES):
-                lanes = slice(LANES * t, LANES * (t + 1))
-                before, here, after = tiles[t : t + 3]
-                codes = [partners_ref[k : k + 1, lanes] for k in range(NEIGH)]
-                chosen = [here[1]] * NEIGH
-                for c in range(3):
-                    views = (
-                        jnp.where(lane < EC, roll(before[c], EC, 1), roll(here[c], EC, 1)),
-                        here[c],
-                        jnp.where(lane >= LANES - EC, roll(after[c], -EC, 1), roll(here[c], -EC, 1)),
-                    )
-                    for r in range(3):
-                        if r == 1 and c == 1:
-                            continue
-                        for k in range(1, NEIGH):
-                            chosen[k] = jnp.where(codes[k] == 3 * r + c, views[r], chosen[k])
-                for k in range(NEIGH):
-                    picked[k, q, :, lanes] = chosen[k]
+        picked[...] = values_ref[...].astype(jnp.bfloat16).astype(jnp.float32).reshape(picked.shape)
 
     def one_tile(t, carry):
         lanes = pl.ds(pl.multiple_of(t * LANES, LANES), LANES)
         totals = [[None] * RHS for _ in range(SUB)]
-        for k in range(NEIGH):
+        for k, blocks_ref in enumerate(blocks):
             for b in range(0, BASIS, 16):
                 values = [
                     [picked[k, q, b + 8 * h : b + 8 * h + 8, lanes] for h in range(2)]
                     for q in range(RHS)
                 ]
                 for a in range(SUB):
-                    weight = blocks_ref[k, a, b : b + 16, lanes].astype(jnp.float32)
+                    weight = blocks_ref[0, a, b : b + 16, lanes].astype(jnp.float32)
                     for q in range(RHS):
                         term = weight[:8] * values[q][0] + weight[8:] * values[q][1]
                         totals[a][q] = term if totals[a][q] is None else totals[a][q] + term
         for q in range(RHS):
-            out_ref[q, :, lanes] = sum_rows([totals[a][q] for a in range(SUB)])
+            value = sum_rows([totals[a][q] for a in range(SUB)])
+            if has_total:
+                value = value + total_ref[q, :, lanes]
+            out_ref[q, :, lanes] = value
         return carry
 
     lax.fori_loop(0, TILES, one_tile, 0)
 
 
-def neighbours(value, axis):
-    count = lax.axis_size(axis)
-    forward = [(i, i + 1) for i in range(count - 1)]
-    backward = [(i + 1, i) for i in range(count - 1)]
-    return forward, backward
+def near_call(values, total, near_blocks, slots, start, stop):
+    elements = near_blocks.shape[3]
+    part = pl.BlockSpec((RHS, SUB, elements), lambda i: (0, i + start, 0))
+
+    def slot_spec(k):
+        return pl.BlockSpec((1, SUB, BASIS, elements), lambda i: (k, i + start, 0, 0))
+
+    return pl.pallas_call(
+        functools.partial(near_kernel, total is not None),
+        grid=(stop - start,),
+        in_specs=[whole(values.shape)]
+        + ([part] if total is not None else [])
+        + [slot_spec(k) for k in slots],
+        out_specs=part,
+        out_shape=jax.ShapeDtypeStruct((RHS, BASIS, elements), jnp.float32),
+        scratch_shapes=[pltpu.VMEM((len(slots), RHS, BASIS, elements), jnp.float32)],
+        input_output_aliases={} if total is None else {1: 0},
+        name="near",
+    )(*([values] if total is None else [values, total]), *([near_blocks] * len(slots)))
 
 
 def whole(shape):
@@ -941,8 +1067,8 @@
             pl.BlockSpec((STEN, BASIS, elements), lambda i: (i, 0, 0)),
             whole((2, elements)),
         ],
-        out_specs=whole((SUB, 80, LANES)),
-        out_shape=struct((SUB, 80, LANES), b16),
+        out_specs=whole((SUB, 128, LANES)),
+        out_shape=struct((SUB, 128, LANES), b16),
         scratch_shapes=[
             pltpu.VMEM((RHS, BASIS, elements), f32),
             pltpu.VMEM((STEN, SUB, SUB, LANES), f32),
@@ -967,45 +1093,31 @@
         out_shape=struct((devices, 40, LANES), b16),
         name="columns",
     )(slab, *col_tables)
+    spectrum, held = lax.optimization_barrier((spectrum, currents))
     arrived = lax.all_to_all(spectrum, ("row", "col"), 0, 0, tiled=True)
+    near = near_call(held, None, near_blocks, (0,), 0, BASIS // SUB)
+    arrived, near = lax.optimization_barrier((arrived, near))
     rows_back = pl.pallas_call(
         functools.partial(row_kernel, row_count, col_count),
         out_shape=struct((devices, 40, LANES), b16),
         name="rows",
     )(arrived, *row_tables)
+    rows_back, ready = lax.optimization_barrier((rows_back, arrived))
     returned = lax.all_to_all(rows_back, ("row", "col"), 0, 0, tiled=True)
+    picked = pl.pallas_call(
+        pick_kernel, out_shape=struct((NEIGH - 1, RHS, BASIS, elements), b16), name="pick"
+    )(held, slab, ready, partners)
+    others = tuple(range(1, NEIGH))
+    near = near_call(picked, near, near_blocks, others, 0, BASIS // SUB // 2)
+    returned, near, picked = lax.optimization_barrier((returned, near, picked))
     potential = pl.pallas_call(
         functools.partial(grid_kernel, col_count),
         out_shape=struct((SUB, 80, LANES), b16),
         name="grid",
     )(returned, *col_tables)
+    potential, near, picked = lax.optimization_barrier((potential, near, picked))
     pieces = lax.all_to_all(potential, "col", 0, 0, tiled=True)
-
-    half = currents.astype(b16)
-    forward, backward = neighbours(half, "col")
-    left = lax.ppermute(half, "col", forward)
-    right = lax.ppermute(half, "col", backward)
-    three = jnp.stack([half, left, right])
-    forward, backward = neighbours(half, "row")
-    above = lax.ppermute(three[..., elements - LANES :], "row", forward)
-    below = lax.ppermute(three[..., :LANES], "row", backward)
-    near = pl.pallas_call(
-        near_kernel,
-        grid=(BASIS // SUB,),
-        in_specs=[
-            whole((RHS, BASIS, elements)),
-            whole((RHS, BASIS, elements)),
-            whole((RHS, BASIS, elements)),
-            whole((3, RHS, BASIS, LANES)),
-            whole((3, RHS, BASIS, LANES)),
-            whole((NEIGH, elements)),
-            pl.BlockSpec((NEIGH, SUB, BASIS, elements), lambda i: (0, i, 0, 0)),
-        ],
-        out_specs=pl.BlockSpec((RHS, SUB, elements), lambda i: (0, i, 0)),
-        out_shape=struct((RHS, BASIS, elements), f32),
-        scratch_shapes=[pltpu.VMEM((NEIGH, RHS, BASIS, elements), f32)],
-        name="near",
-    )(half, left, right, above, below, partners, near_blocks)
+    near = near_call(picked, near, near_blocks, others, BASIS // SUB // 2, BASIS // SUB)
 
     depth = 16
     return pl.pallas_call(

time: 97.6 us -> 88.1 us (0.903)
  waiting for transfers between devices: 25.5 us -> 11.8 us
  Pallas kernels: 43.9 us -> 53.9 us
  starting transfers between devices: 22.6 us -> 18.6 us
  other arithmetic: 1.03 us -> 0 us
    pallas_call x1 -> x4, Pallas kernels: 12.8 us -> 21.4 us  [the longest x3 18.6 us: near_call(): pl.pallas_call(functools.partial(near_kernel, total is not None), grid=(s...]
    all_to_all x1, waiting for transfers between devices: 7.3 us -> 0.54 us  [shards_real(): arrived = lax.all_to_all(spectrum, ('row', 'col'), 0, 0, tiled=True)]
    ppermute x4 -> x0, starting transfers between devices: 6.29 us -> none  [the longest x1 2.02 us: shards_real(): left = lax.ppermute(half, 'col', forward)]
    ppermute x4 -> x0, waiting for transfers between devices: 6.14 us -> none  [the longest x1 4.43 us: shards_real(): below = lax.ppermute(three[..., :LANES], 'row', backward)]
    all_to_all x1, waiting for transfers between devices: 7.71 us -> 3.29 us  [shards_real(): returned = lax.all_to_all(rows_back, ('row', 'col'), 0, 0, tiled=True)]
    all_to_all x1, starting transfers between devices: 2.59 us -> 5.3 us  [shards_real(): returned = lax.all_to_all(rows_back, ('row', 'col'), 0, 0, tiled=True)]
    all_to_all x1, waiting for transfers between devices: 4.3 us -> 6.82 us  [shards_real(): slab = lax.all_to_all(charges, 'col', 0, 0, tiled=True)]
    all_to_all x1, waiting for transfers between devices: 0.01 us -> 1.15 us  [shards_real(): pieces = lax.all_to_all(potential, 'col', 0, 0, tiled=True)]
  transfers between devices with their start and end apart: 8 -> 4, of which waited for: 5 -> 4; matrix products, arithmetic and copies ran while one was open for 1% -> 0% of each run, Pallas kernels for 24% -> 33%
where the time goes in v2:
time: 88.1 us; the launch traced here: 87.1 us
  Pallas kernels  53.9 us (61%)
  starting transfers between devices  18.6 us (21%)
  waiting for transfers between devices  11.8 us (13%)
  local copies, waits for them, and re-layouts  2.83 us (3%)
    pallas_call x3, Pallas kernels, near_call(): pl.pallas_call(functools.partial(near_kernel, total is not None), grid=(s...  18.6 us
    pallas_call x1, Pallas kernels, shards_real(): pl.pallas_call(charge_kernel, grid=(STEN,), in_specs=[whole((RHS, BASIS,...  7.89 us
    all_to_all x1, waiting for transfers between devices, shards_real(): slab = lax.all_to_all(charges, 'col', 0, 0, tiled=True)  6.82 us
    all_to_all x1, starting transfers between devices, shards_real(): slab = lax.all_to_all(charges, 'col', 0, 0, tiled=True)  6.35 us
    pallas_call x1, Pallas kernels, shards_real(): pl.pallas_call(far_kernel, grid=(BASIS // depth,), in_specs=[whole((SUB,...  5.84 us
    all_to_all x1, starting transfers between devices, shards_real(): returned = lax.all_to_all(rows_back, ('row', 'col'), 0, 0, tiled=True)  5.3 us
    pallas_call x1, Pallas kernels, shards_real(): pl.pallas_call(row_table_kernel, out_shape=[table] * 6 + [spread] * 2, na...  4.76 us
    pallas_call x1, Pallas kernels, shards_real(): pl.pallas_call(functools.partial(row_kernel, row_count, col_count), out_s...  4.21 us
  transfers between devices with their start and end apart: 4, of which 4 were waited for; matrix products, arithmetic and copies ran while one was open for 0% of the time, Pallas kernels for 33%

profile of v2, /device:TPU:0, one launch (start us, length us, event | category | flops | bytes accessed | tf_op | source)
XLA Modules:
  0.0 87.1 jit_solution(16906586133686077693)
XLA Ops:
  0.0 7.9 %charges.1 = bf16[8,128,128]{2,1,0:T(8,128)(2,1)} custom-call(f32[2,64,512]{2,1,0:T(8,128)} %currents_ref.2, bf16[64,64,512]{2,1,0:T(8,128)(2,1)} %projection_ref.3, s32[2,512]{1,0:T(2,128)} %shifts_ref.3), custom_call_target="tpu_custom_call" | custom-call | tf_op jit(solution)/shard_map/charges/pallas_call | solution.py:1062
  7.9 6.4 %all-to-all-start = ((bf16[8,128,128]{2,1,0:T(8,128)(2,1)}), bf16[8,128,128]{2,1,0:T(8,128)(2,1)S(1)}, u32[]{:S(2)}, u32[]{:S(2)}) async-start(bf16[8,128,128]{2,1,0:T(8,128)(2,1)} %charges.1), calls=%async_computation | async-start | bytes 524288 | tf_op jit(solution)/shard_map/all_to_all | solution.py:1079
  14.2 2.9 %column_tables.1 = (bf16[512,512]{1,0:T(8,128)(2,1)}, bf16[512,512]{1,0:T(8,128)(2,1)}, bf16[512,512]{1,0:T(8,128)(2,1)}) custom-call(f32[64,512]{1,0:T(8,128)} %constant.40.clone.refs_0_, f32[64,512]{1,0:T(8,128)} %constant.41.clone.refs_1_, f32[8,512]{1,0:T(8,128)} %constant.42.clone.refs_2_, f32[8,512]{1,0:T(8,128)} %constant.43.clone.refs_3_, ...), custom_call_target="tpu_custom_call" | custom-call | tf_op jit(solution)/shard_map/column_tables/pallas_call | solution.py:1083
  17.1 6.8 %all-to-all-done.rows_ref.slab_ref = bf16[8,128,128]{2,1,0:T(8,128)(2,1)S(1)} async-done(((bf16[8,128,128]{2,1,0:T(8,128)(2,1)}), bf16[8,128,128]{2,1,0:T(8,128)(2,1)S(1)}, u32[]{:S(2)}, u32[]{:S(2)}) %all-to-all-start) | async-done | bytes 262176 | tf_op jit(solution)/shard_map/all_to_all | solution.py:1079
  24.0 0.0 copy-start.1
  24.0 0.7 copy-done.1
  24.7 3.8 %columns.1 = bf16[32,40,128]{2,1,0:T(8,128)(2,1)} custom-call(bf16[8,128,128]{2,1,0:T(8,128)(2,1)} %copy-done.1, bf16[512,512]{1,0:T(8,128)(2,1)} %get-tuple-element.28.even_cos, bf16[512,512]{1,0:T(8,128)(2,1)} %get-tuple-element.29.even_sin, bf16[512,512]{1,0:T(8,128)(2,1)} %get-tuple-element.30.odd_cos), custom_call_target="tpu_custom_call" | custom-call | tf_op jit(solution)/shard_map/columns/pallas_call | solution.py:1091
  28.4 3.5 %all-to-all-start.1 = ((bf16[32,40,128]{2,1,0:T(8,128)(2,1)}), bf16[32,40,128]{2,1,0:T(8,128)(2,1)S(1)}, u32[]{:S(2)}, u32[]{:S(2)}) async-start(bf16[32,40,128]{2,1,0:T(8,128)(2,1)} %columns.1), calls=%async_computation.1 | async-start | bytes 655360 | tf_op jit(solution)/shard_map/all_to_all | solution.py:1097
  32.0 4.8 %row_tables.1 = (bf16[512,512]{1,0:T(8,128)(2,1)}, bf16[512,512]{1,0:T(8,128)(2,1)}, bf16[512,512]{1,0:T(8,128)(2,1)}, bf16[512,512]{1,0:T(8,128)(2,1)}, bf16[51...) custom-call(f32[64,2048]{1,0:T(8,128)} %green_ref.1, ...), custom_call_target="tpu_custom_call" | custom-call | tf_op jit(solution)/shard_map/row_tables/pallas_call | solution.py:1087
  36.7 6.7 %near.3.refs_1_ = f32[2,64,512]{2,1,0:T(8,128)} custom-call(f32[2,64,512]{2,1,0:T(8,128)} %currents_ref.2, bf16[4,64,64,512]{3,2,1,0:T(8,128)(2,1)} %refs_4_.5), custom_call_target="tpu_custom_call" | custom-call | tf_op jit(solution)/shard_map/near/pallas_call | solution.py:1033
  43.5 0.5 all-to-all-done.1.in_ref.arrived_ref
  44.0 0.0 copy-start
  44.0 0.7 copy-done
  44.7 4.2 %rows.1 = bf16[32,40,128]{2,1,0:T(8,128)(2,1)} custom-call(bf16[32,40,128]{2,1,0:T(8,128)(2,1)} %copy-done, bf16[512,512]{1,0:T(8,128)(2,1)} %get-tuple-element.34.even_cos, bf16[512,512]{1,0:T(8,128)(2,1)} %get-tuple-element.35.even_sin, bf16[512,512]{1,0:T(8,128)(2,1)} %get-tuple-element.36.odd_cos, bf16[512,512]{1,0:T(8,128)(2,1)} %get-tuple-element.37.back_cos, ...), custom_call_target="tpu_custom_call" | custom-call | tf_op jit(solution)/shard_map/rows/pallas_call | solution.py:1100
  48.9 5.3 %all-to-all-start.2 = ((bf16[32,40,128]{2,1,0:T(8,128)(2,1)}), bf16[32,40,128]{2,1,0:T(8,128)(2,1)S(1)}, u32[]{:S(2)}, u32[]{:S(2)}) async-start(bf16[32,40,128]{2,1,0:T(8,128)(2,1)} %rows.1), calls=%async_computation.2 | async-start | bytes 655360 | tf_op jit(solution)/shard_map/all_to_all | solution.py:1106
  54.2 2.8 %pick.1.refs_0_ = bf16[3,2,64,512]{3,2,1,0:T(8,128)(2,1)} custom-call(f32[2,64,512]{2,1,0:T(8,128)} %currents_ref.2, bf16[8,128,128]{2,1,0:T(8,128)(2,1)} %copy-done.1, bf16[32,40,128]{2,1,0:T(8,128)(2,1)} %copy-done, s32[4,512]{1,0:T(4,128)} %partners_ref.1), custom_call_target="tpu_custom_call" | custom-call | tf_op jit(solution)/shard_map/pick/pallas_call | solution.py:1107
  57.0 5.9 %near.4.refs_1_ = f32[2,64,512]{2,1,0:T(8,128)} custom-call(bf16[3,2,64,512]{3,2,1,0:T(8,128)(2,1)} %pick.1.refs_0_, f32[2,64,512]{2,1,0:T(8,128)} %near.3.refs_1_, bf16[4,64,64,512]{3,2,1,0:T(8,128)(2,1)} %refs_4_.5, bf16[4,64,64,512]{3,2,1,0:T(8,128)(2,1)} %refs_4_.5, bf16[4,64,64,512]{3,2,1,0:T(8,128)(2,1)} %refs_4_.5), custom_call_target="tpu_custom_call", output_to_operand_aliasing={{}: (1, {})} | custom-call | tf_op jit(solution)/shard_map/near/pallas_call | solution.py:1033
  63.0 3.3 %all-to-all-done.2.in_ref = bf16[32,40,128]{2,1,0:T(8,128)(2,1)S(1)} async-done(((bf16[32,40,128]{2,1,0:T(8,128)(2,1)}), bf16[32,40,128]{2,1,0:T(8,128)(2,1)S(1)}, u32[]{:S(2)}, u32[]{:S(2)}) %all-to-all-start.2) | async-done | bytes 327712 | tf_op jit(solution)/shard_map/all_to_all | solution.py:1106
  66.3 0.0 copy-start.2
  66.3 0.7 copy-done.2
  67.0 3.1 %grid.1 = bf16[8,80,128]{2,1,0:T(8,128)(2,1)} custom-call(bf16[32,40,128]{2,1,0:T(8,128)(2,1)} %copy-done.2, bf16[512,512]{1,0:T(8,128)(2,1)} %get-tuple-element.28.even_cos, bf16[512,512]{1,0:T(8,128)(2,1)} %get-tuple-element.29.even_sin, bf16[512,512]{1,0:T(8,128)(2,1)} %get-tuple-element.30.odd_cos), custom_call_target="tpu_custom_call" | custom-call | tf_op jit(solution)/shard_map/grid/pallas_call | solution.py:1113
  70.1 3.4 %all-to-all-start.3 = ((bf16[8,80,128]{2,1,0:T(8,128)(2,1)}), bf16[8,80,128]{2,1,0:T(8,128)(2,1)S(1)}, u32[]{:S(2)}, u32[]{:S(2)}) async-start(bf16[8,80,128]{2,1,0:T(8,128)(2,1)} %grid.1), calls=%async_computation.3 | async-start | bytes 327680 | tf_op jit(solution)/shard_map/all_to_all | solution.py:1119
  73.5 6.0 %near.5.near_ref = f32[2,64,512]{2,1,0:T(8,128)} custom-call(bf16[3,2,64,512]{3,2,1,0:T(8,128)(2,1)} %pick.1.refs_0_, f32[2,64,512]{2,1,0:T(8,128)} %near.4.refs_1_, bf16[4,64,64,512]{3,2,1,0:T(8,128)(2,1)} %refs_4_.5, bf16[4,64,64,512]{3,2,1,0:T(8,128)(2,1)} %refs_4_.5, bf16[4,64,64,512]{3,2,1,0:T(8,128)(2,1)} %refs_4_.5), custom_call_target="tpu_custom_call", output_to_operand_aliasing={{}: (1, {})} | custom-call | tf_op jit(solution)/shard_map/near/pallas_call | solution.py:1033
  79.4 1.2 %all-to-all-done.3.grid_ref = bf16[8,80,128]{2,1,0:T(8,128)(2,1)S(1)} async-done(((bf16[8,80,128]{2,1,0:T(8,128)(2,1)}), bf16[8,80,128]{2,1,0:T(8,128)(2,1)S(1)}, u32[]{:S(2)}, u32[]{:S(2)}) %all-to-all-start.3) | async-done | bytes 163872 | tf_op jit(solution)/shard_map/all_to_all | solution.py:1119
  80.6 0.0 copy-start.3
  80.6 0.7 copy-done.3
  81.2 5.8 %far.1 = f32[2,64,512]{2,1,0:T(8,128)} custom-call(bf16[8,80,128]{2,1,0:T(8,128)(2,1)} %copy-done.3, bf16[64,64,512]{2,1,0:T(8,128)(2,1)} %projection_ref.3, s32[2,512]{1,0:T(2,128)} %shifts_ref.3, f32[2,64,512]{2,1,0:T(8,128)} %near.5.near_ref), custom_call_target="tpu_custom_call" | custom-call | tf_op jit(solution)/shard_map/far/pallas_call | solution.py:1123
Async XLA Ops:
  7.9 16.1 %all-to-all-start = ((bf16[8,128,128]{2,1,0:T(8,128)(2,1)}), bf16[8,128,128]{2,1,0:T(8,128)(2,1)S(1)}, u32[]{:S(2)}, u32[]{:S(2)}) async-start(bf16[8,128,128]{2,1,0:T(8,128)(2,1)} %charges.1), calls=%async_computation | async-start | bytes 524288 | tf_op jit(solution)/shard_map/all_to_all | solution.py:1079
  24.0 0.7 copy-start.1
  28.4 15.6 %all-to-all-start.1 = ((bf16[32,40,128]{2,1,0:T(8,128)(2,1)}), bf16[32,40,128]{2,1,0:T(8,128)(2,1)S(1)}, u32[]{:S(2)}, u32[]{:S(2)}) async-start(bf16[32,40,128]{2,1,0:T(8,128)(2,1)} %columns.1), calls=%async_computation.1 | async-start | bytes 655360 | tf_op jit(solution)/shard_map/all_to_all | solution.py:1097
  44.0 0.7 copy-start
  48.9 17.3 %all-to-all-start.2 = ((bf16[32,40,128]{2,1,0:T(8,128)(2,1)}), bf16[32,40,128]{2,1,0:T(8,128)(2,1)S(1)}, u32[]{:S(2)}, u32[]{:S(2)}) async-start(bf16[32,40,128]{2,1,0:T(8,128)(2,1)} %rows.1), calls=%async_computation.2 | async-start | bytes 655360 | tf_op jit(solution)/shard_map/all_to_all | solution.py:1106
  66.3 0.7 copy-start.2
  70.1 10.5 %all-to-all-start.3 = ((bf16[8,80,128]{2,1,0:T(8,128)(2,1)}), bf16[8,80,128]{2,1,0:T(8,128)(2,1)S(1)}, u32[]{:S(2)}, u32[]{:S(2)}) async-start(bf16[8,80,128]{2,1,0:T(8,128)(2,1)} %grid.1), calls=%async_computation.3 | async-start | bytes 327680 | tf_op jit(solution)/shard_map/all_to_all | solution.py:1119
  80.6 0.7 copy-start.3

commit v3 on v2

--- a/solution.py
+++ b/solution.py
@@ -682,46 +682,64 @@
     return jnp.concatenate(rows * RHS, axis=0)
 
 
-def charge_kernel(currents_ref, projection_ref, shifts_ref, out_ref, current, partial, stencil):
-    step = pl.program_id(0)
-
-    @pl.when(step == 0)
-    def _():
-        current[...] = currents_ref[...].astype(jnp.bfloat16).astype(jnp.float32)
-
-    for t in range(TILES):
-        lanes = slice(LANES * t, LANES * (t + 1))
-        totals = [[None] * RHS for _ in range(STEN)]
-        for b in range(0, BASIS, 16):
-            values = [
-                [current[q, b + 8 * h : b + 8 * h + 8, lanes] for h in range(2)] for q in range(RHS)
-            ]
+def charge_kernel(
+    currents_ref, projection_ref, shifts_ref, out_ref, weights, raw, shifts, current, partial, stencil, sems
+):
+    copies = [
+        pltpu.make_async_copy(currents_ref, raw, sems.at[STEN]),
+        pltpu.make_async_copy(shifts_ref, shifts, sems.at[STEN + 1]),
+    ]
+
+    def weight_copy(step):
+        rows = pl.ds(step * STEN, STEN)
+        return pltpu.make_async_copy(projection_ref.at[rows], weights.at[rows], sems.at[step])
+
+    copies[0].start()
+    for step in range(STEN):
+        weight_copy(step).start()
+    copies[1].start()
+    copies[0].wait()
+    current[...] = raw[...].astype(jnp.bfloat16).astype(jnp.float32)
+
+    def one_row(step, carry):
+        weight_copy(step).wait()
+        for t in range(TILES):
+            lanes = slice(LANES * t, LANES * (t + 1))
+            totals = [[None] * RHS for _ in range(STEN)]
+            for b in range(0, BASIS, 16):
+                values = [
+                    [current[q, b + 8 * h : b + 8 * h + 8, lanes] for h in range(2)]
+                    for q in range(RHS)
+                ]
+                for s in range(STEN):
+                    weight = weights[step * STEN + s, b : b + 16, lanes].astype(jnp.float32)
+                    for q in range(RHS):
+                        term = weight[:8] * values[q][0] + weight[8:] * values[q][1]
+                        totals[s][q] = term if totals[s][q] is None else totals[s][q] + term
             for s in range(STEN):
-                weight = projection_ref[s, b : b + 16, lanes].astype(jnp.float32)
                 for q in range(RHS):
-                    term = weight[:8] * values[q][0] + weight[8:] * values[q][1]
-                    totals[s][q] = term if totals[s][q] is None else totals[s][q] + term
+                    partial[s, q * TILES + t] = totals[s][q]
         for s in range(STEN):
-            for q in range(RHS):
-                partial[s, q * TILES + t] = totals[s][q]
-    for s in range(STEN):
-        stencil[step * STEN + s] = sum_rows([partial[s, i] for i in range(SUB)])
-
-    @pl.when(step == pl.num_programs(0) - 1)
-    def _():
-        chunks = place_charges(
-            lambda s: stencil[s], tiled_shifts(shifts_ref, 0), tiled_shifts(shifts_ref, 1)
-        )
-        to_next, to_previous, to_rows = pack_currents(
-            lambda q, t: current[q, :, LANES * t : LANES * (t + 1)]
-        )
-        mine = lax.axis_index("col")
-        blank = jnp.zeros((SUB, LANES), jnp.float32)
-        for e in range(SUB):
-            after = (mine == e - 1).astype(jnp.float32)
-            before = (mine == e + 1).astype(jnp.float32)
-            rows = chunks[e] + [to_next * after + to_previous * before, to_rows[e], blank]
-            out_ref[e] = jnp.concatenate(rows, axis=0).astype(out_ref.dtype)
+            stencil[step * STEN + s] = sum_rows([partial[s, i] for i in range(SUB)])
+        return carry
+
+    lax.fori_loop(0, STEN, one_row, 0)
+    copies[1].wait()
+    chunks = place_charges(
+        lambda s: stencil[s], tiled_shifts(shifts, 0), tiled_shifts(shifts, 1)
+    )
+    to_next, to_previous, to_rows = pack_currents(
+        lambda q, t: current[q, :, LANES * t : LANES * (t + 1)]
+    )
+    mine = lax.axis_index("col")
+    block = lane_index((SUB, LANES)) // EC
+    middle = ((block & 3) == 1) | ((block & 3) == 2)
+    for e in range(SUB):
+        after = (mine == e - 1).astype(jnp.float32)
+        before = (mine == e + 1).astype(jnp.float32)
+        edge = jnp.where(middle, to_rows[e], chunks[e][GROUPS])
+        rows = chunks[e][:GROUPS] + [edge, to_next * after + to_previous * before]
+        out_ref[e] = jnp.concatenate(rows, axis=0).astype(out_ref.dtype)
 
 
 def pack_currents(tile):
@@ -745,16 +763,16 @@
         rows = jnp.zeros((SUB, LANES), jnp.float32)
         for q in range(RHS):
             span = slice(SUB * e, SUB * (e + 1))
-            last = roll(tile(q, TILES - 1)[span], EC * q - (LANES - EC), 1)
-            first = roll(tile(q, 0)[span], 2 * EC + EC * q, 1)
-            rows = jnp.where(lane // EC == q, last, jnp.where(lane // EC == 2 + q, first, rows))
+            last = roll(tile(q, TILES - 1)[span], EC + EC * q - (LANES - EC), 1)
+            first = roll(tile(q, 0)[span], 64 + EC + EC * q, 1)
+            rows = jnp.where(lane // EC == 1 + q, last, jnp.where(lane // EC == 5 + q, first, rows))
         to_rows.append(rows)
     return to_next, to_previous, to_rows
 
 
 def forward_rows(edge_row, j, count, which):
     lane = lane_index((SUB, LANES))
-    start = 2 * EC * which
+    start = EC + 64 * which
     value = roll(edge_row(j), -start, 1)
     for q in range(RHS):
         place = 2 * EC + 2 * q
@@ -784,7 +802,7 @@
     half = out_ref.shape[1]
     mine = lax.axis_index("row")
     ends = [
-        [forward_rows(lambda k: part(k, GROUPS + 5), j, count, which) for which in range(2)]
+        [forward_rows(lambda k: part(k, GROUPS), j, count, which) for which in range(2)]
         for j in range(count)
     ]
     sub = sub_index((SUB, LANES))
@@ -804,18 +822,29 @@
                 device += 1
 
 
-def row_kernel(row_count, col_count, in_ref, even_cos, even_sin, odd_cos, back_cos, back_sin, back_odd,
-               sum_ref, diff_ref, out_ref):
+def row_kernel(row_count, col_count, in_ref, *refs):
+    sources, out_ref, held, sems = refs[:8], refs[8], refs[9:17], refs[17]
+    loads = [
+        pltpu.make_async_copy(source, target, sems.at[n])
+        for n, (source, target) in enumerate(zip(sources, held))
+    ]
+    for load in loads:
+        load.start()
+    even_cos, even_sin, odd_cos, back_cos, back_sin, back_odd, sum_ref, diff_ref = held
     even, odd = add_outer_rows(
         lambda i, j: in_ref[i * col_count + j].astype(jnp.float32), row_count, col_count
     )
     flip = jnp.where((sub_index(odd.shape) & 4) == 0, 1.0, -1.0)
     both = jnp.concatenate([odd, odd * flip], axis=1).astype(jnp.bfloat16)
     even = even.astype(jnp.bfloat16)
+    for n in range(3):
+        loads[n].wait()
     a = [dot(even_cos[...], even), dot(even_sin[...], even)]
     both = dot(odd_cos[...], both)
     b = [both[:, :LANES], both[:, LANES:]]
     quarter = odd.shape[0]
+    for n in range(3, 8):
+        loads[n].wait()
 
     def pieces(left, right):
         for k in range(2):
@@ -877,43 +906,60 @@
     scatter_rows(even, odd, count, put)
 
 
-def far_kernel(grid_ref, projection_ref, shifts_ref, near_ref, out_ref, samples):
-    @pl.when(pl.program_id(0) == 0)
-    def _():
-        def part(e, r):
-            return grid_ref[e, 8 * r : 8 * r + 8, :].astype(jnp.float32)
-
-        def put(s, value):
-            samples[s] = value
-
-        read_samples(
-            part,
-            lambda e: part(e, GROUPS),
-            tiled_shifts(shifts_ref, 0),
-            tiled_shifts(shifts_ref, 1),
-            put,
+def far_kernel(grid_ref, projection_ref, shifts_ref, near_ref, out_ref, weights, samples, shifts, totals_ref, sems):
+    depth = 16
+    count = BASIS // depth
+
+    def load(i):
+        rows = pl.ds(i * depth, depth)
+        return pltpu.make_async_copy(
+            projection_ref.at[:, rows], weights.at[:, rows], sems.at[1 + count + i]
         )
 
-    depth = out_ref.shape[1]
-
-    def add_row(a, totals):
-        totals = list(totals)
-        for b in range(STEN):
-            s = a * STEN + b
+    load_shifts = pltpu.make_async_copy(shifts_ref, shifts, sems.at[0])
+    load_shifts.start()
+    for i in range(count):
+        load(i).start()
+
+    def part(e, r):
+        return grid_ref[e, 8 * r : 8 * r + 8, :].astype(jnp.float32)
+
+    def put(s, value):
+        samples[s] = value
+
+    load_shifts.wait()
+    read_samples(
+        part, lambda e: part(e, GROUPS), tiled_shifts(shifts, 0), tiled_shifts(shifts, 1), put
+    )
+    def store(i):
+        rows = pl.ds(i * depth, depth)
+        return pltpu.make_async_copy(totals_ref.at[:, rows], out_ref.at[:, rows], sems.at[1 + i])
+
+    for i in range(count):
+        span = slice(i * depth, (i + 1) * depth)
+        load(i).wait()
+
+        def add_row(a, totals):
+            totals = list(totals)
+            for b in range(STEN):
+                s = a * STEN + b
+                for t in range(TILES):
+                    weight = weights[s, span, LANES * t : LANES * (t + 1)].astype(jnp.float32)
+                    for q in range(RHS):
+                        index = q * TILES + t
+                        totals[index] = totals[index] + weight * samples[s, index : index + 1, :]
+            return tuple(totals)
+
+        start = tuple(
+            near_ref[q, span, LANES * t : LANES * (t + 1)] for q in range(RHS) for t in range(TILES)
+        )
+        totals = lax.fori_loop(0, STEN, add_row, start)
+        for q in range(RHS):
             for t in range(TILES):
-                weight = projection_ref[s, :, LANES * t : LANES * (t + 1)].astype(jnp.float32)
-                for q in range(RHS):
-                    index = q * TILES + t
-                    totals[index] = totals[index] + weight * samples[s, index : index + 1, :]
-        return tuple(totals)
-
-    start = tuple(
-        near_ref[q, :, LANES * t : LANES * (t + 1)] for q in range(RHS) for t in range(TILES)
-    )
-    totals = lax.fori_loop(0, STEN, add_row, start)
-    for q in range(RHS):
-        for t in range(TILES):
-            out_ref[q, :, LANES * t : LANES * (t + 1)] = totals[q * TILES + t]
+                totals_ref[q, span, LANES * t : LANES * (t + 1)] = totals[q * TILES + t]
+        store(i).start()
+    for i in range(count):
+        store(i).wait()
 
 
 def pick_kernel(currents_ref, slab_ref, arrived_ref, partners_ref, out_ref):
@@ -988,60 +1034,79 @@
                 out_ref[k, q, :, lanes] = chosen[k].astype(out_ref.dtype)
 
 
-def near_kernel(has_total, *refs):
+def near_kernel(has_total, slots, start, stop, *refs):
     values_ref, refs = refs[0], refs[1:]
     total_ref = None
     if has_total:
         total_ref, refs = refs[0], refs[1:]
-    blocks, out_ref, picked = refs[:-2], refs[-2], refs[-1]
-
-    @pl.when(pl.program_id(0) == 0)
-    def _():
-        picked[...] = values_ref[...].astype(jnp.bfloat16).astype(jnp.float32).reshape(picked.shape)
-
-    def one_tile(t, carry):
-        lanes = pl.ds(pl.multiple_of(t * LANES, LANES), LANES)
-        totals = [[None] * RHS for _ in range(SUB)]
-        for k, blocks_ref in enumerate(blocks):
-            for b in range(0, BASIS, 16):
-                values = [
-                    [picked[k, q, b + 8 * h : b + 8 * h + 8, lanes] for h in range(2)]
-                    for q in range(RHS)
-                ]
-                for a in range(SUB):
-                    weight = blocks_ref[0, a, b : b + 16, lanes].astype(jnp.float32)
-                    for q in range(RHS):
-                        term = weight[:8] * values[q][0] + weight[8:] * values[q][1]
-                        totals[a][q] = term if totals[a][q] is None else totals[a][q] + term
-        for q in range(RHS):
-            value = sum_rows([totals[a][q] for a in range(SUB)])
-            if has_total:
-                value = value + total_ref[q, :, lanes]
-            out_ref[q, :, lanes] = value
+    blocks_ref, out_ref, blocks, picked, sems = refs
+    chunks = (stop - start) // SUB
+
+    def load(chunk, k):
+        rows = pl.ds(start + chunk * SUB, SUB)
+        return pltpu.make_async_copy(
+            blocks_ref.at[slots[k], rows], blocks.at[chunk, k], sems.at[chunk, k]
+        )
+
+    for chunk in range(chunks):
+        for k in range(len(slots)):
+            load(chunk, k).start()
+    picked[...] = values_ref[...].astype(jnp.bfloat16).astype(jnp.float32).reshape(picked.shape)
+    if has_total:
+        out_ref[...] = total_ref[...]
+
+    def one_chunk(chunk, carry):
+        for k in range(len(slots)):
+            load(chunk, k).wait()
+        rows = pl.ds(pl.multiple_of(start + chunk * SUB, SUB), SUB)
+        for t in range(TILES):
+            lanes = slice(t * LANES, (t + 1) * LANES)
+            totals = [[None] * RHS for _ in range(SUB)]
+            for k in range(len(slots)):
+                for b in range(0, BASIS, 16):
+                    values = [
+                        [picked[k, q, b + 8 * h : b + 8 * h + 8, lanes] for h in range(2)]
+                        for q in range(RHS)
+                    ]
+                    for a in range(SUB):
+                        weight = blocks[chunk, k, a, b : b + 16, lanes].astype(jnp.float32)
+                        for q in range(RHS):
+                            term = weight[:8] * values[q][0] + weight[8:] * values[q][1]
+                            totals[a][q] = term if totals[a][q] is None else totals[a][q] + term
+            for q in range(RHS):
+                value = sum_rows([totals[a][q] for a in range(SUB)])
+                if has_total:
+                    value = value + total_ref[q, rows, lanes]
+                out_ref[q, rows, lanes] = value
         return carry
 
-    lax.fori_loop(0, TILES, one_tile, 0)
+    lax.fori_loop(0, chunks, one_chunk, 0)
 
 
 def near_call(values, total, near_blocks, slots, start, stop):
     elements = near_blocks.shape[3]
-    part = pl.BlockSpec((RHS, SUB, elements), lambda i: (0, i + start, 0))
-
-    def slot_spec(k):
-        return pl.BlockSpec((1, SUB, BASIS, elements), lambda i: (k, i + start, 0, 0))
-
+    chunks = (stop - start) // SUB
     return pl.pallas_call(
-        functools.partial(near_kernel, total is not None),
-        grid=(stop - start,),
-        in_specs=[whole(values.shape)]
-        + ([part] if total is not None else [])
-        + [slot_spec(k) for k in slots],
-        out_specs=part,
+        functools.partial(near_kernel, total is not None, slots, start, stop),
+        in_specs=[ON_CHIP] * (1 if total is None else 2) + [IN_PLACE],
+        out_specs=ON_CHIP,
         out_shape=jax.ShapeDtypeStruct((RHS, BASIS, elements), jnp.float32),
-        scratch_shapes=[pltpu.VMEM((len(slots), RHS, BASIS, elements), jnp.float32)],
-        input_output_aliases={} if total is None else {1: 0},
+        scratch_shapes=[
+            pltpu.VMEM((chunks, len(slots), SUB, BASIS, elements), jnp.bfloat16),
+            pltpu.VMEM((len(slots), RHS, BASIS, elements), jnp.float32),
+            pltpu.SemaphoreType.DMA((chunks, len(slots))),
+        ],
+        compiler_params=NEAR_PARAMS,
         name="near",
-    )(*([values] if total is None else [values, total]), *([near_blocks] * len(slots)))
+    )(*([values] if total is None else [values, total]), near_blocks)
+
+
+ON_CHIP = pl.BlockSpec(memory_space=pltpu.VMEM)
+IN_PLACE = pl.BlockSpec(memory_space=pltpu.HBM)
+PARAMS = pltpu.CompilerParams(vmem_limit_bytes=48 << 20)
+CHARGE_PARAMS = pltpu.CompilerParams(vmem_limit_bytes=60 << 20)
+FULL_PARAMS = pltpu.CompilerParams(vmem_limit_bytes=60 << 20)
+NEAR_PARAMS = pltpu.CompilerParams(vmem_limit_bytes=48 << 20)
 
 
 def whole(shape):
@@ -1061,77 +1126,102 @@
 
     charges = pl.pallas_call(
         charge_kernel,
-        grid=(STEN,),
-        in_specs=[
-            whole((RHS, BASIS, elements)),
-            pl.BlockSpec((STEN, BASIS, elements), lambda i: (i, 0, 0)),
-            whole((2, elements)),
-        ],
-        out_specs=whole((SUB, 128, LANES)),
-        out_shape=struct((SUB, 128, LANES), b16),
+        in_specs=[IN_PLACE] * 3,
+        out_specs=ON_CHIP,
+        out_shape=struct((SUB, 112, LANES), b16),
         scratch_shapes=[
+            pltpu.VMEM(projection.shape, b16),
+            pltpu.VMEM((RHS, BASIS, elements), f32),
+            pltpu.VMEM((2, elements), jnp.int32),
             pltpu.VMEM((RHS, BASIS, elements), f32),
             pltpu.VMEM((STEN, SUB, SUB, LANES), f32),
             pltpu.VMEM((STEN * STEN, SUB, LANES), f32),
+            pltpu.SemaphoreType.DMA((STEN + 2,)),
         ],
+        compiler_params=CHARGE_PARAMS,
         name="charges",
     )(currents, projection, shifts)
     slab = lax.all_to_all(charges, "col", 0, 0, tiled=True)
 
     columns, rows = even_positions(row_count, col_count)
     table = struct((quarter, quarter), b16)
-    col_tables = pl.pallas_call(column_table_kernel, out_shape=[table] * 3, name="column_tables")(
-        *position_bases(columns, length)
-    )
+    col_tables = pl.pallas_call(
+        column_table_kernel,
+        out_specs=[ON_CHIP] * 3,
+        out_shape=[table] * 3,
+        compiler_params=PARAMS,
+        name="column_tables",
+    )(*position_bases(columns, length))
     spread = struct((2 * quarter, LANES), f32)
     row_tables = pl.pallas_call(
-        row_table_kernel, out_shape=[table] * 6 + [spread] * 2, name="row_tables"
+        row_table_kernel,
+        out_shape=[table] * 6 + [spread] * 2,
+        compiler_params=FULL_PARAMS,
+        name="row_tables",
     )(green, *position_bases(rows, length), *order_bases(rows, length))
+    slab, *row_tables = lax.optimization_barrier((slab, *row_tables))
 
     spectrum = pl.pallas_call(
         functools.partial(column_kernel, col_count),
         out_shape=struct((devices, 40, LANES), b16),
+        in_specs=[ON_CHIP] * 4,
+        out_specs=ON_CHIP,
+        compiler_params=PARAMS,
         name="columns",
     )(slab, *col_tables)
     spectrum, held = lax.optimization_barrier((spectrum, currents))
     arrived = lax.all_to_all(spectrum, ("row", "col"), 0, 0, tiled=True)
-    near = near_call(held, None, near_blocks, (0,), 0, BASIS // SUB)
+    near = near_call(held, None, near_blocks, (0,), 0, BASIS)
     arrived, near = lax.optimization_barrier((arrived, near))
     rows_back = pl.pallas_call(
         functools.partial(row_kernel, row_count, col_count),
         out_shape=struct((devices, 40, LANES), b16),
+        in_specs=[ON_CHIP] + [IN_PLACE] * 8,
+        out_specs=ON_CHIP,
+        scratch_shapes=[pltpu.VMEM((quarter, quarter), b16)] * 6
+        + [pltpu.VMEM((2 * quarter, LANES), f32)] * 2
+        + [pltpu.SemaphoreType.DMA((8,))],
+        compiler_params=FULL_PARAMS,
         name="rows",
     )(arrived, *row_tables)
     rows_back, ready = lax.optimization_barrier((rows_back, arrived))
     returned = lax.all_to_all(rows_back, ("row", "col"), 0, 0, tiled=True)
     picked = pl.pallas_call(
-        pick_kernel, out_shape=struct((NEIGH - 1, RHS, BASIS, elements), b16), name="pick"
+        pick_kernel,
+        in_specs=[whole(currents.shape), ON_CHIP, ON_CHIP, whole(partners.shape)],
+        out_specs=ON_CHIP,
+        out_shape=struct((NEIGH - 1, RHS, BASIS, elements), b16),
+        compiler_params=PARAMS,
+        name="pick",
     )(held, slab, ready, partners)
     others = tuple(range(1, NEIGH))
-    near = near_call(picked, near, near_blocks, others, 0, BASIS // SUB // 2)
+    near = near_call(picked, near, near_blocks, others, 0, BASIS // 2)
     returned, near, picked = lax.optimization_barrier((returned, near, picked))
     potential = pl.pallas_call(
         functools.partial(grid_kernel, col_count),
         out_shape=struct((SUB, 80, LANES), b16),
+        in_specs=[ON_CHIP] * 4,
+        out_specs=ON_CHIP,
+        compiler_params=PARAMS,
         name="grid",
     )(returned, *col_tables)
     potential, near, picked = lax.optimization_barrier((potential, near, picked))
     pieces = lax.all_to_all(potential, "col", 0, 0, tiled=True)
-    near = near_call(picked, near, near_blocks, others, BASIS // SUB // 2, BASIS // SUB)
-
-    depth = 16
+    near = near_call(picked, near, near_blocks, others, BASIS // 2, BASIS)
+
     return pl.pallas_call(
         far_kernel,
-        grid=(BASIS // depth,),
-        in_specs=[
-            whole((SUB, 80, LANES)),
-            pl.BlockSpec((STEN * STEN, depth, elements), lambda i: (0, i, 0)),
-            whole((2, elements)),
-            pl.BlockSpec((RHS, depth, elements), lambda i: (0, i, 0)),
+        in_specs=[ON_CHIP, IN_PLACE, IN_PLACE, ON_CHIP],
+        out_specs=IN_PLACE,
+        out_shape=struct((RHS, BASIS, elements), f32),
+        scratch_shapes=[
+            pltpu.VMEM(projection.shape, b16),
+            pltpu.VMEM((STEN * STEN, SUB, LANES), f32),
+            pltpu.VMEM((2, elements), jnp.int32),
+            pltpu.VMEM((RHS, BASIS, elements), f32),
+            pltpu.SemaphoreType.DMA((9,)),
         ],
-        out_specs=pl.BlockSpec((RHS, depth, elements), lambda i: (0, i, 0)),
-        out_shape=struct((RHS, BASIS, elements), f32),
-        scratch_shapes=[pltpu.VMEM((STEN * STEN, SUB, LANES), f32)],
+        compiler_params=FULL_PARAMS,
         name="far",
     )(pieces, projection, shifts, near)
 

time: 88.1 us -> 80.9 us (0.918)
  Pallas kernels: 53.9 us -> 35.3 us
  local copies, waits for them, and re-layouts: 2.83 us -> 8.68 us
  waiting for transfers between devices: 11.8 us -> 17.5 us
    pallas_call x8, Pallas kernels: 42.8 us -> 26.9 us  [the longest x3 10.1 us: near_call(): pl.pallas_call(functools.partial(near_kernel, total is not None, slots, s...]
    all_to_all x1, waiting for transfers between devices: 0.54 us -> 8.28 us  [shards_real(): arrived = lax.all_to_all(spectrum, ('row', 'col'), 0, 0, tiled=True)]
    all_to_all x1, waiting for transfers between devices: 6.82 us -> 0.01 us  [shards_real(): slab = lax.all_to_all(charges, 'col', 0, 0, tiled=True)]
    unnamed x8 -> x26, local copies, waits for them, and re-layouts: 2.83 us -> 8.68 us
    all_to_all x1, waiting for transfers between devices: 3.29 us -> 6.45 us  [shards_real(): returned = lax.all_to_all(rows_back, ('row', 'col'), 0, 0, tiled=True)]
    all_to_all x1, starting transfers between devices: 5.3 us -> 2.61 us  [shards_real(): returned = lax.all_to_all(rows_back, ('row', 'col'), 0, 0, tiled=True)]
    all_to_all x1, starting transfers between devices: 3.54 us -> 6.07 us  [shards_real(): arrived = lax.all_to_all(spectrum, ('row', 'col'), 0, 0, tiled=True)]
    pallas_call x1, Pallas kernels: 3.76 us -> 2.13 us  [shards_real(): pl.pallas_call(functools.partial(column_kernel, col_count), out_shape=str...]
  transfers between devices with their start and end apart: 4 -> 4, of which waited for: 4 -> 3; matrix products, arithmetic and copies ran while one was open for 0% -> 0% of each run, Pallas kernels for 33% -> 21%
where the time goes in v3:
time: 80.9 us; the launch traced here: 80 us
  Pallas kernels  35.3 us (44%)
  starting transfers between devices  18.4 us (23%)
  waiting for transfers between devices  17.5 us (22%)
  local copies, waits for them, and re-layouts  8.68 us (11%)
    pallas_call x3, Pallas kernels, near_call(): pl.pallas_call(functools.partial(near_kernel, total is not None, slots, s...  10.1 us
    unnamed x26, local copies, waits for them, and re-layouts  8.68 us
    all_to_all x1, waiting for transfers between devices, shards_real(): arrived = lax.all_to_all(spectrum, ('row', 'col'), 0, 0, tiled=True)  8.28 us
    all_to_all x1, waiting for transfers between devices, shards_real(): returned = lax.all_to_all(rows_back, ('row', 'col'), 0, 0, tiled=True)  6.45 us
    all_to_all x1, starting transfers between devices, shards_real(): slab = lax.all_to_all(charges, 'col', 0, 0, tiled=True)  6.37 us
    all_to_all x1, starting transfers between devices, shards_real(): arrived = lax.all_to_all(spectrum, ('row', 'col'), 0, 0, tiled=True)  6.07 us
    pallas_call x1, Pallas kernels, shards_real(): pl.pallas_call(charge_kernel, in_specs=[IN_PLACE] * 3, out_specs=ON_CHIP,...  5.26 us
    pallas_call x1, Pallas kernels, shards_real(): pl.pallas_call(far_kernel, in_specs=[ON_CHIP, IN_PLACE, IN_PLACE, ON_CHIP...  5.17 us
  transfers between devices with their start and end apart: 4, of which 3 were waited for; matrix products, arithmetic and copies ran while one was open for 0% of the time, Pallas kernels for 21%

profile of v3, /device:TPU:0, one launch (start us, length us, event | category | flops | bytes accessed | tf_op | source)
XLA Modules:
  0.0 80.0 jit_solution(6406564334557946239)
XLA Ops:
  0.0 0.0 copy-start.3
  0.0 0.0 copy-start.11
  0.0 5.3 %charges.1 = bf16[8,112,128]{2,1,0:T(8,128)(2,1)} custom-call(f32[2,64,512]{2,1,0:T(8,128)} %currents_ref.2, bf16[64,64,512]{2,1,0:T(8,128)(2,1)} %projection_ref.3, s32[2,512]{1,0:T(2,128)} %shifts_ref.3), custom_call_target="tpu_custom_call" | custom-call | tf_op jit(solution)/shard_map/charges/pallas_call | solution.py:1127
  5.3 6.4 %all-to-all-start = ((bf16[8,112,128]{2,1,0:T(8,128)(2,1)}), bf16[8,112,128]{2,1,0:T(8,128)(2,1)S(1)}, u32[]{:S(2)}, u32[]{:S(2)}) async-start(bf16[8,112,128]{2,1,0:T(8,128)(2,1)} %charges.1), calls=%async_computation | async-start | bytes 458752 | tf_op jit(solution)/shard_map/all_to_all | solution.py:1144
  11.6 0.0 copy-start.5
  11.6 0.9 %copy-done.5 = f32[64,512]{1,0:T(8,128)S(1)} copy-done((f32[64,512]{1,0:T(8,128)S(1)}, f32[64,512]{1,0:T(8,128)}, u32[]{:S(2)}) %copy-start.5) | copy-done | bytes 131096
  12.5 0.0 copy-start.6
  12.5 0.9 %copy-done.6 = f32[64,512]{1,0:T(8,128)S(1)} copy-done((f32[64,512]{1,0:T(8,128)S(1)}, f32[64,512]{1,0:T(8,128)}, u32[]{:S(2)}) %copy-start.6) | copy-done | bytes 131096
  13.5 0.0 copy-start.7
  13.5 0.7 copy-done.7
  14.2 0.0 copy-start.8
  14.2 0.7 copy-done.8
  14.9 0.0 copy-start.9
  14.9 0.7 copy-done.9
  15.6 0.0 copy-start.10
  15.6 0.7 copy-done.10
  16.3 0.7 column_tables.1
  17.1 4.7 %row_tables.1 = (bf16[512,512]{1,0:T(8,128)(2,1)}, bf16[512,512]{1,0:T(8,128)(2,1)}, bf16[512,512]{1,0:T(8,128)(2,1)}, bf16[512,512]{1,0:T(8,128)(2,1)}, bf16[51...) custom-call(f32[64,2048]{1,0:T(8,128)} %green_ref.1, ...), custom_call_target="tpu_custom_call" | custom-call | tf_op jit(solution)/shard_map/row_tables/pallas_call | solution.py:1156
  21.8 0.0 all-to-all-done.rows_ref.slab_ref
  21.8 2.1 %columns.1 = bf16[32,40,128]{2,1,0:T(8,128)(2,1)} custom-call(bf16[8,112,128]{2,1,0:T(8,128)(2,1)S(1)} %all-to-all-done.rows_ref.slab_ref, bf16[512,512]{1,0:T(8,128)(2,1)S(1)} %get-tuple-element.46.even_cos, bf16[512,512]{1,0:T(8,128)(2,1)S(1)} %get-tuple-element.47.even_sin, bf16[512,512]{1,0:T(8,128)(2,1)S(1)} %get-tuple-element.48.odd_cos), custom_call_target="tpu_custom_call" | custom-call | tf_op jit(solution)/shard_map/columns/pallas_call | solution.py:1164
  23.9 6.1 %all-to-all-start.1 = ((bf16[32,40,128]{2,1,0:T(8,128)(2,1)}), bf16[32,40,128]{2,1,0:T(8,128)(2,1)S(1)}, u32[]{:S(2)}, u32[]{:S(2)}) async-start(bf16[32,40,128]{2,1,0:T(8,128)(2,1)} %columns.1), calls=%async_computation.1 | async-start | bytes 655360 | tf_op jit(solution)/shard_map/all_to_all | solution.py:1173
  30.0 0.0 copy-start.2
  30.0 0.9 %copy-done.2 = f32[2,64,512]{2,1,0:T(8,128)S(1)} copy-done((f32[2,64,512]{2,1,0:T(8,128)S(1)}, f32[2,64,512]{2,1,0:T(8,128)}, u32[]{:S(2)}) %copy-start.2) | copy-done | bytes 262168
  30.9 2.8 %near.3.refs_1_ = f32[2,64,512]{2,1,0:T(8,128)S(1)} custom-call(f32[2,64,512]{2,1,0:T(8,128)S(1)} %copy-done.2, bf16[4,64,64,512]{3,2,1,0:T(8,128)(2,1)} %refs_2_.5), custom_call_target="tpu_custom_call" | custom-call | tf_op jit(solution)/shard_map/near/pallas_call | solution.py:1089
  33.7 8.3 %all-to-all-done.1.in_ref.arrived_ref = bf16[32,40,128]{2,1,0:T(8,128)(2,1)S(1)} async-done(((bf16[32,40,128]{2,1,0:T(8,128)(2,1)}), bf16[32,40,128]{2,1,0:T(8,128)(2,1)S(1)}, u32[]{:S(2)}, u32[]{:S(2)}) %all-to-all-start.1) | async-done | bytes 327712 | tf_op jit(solution)/shard_map/all_to_all | solution.py:1173
  42.0 0.0 copy-start
  42.0 0.7 copy-done
  42.7 4.7 %rows.1 = bf16[32,40,128]{2,1,0:T(8,128)(2,1)} custom-call(bf16[32,40,128]{2,1,0:T(8,128)(2,1)} %copy-done, bf16[512,512]{1,0:T(8,128)(2,1)} %get-tuple-element.52.refs_0_, bf16[512,512]{1,0:T(8,128)(2,1)} %get-tuple-element.53.refs_1_, bf16[512,512]{1,0:T(8,128)(2,1)} %get-tuple-element.54.refs_2_, bf16[512,512]{1,0:T(8,128)(2,1)} %get-tuple-element.55.refs_3_, ...), custom_call_target="tpu_custom_call" | custom-call | tf_op jit(solution)/shard_map/rows/pallas_call | solution.py:1176
  47.4 2.6 %all-to-all-start.2 = ((bf16[32,40,128]{2,1,0:T(8,128)(2,1)}), bf16[32,40,128]{2,1,0:T(8,128)(2,1)S(1)}, u32[]{:S(2)}, u32[]{:S(2)}) async-start(bf16[32,40,128]{2,1,0:T(8,128)(2,1)} %rows.1), calls=%async_computation.2 | async-start | bytes 655360 | tf_op jit(solution)/shard_map/all_to_all | solution.py:1188
  50.0 0.0 copy-done.3
  50.0 0.0 copy-done.11
  50.1 0.0 copy-start.1
  50.1 1.0 %copy-done.1 = bf16[32,40,128]{2,1,0:T(8,128)(2,1)S(1)} copy-done((bf16[32,40,128]{2,1,0:T(8,128)(2,1)S(1)}, bf16[32,40,128]{2,1,0:T(8,128)(2,1)}, u32[]{:S(2)}) %copy-start.1) | copy-done | bytes 327704
  51.0 0.9 %pick.1.refs_0_ = bf16[3,2,64,512]{3,2,1,0:T(8,128)(2,1)S(1)} custom-call(f32[2,64,512]{2,1,0:T(8,128)S(1)} %copy-done.3, bf16[8,112,128]{2,1,0:T(8,128)(2,1)S(1)} %all-to-all-done.rows_ref.slab_ref, bf16[32,40,128]{2,1,0:T(8,128)(2,1)S(1)} %copy-done.1, s32[4,512]{1,0:T(4,128)S(1)} %copy-done.11), custom_call_target="tpu_custom_call" | custom-call | tf_op jit(solution)/shard_map/pick/pallas_call | solution.py:1189
  51.9 3.7 %near.4.refs_1_ = f32[2,64,512]{2,1,0:T(8,128)S(1)} custom-call(bf16[3,2,64,512]{3,2,1,0:T(8,128)(2,1)S(1)} %pick.1.refs_0_, f32[2,64,512]{2,1,0:T(8,128)S(1)} %near.3.refs_1_, bf16[4,64,64,512]{3,2,1,0:T(8,128)(2,1)} %refs_2_.5), custom_call_target="tpu_custom_call" | custom-call | tf_op jit(solution)/shard_map/near/pallas_call | solution.py:1089
  55.6 6.4 %all-to-all-done.2.in_ref = bf16[32,40,128]{2,1,0:T(8,128)(2,1)S(1)} async-done(((bf16[32,40,128]{2,1,0:T(8,128)(2,1)}), bf16[32,40,128]{2,1,0:T(8,128)(2,1)S(1)}, u32[]{:S(2)}, u32[]{:S(2)}) %all-to-all-start.2) | async-done | bytes 327712 | tf_op jit(solution)/shard_map/all_to_all | solution.py:1188
  62.1 1.6 %grid.1 = bf16[8,80,128]{2,1,0:T(8,128)(2,1)} custom-call(bf16[32,40,128]{2,1,0:T(8,128)(2,1)S(1)} %all-to-all-done.2.in_ref, bf16[512,512]{1,0:T(8,128)(2,1)S(1)} %get-tuple-element.46.even_cos, bf16[512,512]{1,0:T(8,128)(2,1)S(1)} %get-tuple-element.47.even_sin, bf16[512,512]{1,0:T(8,128)(2,1)S(1)} %get-tuple-element.48.odd_cos), custom_call_target="tpu_custom_call" | custom-call | tf_op jit(solution)/shard_map/grid/pallas_call | solution.py:1200
  63.7 3.4 %all-to-all-start.3 = ((bf16[8,80,128]{2,1,0:T(8,128)(2,1)}), bf16[8,80,128]{2,1,0:T(8,128)(2,1)S(1)}, u32[]{:S(2)}, u32[]{:S(2)}) async-start(bf16[8,80,128]{2,1,0:T(8,128)(2,1)} %grid.1), calls=%async_computation.3 | async-start | bytes 327680 | tf_op jit(solution)/shard_map/all_to_all | solution.py:1209
  67.1 3.7 %near.5.near_ref = f32[2,64,512]{2,1,0:T(8,128)S(1)} custom-call(bf16[3,2,64,512]{3,2,1,0:T(8,128)(2,1)S(1)} %pick.1.refs_0_, f32[2,64,512]{2,1,0:T(8,128)S(1)} %near.4.refs_1_, bf16[4,64,64,512]{3,2,1,0:T(8,128)(2,1)} %refs_2_.5), custom_call_target="tpu_custom_call" | custom-call | tf_op jit(solution)/shard_map/near/pallas_call | solution.py:1089
  70.7 0.0 copy-start.4
  70.7 0.7 copy-done.4
  71.4 2.8 %all-to-all-done.3.grid_ref = bf16[8,80,128]{2,1,0:T(8,128)(2,1)S(1)} async-done(((bf16[8,80,128]{2,1,0:T(8,128)(2,1)}), bf16[8,80,128]{2,1,0:T(8,128)(2,1)S(1)}, u32[]{:S(2)}, u32[]{:S(2)}) %all-to-all-start.3) | async-done | bytes 163872 | tf_op jit(solution)/shard_map/all_to_all | solution.py:1209
  74.2 0.0 copy-start.12
  74.2 0.7 copy-done.12
  74.9 5.2 %far.1 = f32[2,64,512]{2,1,0:T(8,128)} custom-call(bf16[8,80,128]{2,1,0:T(8,128)(2,1)} %copy-done.12, bf16[64,64,512]{2,1,0:T(8,128)(2,1)} %projection_ref.3, s32[2,512]{1,0:T(2,128)} %shifts_ref.3, f32[2,64,512]{2,1,0:T(8,128)} %copy-done.4), custom_call_target="tpu_custom_call" | custom-call | tf_op jit(solution)/shard_map/far/pallas_call | solution.py:1212
Async XLA Ops:
  0.0 50.0 %copy-start.3 = (f32[2,64,512]{2,1,0:T(8,128)S(1)}, f32[2,64,512]{2,1,0:T(8,128)}, u32[]{:S(2)}) copy-start(f32[2,64,512]{2,1,0:T(8,128)} %currents_ref.2) | copy-start | bytes 786436
  0.0 50.0 %copy-start.11 = (s32[4,512]{1,0:T(4,128)S(1)}, s32[4,512]{1,0:T(4,128)}, u32[]{:S(2)}) copy-start(s32[4,512]{1,0:T(4,128)} %partners_ref.1) | copy-start | bytes 24580
  5.3 16.5 %all-to-all-start = ((bf16[8,112,128]{2,1,0:T(8,128)(2,1)}), bf16[8,112,128]{2,1,0:T(8,128)(2,1)S(1)}, u32[]{:S(2)}, u32[]{:S(2)}) async-start(bf16[8,112,128]{2,1,0:T(8,128)(2,1)} %charges.1), calls=%async_computation | async-start | bytes 458752 | tf_op jit(solution)/shard_map/all_to_all | solution.py:1144
  11.6 0.9 %copy-start.5 = (f32[64,512]{1,0:T(8,128)S(1)}, f32[64,512]{1,0:T(8,128)}, u32[]{:S(2)}) copy-start(f32[64,512]{1,0:T(8,128)} %constant.41.clone.refs_1_) | copy-start | bytes 393220
  12.5 0.9 %copy-start.6 = (f32[64,512]{1,0:T(8,128)S(1)}, f32[64,512]{1,0:T(8,128)}, u32[]{:S(2)}) copy-start(f32[64,512]{1,0:T(8,128)} %constant.40.clone.refs_0_) | copy-start | bytes 393220
  13.5 0.7 copy-start.7
  14.2 0.7 copy-start.8
  14.9 0.7 copy-start.9
  15.6 0.7 copy-start.10
  23.9 18.1 %all-to-all-start.1 = ((bf16[32,40,128]{2,1,0:T(8,128)(2,1)}), bf16[32,40,128]{2,1,0:T(8,128)(2,1)S(1)}, u32[]{:S(2)}, u32[]{:S(2)}) async-start(bf16[32,40,128]{2,1,0:T(8,128)(2,1)} %columns.1), calls=%async_computation.1 | async-start | bytes 655360 | tf_op jit(solution)/shard_map/all_to_all | solution.py:1173
  30.0 1.0 %copy-start.2 = (f32[2,64,512]{2,1,0:T(8,128)S(1)}, f32[2,64,512]{2,1,0:T(8,128)}, u32[]{:S(2)}) copy-start(f32[2,64,512]{2,1,0:T(8,128)} %currents_ref.2) | copy-start | bytes 786436
  42.0 0.7 copy-start
  47.4 14.6 %all-to-all-start.2 = ((bf16[32,40,128]{2,1,0:T(8,128)(2,1)}), bf16[32,40,128]{2,1,0:T(8,128)(2,1)S(1)}, u32[]{:S(2)}, u32[]{:S(2)}) async-start(bf16[32,40,128]{2,1,0:T(8,128)(2,1)} %rows.1), calls=%async_computation.2 | async-start | bytes 655360 | tf_op jit(solution)/shard_map/all_to_all | solution.py:1188
  50.1 1.0 %copy-start.1 = (bf16[32,40,128]{2,1,0:T(8,128)(2,1)S(1)}, bf16[32,40,128]{2,1,0:T(8,128)(2,1)}, u32[]{:S(2)}) copy-start(bf16[32,40,128]{2,1,0:T(8,128)(2,1)} %copy-done) | copy-start | bytes 983044
  63.7 10.5 %all-to-all-start.3 = ((bf16[8,80,128]{2,1,0:T(8,128)(2,1)}), bf16[8,80,128]{2,1,0:T(8,128)(2,1)S(1)}, u32[]{:S(2)}, u32[]{:S(2)}) async-start(bf16[8,80,128]{2,1,0:T(8,128)(2,1)} %grid.1), calls=%async_computation.3 | async-start | bytes 327680 | tf_op jit(solution)/shard_map/all_to_all | solution.py:1209
  70.7 0.7 copy-start.4
  74.2 0.7 copy-start.12

commit v4 on v3

--- a/solution.py
+++ b/solution.py
@@ -582,11 +582,21 @@
     grouped = positions.reshape(-1, SUB)
     offsets = grouped[0] - grouped[0, 0]
     assert (grouped == grouped[:, :1] + offsets[None, :]).all()
-    return (
-        *angle_pair(grouped[:, 0], orders, length),
-        *angle_pair(offsets, orders, length),
-        *angle_pair(offsets + 1, orders, length),
-    )
+    return np.concatenate(
+        [
+            *angle_pair(grouped[:, 0], orders, length),
+            *angle_pair(offsets, orders, length),
+            *angle_pair(offsets + 1, orders, length),
+        ]
+    )
+
+
+def split_rows(ref, *counts):
+    start, parts = 0, []
+    for count in counts:
+        parts.append(ref.at[start : start + count])
+        start += count
+    return parts
 
 
 def order_bases(positions, length):
@@ -595,7 +605,7 @@
     for parity in range(2):
         result.extend(angle_pair(bases, positions + parity, length))
         result.extend(angle_pair(np.arange(SUB), positions + parity, length))
-    return tuple(result)
+    return np.concatenate(result)
 
 
 def fill_by_position(sign_of, bases, out_refs):
@@ -619,12 +629,16 @@
     lax.fori_loop(0, base_cos.shape[0] // 2, pair, 0)
 
 
-def column_table_kernel(*refs):
-    fill_by_position(lambda row: (1 - 2 * ((row // 2) & 1)).astype(jnp.float32), refs[:6], refs[6:])
-
-
-def row_table_kernel(green_ref, *refs):
-    position, order, outs = refs[:6], refs[6:14], refs[14:]
+def column_table_kernel(bases_ref, *outs):
+    count = (bases_ref.shape[0] - 4 * SUB) // 2
+    bases = split_rows(bases_ref, count, count, SUB, SUB, SUB, SUB)
+    fill_by_position(lambda row: (1 - 2 * ((row // 2) & 1)).astype(jnp.float32), bases, outs)
+
+
+def row_table_kernel(green_ref, position_ref, order_ref, *outs):
+    count = (position_ref.shape[0] - 4 * SUB) // 2
+    position = split_rows(position_ref, count, count, SUB, SUB, SUB, SUB)
+    order = split_rows(order_ref, count, count, SUB, SUB, count, count, SUB, SUB)
     quarter = position[0].shape[1]
     tiles = quarter // LANES
     sub = sub_index((SUB, quarter))
@@ -822,28 +836,29 @@
                 device += 1
 
 
-def row_kernel(row_count, col_count, in_ref, *refs):
-    sources, out_ref, held, sems = refs[:8], refs[8], refs[9:17], refs[17]
+def row_kernel(row_count, col_count, *refs):
+    sources, out_ref, held, sems = refs[:9], refs[9], refs[10:19], refs[19]
     loads = [
         pltpu.make_async_copy(source, target, sems.at[n])
         for n, (source, target) in enumerate(zip(sources, held))
     ]
     for load in loads:
         load.start()
-    even_cos, even_sin, odd_cos, back_cos, back_sin, back_odd, sum_ref, diff_ref = held
+    in_ref, even_cos, even_sin, odd_cos, back_cos, back_sin, back_odd, sum_ref, diff_ref = held
+    loads[0].wait()
     even, odd = add_outer_rows(
         lambda i, j: in_ref[i * col_count + j].astype(jnp.float32), row_count, col_count
     )
     flip = jnp.where((sub_index(odd.shape) & 4) == 0, 1.0, -1.0)
     both = jnp.concatenate([odd, odd * flip], axis=1).astype(jnp.bfloat16)
     even = even.astype(jnp.bfloat16)
-    for n in range(3):
+    for n in range(1, 4):
         loads[n].wait()
     a = [dot(even_cos[...], even), dot(even_sin[...], even)]
     both = dot(odd_cos[...], both)
     b = [both[:, :LANES], both[:, LANES:]]
     quarter = odd.shape[0]
-    for n in range(3, 8):
+    for n in range(4, 9):
         loads[n].wait()
 
     def pieces(left, right):
@@ -906,7 +921,9 @@
     scatter_rows(even, odd, count, put)
 
 
-def far_kernel(grid_ref, projection_ref, shifts_ref, near_ref, out_ref, weights, samples, shifts, totals_ref, sems):
+def far_kernel(
+    source_ref, projection_ref, shifts_ref, near_ref, out_ref, grid_ref, weights, samples, shifts, totals_ref, sems
+):
     depth = 16
     count = BASIS // depth
 
@@ -917,7 +934,11 @@
         )
 
     load_shifts = pltpu.make_async_copy(shifts_ref, shifts, sems.at[0])
+    load_grid = pltpu.make_async_copy(source_ref, grid_ref, sems.at[1 + 2 * count])
+    load_near = pltpu.make_async_copy(near_ref, totals_ref, sems.at[2 + 2 * count])
+    load_grid.start()
     load_shifts.start()
+    load_near.start()
     for i in range(count):
         load(i).start()
 
@@ -928,9 +949,12 @@
         samples[s] = value
 
     load_shifts.wait()
+    load_grid.wait()
     read_samples(
         part, lambda e: part(e, GROUPS), tiled_shifts(shifts, 0), tiled_shifts(shifts, 1), put
     )
+    load_near.wait()
+
     def store(i):
         rows = pl.ds(i * depth, depth)
         return pltpu.make_async_copy(totals_ref.at[:, rows], out_ref.at[:, rows], sems.at[1 + i])
@@ -951,7 +975,7 @@
             return tuple(totals)
 
         start = tuple(
-            near_ref[q, span, LANES * t : LANES * (t + 1)] for q in range(RHS) for t in range(TILES)
+            totals_ref[q, span, LANES * t : LANES * (t + 1)] for q in range(RHS) for t in range(TILES)
         )
         totals = lax.fori_loop(0, STEN, add_row, start)
         for q in range(RHS):
@@ -1151,16 +1175,7 @@
         out_shape=[table] * 3,
         compiler_params=PARAMS,
         name="column_tables",
-    )(*position_bases(columns, length))
-    spread = struct((2 * quarter, LANES), f32)
-    row_tables = pl.pallas_call(
-        row_table_kernel,
-        out_shape=[table] * 6 + [spread] * 2,
-        compiler_params=FULL_PARAMS,
-        name="row_tables",
-    )(green, *position_bases(rows, length), *order_bases(rows, length))
-    slab, *row_tables = lax.optimization_barrier((slab, *row_tables))
-
+    )(jnp.asarray(position_bases(columns, length)))
     spectrum = pl.pallas_call(
         functools.partial(column_kernel, col_count),
         out_shape=struct((devices, 40, LANES), b16),
@@ -1169,18 +1184,26 @@
         compiler_params=PARAMS,
         name="columns",
     )(slab, *col_tables)
-    spectrum, held = lax.optimization_barrier((spectrum, currents))
+    spectrum, held, held_green = lax.optimization_barrier((spectrum, currents, green))
     arrived = lax.all_to_all(spectrum, ("row", "col"), 0, 0, tiled=True)
     near = near_call(held, None, near_blocks, (0,), 0, BASIS)
-    arrived, near = lax.optimization_barrier((arrived, near))
+    spread = struct((2 * quarter, LANES), f32)
+    row_tables = pl.pallas_call(
+        row_table_kernel,
+        out_shape=[table] * 6 + [spread] * 2,
+        compiler_params=FULL_PARAMS,
+        name="row_tables",
+    )(held_green, jnp.asarray(position_bases(rows, length)), jnp.asarray(order_bases(rows, length)))
+    arrived, near, *row_tables = lax.optimization_barrier((arrived, near, *row_tables))
     rows_back = pl.pallas_call(
         functools.partial(row_kernel, row_count, col_count),
         out_shape=struct((devices, 40, LANES), b16),
-        in_specs=[ON_CHIP] + [IN_PLACE] * 8,
+        in_specs=[IN_PLACE] * 9,
         out_specs=ON_CHIP,
-        scratch_shapes=[pltpu.VMEM((quarter, quarter), b16)] * 6
+        scratch_shapes=[pltpu.VMEM((devices, 40, LANES), b16)]
+        + [pltpu.VMEM((quarter, quarter), b16)] * 6
         + [pltpu.VMEM((2 * quarter, LANES), f32)] * 2
-        + [pltpu.SemaphoreType.DMA((8,))],
+        + [pltpu.SemaphoreType.DMA((9,))],
         compiler_params=FULL_PARAMS,
         name="rows",
     )(arrived, *row_tables)
@@ -1211,15 +1234,16 @@
 
     return pl.pallas_call(
         far_kernel,
-        in_specs=[ON_CHIP, IN_PLACE, IN_PLACE, ON_CHIP],
+        in_specs=[IN_PLACE] * 4,
         out_specs=IN_PLACE,
         out_shape=struct((RHS, BASIS, elements), f32),
         scratch_shapes=[
+            pltpu.VMEM((SUB, 80, LANES), b16),
             pltpu.VMEM(projection.shape, b16),
             pltpu.VMEM((STEN * STEN, SUB, LANES), f32),
             pltpu.VMEM((2, elements), jnp.int32),
             pltpu.VMEM((RHS, BASIS, elements), f32),
-            pltpu.SemaphoreType.DMA((9,)),
+            pltpu.SemaphoreType.DMA((11,)),
         ],
         compiler_params=FULL_PARAMS,
         name="far",

time: 80.9 us -> 75.4 us (0.932)
  local copies, waits for them, and re-layouts: 8.68 us -> 4.97 us
  waiting for transfers between devices: 17.5 us -> 20.2 us
  starting transfers between devices: 18.4 us -> 15.9 us
  Pallas kernels: 35.3 us -> 33.6 us
    all_to_all x1, waiting for transfers between devices: 0.01 us -> 7.31 us  [shards_real(): slab = lax.all_to_all(charges, 'col', 0, 0, tiled=True)]
    all_to_all x1, waiting for transfers between devices: 8.28 us -> 3.66 us  [shards_real(): arrived = lax.all_to_all(spectrum, ('row', 'col'), 0, 0, tiled=True)]
    unnamed x26 -> x16, local copies, waits for them, and re-layouts: 8.68 us -> 4.97 us
    all_to_all x1, starting transfers between devices: 6.07 us -> 3.54 us  [shards_real(): arrived = lax.all_to_all(spectrum, ('row', 'col'), 0, 0, tiled=True)]
    pallas_call x1, Pallas kernels: 4.69 us -> 3.8 us  [shards_real(): pl.pallas_call(functools.partial(row_kernel, row_count, col_count), out_s...]
  transfers between devices with their start and end apart: 4 -> 4, of which waited for: 3 -> 4; matrix products, arithmetic and copies ran while one was open for 0% -> 0% of each run, Pallas kernels for 21% -> 22%
where the time goes in v4:
time: 75.4 us; the launch traced here: 74.8 us
  Pallas kernels  33.6 us (45%)
  waiting for transfers between devices  20.2 us (27%)
  starting transfers between devices  15.9 us (21%)
  local copies, waits for them, and re-layouts  4.97 us (7%)
    pallas_call x3, Pallas kernels, near_call(): pl.pallas_call(functools.partial(near_kernel, total is not None, slots, s...  10.1 us
    all_to_all x1, waiting for transfers between devices, shards_real(): slab = lax.all_to_all(charges, 'col', 0, 0, tiled=True)  7.31 us
    all_to_all x1, waiting for transfers between devices, shards_real(): returned = lax.all_to_all(rows_back, ('row', 'col'), 0, 0, tiled=True)  6.44 us
    all_to_all x1, starting transfers between devices, shards_real(): slab = lax.all_to_all(charges, 'col', 0, 0, tiled=True)  6.37 us
    pallas_call x1, Pallas kernels, shards_real(): pl.pallas_call(charge_kernel, in_specs=[IN_PLACE] * 3, out_specs=ON_CHIP,...  5.37 us
    unnamed x16, local copies, waits for them, and re-layouts  4.97 us
    pallas_call x1, Pallas kernels, shards_real(): pl.pallas_call(row_table_kernel, out_shape=[table] * 6 + [spread] * 2, co...  4.62 us
    pallas_call x1, Pallas kernels, shards_real(): pl.pallas_call(far_kernel, in_specs=[IN_PLACE] * 4, out_specs=IN_PLACE, o...  4.38 us
  transfers between devices with their start and end apart: 4, of which 4 were waited for; matrix products, arithmetic and copies ran while one was open for 0% of the time, Pallas kernels for 22%

profile of v4, /device:TPU:0, one launch (start us, length us, event | category | flops | bytes accessed | tf_op | source)
XLA Modules:
  0.0 74.8 jit_solution(17618984779752465942)
XLA Ops:
  0.0 0.0 copy-start.3
  0.0 0.0 copy-start.6
  0.0 5.4 %charges.1 = bf16[8,112,128]{2,1,0:T(8,128)(2,1)} custom-call(f32[2,64,512]{2,1,0:T(8,128)} %currents_ref.2, bf16[64,64,512]{2,1,0:T(8,128)(2,1)} %projection_ref.3, s32[2,512]{1,0:T(2,128)} %shifts_ref.3), custom_call_target="tpu_custom_call" | custom-call | tf_op jit(solution)/shard_map/charges/pallas_call | solution.py:1151
  5.4 6.4 %all-to-all-start = ((bf16[8,112,128]{2,1,0:T(8,128)(2,1)}), bf16[8,112,128]{2,1,0:T(8,128)(2,1)S(1)}, u32[]{:S(2)}, u32[]{:S(2)}) async-start(bf16[8,112,128]{2,1,0:T(8,128)(2,1)} %charges.1), calls=%async_computation | async-start | bytes 458752 | tf_op jit(solution)/shard_map/all_to_all | solution.py:1168
  11.7 0.0 copy-start.5
  11.8 1.0 %copy-done.5 = f32[160,512]{1,0:T(8,128)S(1)} copy-done((f32[160,512]{1,0:T(8,128)S(1)}, f32[160,512]{1,0:T(8,128)}, u32[]{:S(2)}) %copy-start.5) | copy-done | bytes 327704
  12.7 0.7 column_tables.1
  13.4 7.3 %all-to-all-done.rows_ref.slab_ref = bf16[8,112,128]{2,1,0:T(8,128)(2,1)S(1)} async-done(((bf16[8,112,128]{2,1,0:T(8,128)(2,1)}), bf16[8,112,128]{2,1,0:T(8,128)(2,1)S(1)}, u32[]{:S(2)}, u32[]{:S(2)}) %all-to-all-start) | async-done | bytes 229408 | tf_op jit(solution)/shard_map/all_to_all | solution.py:1168
  20.8 2.1 %columns.1 = bf16[32,40,128]{2,1,0:T(8,128)(2,1)} custom-call(bf16[8,112,128]{2,1,0:T(8,128)(2,1)S(1)} %all-to-all-done.rows_ref.slab_ref, bf16[512,512]{1,0:T(8,128)(2,1)S(1)} %get-tuple-element.37.even_cos, bf16[512,512]{1,0:T(8,128)(2,1)S(1)} %get-tuple-element.38.even_sin, bf16[512,512]{1,0:T(8,128)(2,1)S(1)} %get-tuple-element.39.odd_cos), custom_call_target="tpu_custom_call" | custom-call | tf_op jit(solution)/shard_map/columns/pallas_call | solution.py:1179
  22.9 3.5 %all-to-all-start.1 = ((bf16[32,40,128]{2,1,0:T(8,128)(2,1)}), bf16[32,40,128]{2,1,0:T(8,128)(2,1)S(1)}, u32[]{:S(2)}, u32[]{:S(2)}) async-start(bf16[32,40,128]{2,1,0:T(8,128)(2,1)} %columns.1), calls=%async_computation.1 | async-start | bytes 655360 | tf_op jit(solution)/shard_map/all_to_all | solution.py:1188
  26.4 0.0 copy-start.2
  26.4 0.9 %copy-done.2 = f32[2,64,512]{2,1,0:T(8,128)S(1)} copy-done((f32[2,64,512]{2,1,0:T(8,128)S(1)}, f32[2,64,512]{2,1,0:T(8,128)}, u32[]{:S(2)}) %copy-start.2) | copy-done | bytes 262168
  27.4 2.8 %near.3.refs_1_ = f32[2,64,512]{2,1,0:T(8,128)S(1)} custom-call(f32[2,64,512]{2,1,0:T(8,128)S(1)} %copy-done.2, bf16[4,64,64,512]{3,2,1,0:T(8,128)(2,1)} %refs_2_.3), custom_call_target="tpu_custom_call" | custom-call | tf_op jit(solution)/shard_map/near/pallas_call | solution.py:1113
  30.2 4.6 %row_tables.1 = (bf16[512,512]{1,0:T(8,128)(2,1)}, bf16[512,512]{1,0:T(8,128)(2,1)}, bf16[512,512]{1,0:T(8,128)(2,1)}, bf16[512,512]{1,0:T(8,128)(2,1)}, bf16[51...) custom-call(f32[64,2048]{1,0:T(8,128)} %green_ref, ...), custom_call_target="tpu_custom_call" | custom-call | tf_op jit(solution)/shard_map/row_tables/pallas_call | solution.py:1191
  34.8 3.7 %all-to-all-done.1.refs_0_.arrived_ref = bf16[32,40,128]{2,1,0:T(8,128)(2,1)S(1)} async-done(((bf16[32,40,128]{2,1,0:T(8,128)(2,1)}), bf16[32,40,128]{2,1,0:T(8,128)(2,1)S(1)}, u32[]{:S(2)}, u32[]{:S(2)}) %all-to-all-start.1) | async-done | bytes 327712 | tf_op jit(solution)/shard_map/all_to_all | solution.py:1188
  38.5 0.0 copy-start
  38.5 0.7 copy-done
  39.2 3.8 %rows.1 = bf16[32,40,128]{2,1,0:T(8,128)(2,1)} custom-call(bf16[32,40,128]{2,1,0:T(8,128)(2,1)} %copy-done, bf16[512,512]{1,0:T(8,128)(2,1)} %get-tuple-element.52.refs_1_, bf16[512,512]{1,0:T(8,128)(2,1)} %get-tuple-element.53.refs_2_, bf16[512,512]{1,0:T(8,128)(2,1)} %get-tuple-element.54.refs_3_, bf16[512,512]{1,0:T(8,128)(2,1)} %get-tuple-element.55.refs_4_, ...), custom_call_target="tpu_custom_call" | custom-call | tf_op jit(solution)/shard_map/rows/pallas_call | solution.py:1198
  43.0 2.6 %all-to-all-start.2 = ((bf16[32,40,128]{2,1,0:T(8,128)(2,1)}), bf16[32,40,128]{2,1,0:T(8,128)(2,1)S(1)}, u32[]{:S(2)}, u32[]{:S(2)}) async-start(bf16[32,40,128]{2,1,0:T(8,128)(2,1)} %rows.1), calls=%async_computation.2 | async-start | bytes 655360 | tf_op jit(solution)/shard_map/all_to_all | solution.py:1211
  45.6 0.0 copy-done.3
  45.6 0.0 copy-done.6
  45.6 0.0 copy-start.1
  45.6 1.0 %copy-done.1 = bf16[32,40,128]{2,1,0:T(8,128)(2,1)S(1)} copy-done((bf16[32,40,128]{2,1,0:T(8,128)(2,1)S(1)}, bf16[32,40,128]{2,1,0:T(8,128)(2,1)}, u32[]{:S(2)}) %copy-start.1) | copy-done | bytes 327704
  46.6 0.9 %pick.1.refs_0_ = bf16[3,2,64,512]{3,2,1,0:T(8,128)(2,1)S(1)} custom-call(f32[2,64,512]{2,1,0:T(8,128)S(1)} %copy-done.3, bf16[8,112,128]{2,1,0:T(8,128)(2,1)S(1)} %all-to-all-done.rows_ref.slab_ref, bf16[32,40,128]{2,1,0:T(8,128)(2,1)S(1)} %copy-done.1, s32[4,512]{1,0:T(4,128)S(1)} %copy-done.6), custom_call_target="tpu_custom_call" | custom-call | tf_op jit(solution)/shard_map/pick/pallas_call | solution.py:1212
  47.5 3.7 %near.4.refs_1_ = f32[2,64,512]{2,1,0:T(8,128)S(1)} custom-call(bf16[3,2,64,512]{3,2,1,0:T(8,128)(2,1)S(1)} %pick.1.refs_0_, f32[2,64,512]{2,1,0:T(8,128)S(1)} %near.3.refs_1_, bf16[4,64,64,512]{3,2,1,0:T(8,128)(2,1)} %refs_2_.3), custom_call_target="tpu_custom_call" | custom-call | tf_op jit(solution)/shard_map/near/pallas_call | solution.py:1113
  51.2 6.4 %all-to-all-done.2.in_ref = bf16[32,40,128]{2,1,0:T(8,128)(2,1)S(1)} async-done(((bf16[32,40,128]{2,1,0:T(8,128)(2,1)}), bf16[32,40,128]{2,1,0:T(8,128)(2,1)S(1)}, u32[]{:S(2)}, u32[]{:S(2)}) %all-to-all-start.2) | async-done | bytes 327712 | tf_op jit(solution)/shard_map/all_to_all | solution.py:1211
  57.6 1.6 %grid.1 = bf16[8,80,128]{2,1,0:T(8,128)(2,1)} custom-call(bf16[32,40,128]{2,1,0:T(8,128)(2,1)S(1)} %all-to-all-done.2.in_ref, bf16[512,512]{1,0:T(8,128)(2,1)S(1)} %get-tuple-element.37.even_cos, bf16[512,512]{1,0:T(8,128)(2,1)S(1)} %get-tuple-element.38.even_sin, bf16[512,512]{1,0:T(8,128)(2,1)S(1)} %get-tuple-element.39.odd_cos), custom_call_target="tpu_custom_call" | custom-call | tf_op jit(solution)/shard_map/grid/pallas_call | solution.py:1223
  59.3 3.4 %all-to-all-start.3 = ((bf16[8,80,128]{2,1,0:T(8,128)(2,1)}), bf16[8,80,128]{2,1,0:T(8,128)(2,1)S(1)}, u32[]{:S(2)}, u32[]{:S(2)}) async-start(bf16[8,80,128]{2,1,0:T(8,128)(2,1)} %grid.1), calls=%async_computation.3 | async-start | bytes 327680 | tf_op jit(solution)/shard_map/all_to_all | solution.py:1232
  62.6 3.7 %near.5.near_ref = f32[2,64,512]{2,1,0:T(8,128)S(1)} custom-call(bf16[3,2,64,512]{3,2,1,0:T(8,128)(2,1)S(1)} %pick.1.refs_0_, f32[2,64,512]{2,1,0:T(8,128)S(1)} %near.4.refs_1_, bf16[4,64,64,512]{3,2,1,0:T(8,128)(2,1)} %refs_2_.3), custom_call_target="tpu_custom_call" | custom-call | tf_op jit(solution)/shard_map/near/pallas_call | solution.py:1113
  66.3 0.0 copy-start.4
  66.3 0.7 copy-done.4
  67.0 2.8 %all-to-all-done.3.source_ref = bf16[8,80,128]{2,1,0:T(8,128)(2,1)S(1)} async-done(((bf16[8,80,128]{2,1,0:T(8,128)(2,1)}), bf16[8,80,128]{2,1,0:T(8,128)(2,1)S(1)}, u32[]{:S(2)}, u32[]{:S(2)}) %all-to-all-start.3) | async-done | bytes 163872 | tf_op jit(solution)/shard_map/all_to_all | solution.py:1232
  69.8 0.0 copy-start.7
  69.8 0.7 copy-done.7
  70.4 4.4 %far.1 = f32[2,64,512]{2,1,0:T(8,128)} custom-call(bf16[8,80,128]{2,1,0:T(8,128)(2,1)} %copy-done.7, bf16[64,64,512]{2,1,0:T(8,128)(2,1)} %projection_ref.3, s32[2,512]{1,0:T(2,128)} %shifts_ref.3, f32[2,64,512]{2,1,0:T(8,128)} %copy-done.4), custom_call_target="tpu_custom_call" | custom-call | tf_op jit(solution)/shard_map/far/pallas_call | solution.py:1235
Async XLA Ops:
  0.0 45.6 %copy-start.3 = (f32[2,64,512]{2,1,0:T(8,128)S(1)}, f32[2,64,512]{2,1,0:T(8,128)}, u32[]{:S(2)}) copy-start(f32[2,64,512]{2,1,0:T(8,128)} %currents_ref.2) | copy-start | bytes 786436
  0.0 45.6 %copy-start.6 = (s32[4,512]{1,0:T(4,128)S(1)}, s32[4,512]{1,0:T(4,128)}, u32[]{:S(2)}) copy-start(s32[4,512]{1,0:T(4,128)} %partners_ref.1) | copy-start | bytes 24580
  5.4 15.4 %all-to-all-start = ((bf16[8,112,128]{2,1,0:T(8,128)(2,1)}), bf16[8,112,128]{2,1,0:T(8,128)(2,1)S(1)}, u32[]{:S(2)}, u32[]{:S(2)}) async-start(bf16[8,112,128]{2,1,0:T(8,128)(2,1)} %charges.1), calls=%async_computation | async-start | bytes 458752 | tf_op jit(solution)/shard_map/all_to_all | solution.py:1168
  11.7 1.0 %copy-start.5 = (f32[160,512]{1,0:T(8,128)S(1)}, f32[160,512]{1,0:T(8,128)}, u32[]{:S(2)}) copy-start(f32[160,512]{1,0:T(8,128)} %constant.6.clone.bases_ref) | copy-start | bytes 983044
  22.9 15.6 %all-to-all-start.1 = ((bf16[32,40,128]{2,1,0:T(8,128)(2,1)}), bf16[32,40,128]{2,1,0:T(8,128)(2,1)S(1)}, u32[]{:S(2)}, u32[]{:S(2)}) async-start(bf16[32,40,128]{2,1,0:T(8,128)(2,1)} %columns.1), calls=%async_computation.1 | async-start | bytes 655360 | tf_op jit(solution)/shard_map/all_to_all | solution.py:1188
  26.4 1.0 %copy-start.2 = (f32[2,64,512]{2,1,0:T(8,128)S(1)}, f32[2,64,512]{2,1,0:T(8,128)}, u32[]{:S(2)}) copy-start(f32[2,64,512]{2,1,0:T(8,128)} %currents_ref.2) | copy-start | bytes 786436
  38.5 0.7 copy-start
  43.0 14.6 %all-to-all-start.2 = ((bf16[32,40,128]{2,1,0:T(8,128)(2,1)}), bf16[32,40,128]{2,1,0:T(8,128)(2,1)S(1)}, u32[]{:S(2)}, u32[]{:S(2)}) async-start(bf16[32,40,128]{2,1,0:T(8,128)(2,1)} %rows.1), calls=%async_computation.2 | async-start | bytes 655360 | tf_op jit(solution)/shard_map/all_to_all | solution.py:1211
  45.6 1.0 %copy-start.1 = (bf16[32,40,128]{2,1,0:T(8,128)(2,1)S(1)}, bf16[32,40,128]{2,1,0:T(8,128)(2,1)}, u32[]{:S(2)}) copy-start(bf16[32,40,128]{2,1,0:T(8,128)(2,1)} %copy-done) | copy-start | bytes 983044
  59.3 10.5 %all-to-all-start.3 = ((bf16[8,80,128]{2,1,0:T(8,128)(2,1)}), bf16[8,80,128]{2,1,0:T(8,128)(2,1)S(1)}, u32[]{:S(2)}, u32[]{:S(2)}) async-start(bf16[8,80,128]{2,1,0:T(8,128)(2,1)} %grid.1), calls=%async_computation.3 | async-start | bytes 327680 | tf_op jit(solution)/shard_map/all_to_all | solution.py:1232
  66.3 0.7 copy-start.4
  69.8 0.7 copy-start.7

commit v5 on v4

--- a/solution.py
+++ b/solution.py
@@ -1129,7 +1129,7 @@
 IN_PLACE = pl.BlockSpec(memory_space=pltpu.HBM)
 PARAMS = pltpu.CompilerParams(vmem_limit_bytes=48 << 20)
 CHARGE_PARAMS = pltpu.CompilerParams(vmem_limit_bytes=60 << 20)
-FULL_PARAMS = pltpu.CompilerParams(vmem_limit_bytes=60 << 20)
+FULL_PARAMS = pltpu.CompilerParams(vmem_limit_bytes=53 << 20)
 NEAR_PARAMS = pltpu.CompilerParams(vmem_limit_bytes=48 << 20)
 
 
@@ -1198,7 +1198,7 @@
     rows_back = pl.pallas_call(
         functools.partial(row_kernel, row_count, col_count),
         out_shape=struct((devices, 40, LANES), b16),
-        in_specs=[IN_PLACE] * 9,
+        in_specs=[ON_CHIP] + [IN_PLACE] * 8,
         out_specs=ON_CHIP,
         scratch_shapes=[pltpu.VMEM((devices, 40, LANES), b16)]
         + [pltpu.VMEM((quarter, quarter), b16)] * 6
@@ -1234,7 +1234,7 @@
 
     return pl.pallas_call(
         far_kernel,
-        in_specs=[IN_PLACE] * 4,
+        in_specs=[ON_CHIP, IN_PLACE, IN_PLACE, ON_CHIP],
         out_specs=IN_PLACE,
         out_shape=struct((RHS, BASIS, elements), f32),
         scratch_shapes=[

time: 75.4 us -> 73.4 us (0.973)
  local copies, waits for them, and re-layouts: 4.97 us -> 2.74 us
  waiting for transfers between devices: 20.2 us -> 21.3 us
  Pallas kernels: 33.6 us -> 32.7 us
    unnamed x16 -> x14, local copies, waits for them, and re-layouts: 4.97 us -> 2.74 us
    all_to_all x1, waiting for transfers between devices: 6.44 us -> 7.4 us  [shards_real(): returned = lax.all_to_all(rows_back, ('row', 'col'), 0, 0, tiled=True)]
where the time goes in v5:
time: 73.4 us; the launch traced here: 72.9 us
  Pallas kernels  32.7 us (45%)
  waiting for transfers between devices  21.3 us (29%)
  starting transfers between devices  16 us (22%)
  local copies, waits for them, and re-layouts  2.74 us (4%)
    pallas_call x3, Pallas kernels, near_call(): pl.pallas_call(functools.partial(near_kernel, total is not None, slots, s...  10.1 us
    all_to_all x1, waiting for transfers between devices, shards_real(): returned = lax.all_to_all(rows_back, ('row', 'col'), 0, 0, tiled=True)  7.4 us
    all_to_all x1, waiting for transfers between devices, shards_real(): slab = lax.all_to_all(charges, 'col', 0, 0, tiled=True)  7.31 us
    all_to_all x1, starting transfers between devices, shards_real(): slab = lax.all_to_all(charges, 'col', 0, 0, tiled=True)  6.37 us
    pallas_call x1, Pallas kernels, shards_real(): pl.pallas_call(charge_kernel, in_specs=[IN_PLACE] * 3, out_specs=ON_CHIP,...  5.39 us
    pallas_call x1, Pallas kernels, shards_real(): pl.pallas_call(row_table_kernel, out_shape=[table] * 6 + [spread] * 2, co...  4.33 us
    pallas_call x1, Pallas kernels, shards_real(): pl.pallas_call(functools.partial(row_kernel, row_count, col_count), out_s...  3.82 us
    pallas_call x1, Pallas kernels, shards_real(): pl.pallas_call(far_kernel, in_specs=[ON_CHIP, IN_PLACE, IN_PLACE, ON_CHIP...  3.69 us
  transfers between devices with their start and end apart: 4, of which 4 were waited for; matrix products, arithmetic and copies ran while one was open for 0% of the time, Pallas kernels for 22%

profile of v5, /device:TPU:0, one launch (start us, length us, event | category | flops | bytes accessed | tf_op | source)
XLA Modules:
  0.0 72.9 jit_solution(14881123366148746006)
XLA Ops:
  0.0 0.0 copy-start.4
  0.0 0.0 copy-start.1
  0.0 0.0 copy-start.6
  0.0 5.4 %charges.1 = bf16[8,112,128]{2,1,0:T(8,128)(2,1)} custom-call(f32[2,64,512]{2,1,0:T(8,128)} %currents_ref.2, bf16[64,64,512]{2,1,0:T(8,128)(2,1)} %projection_ref.3, s32[2,512]{1,0:T(2,128)} %shifts_ref.3), custom_call_target="tpu_custom_call" | custom-call | tf_op jit(solution)/shard_map/charges/pallas_call | solution.py:1151
  5.4 6.4 %all-to-all-start = ((bf16[8,112,128]{2,1,0:T(8,128)(2,1)}), bf16[8,112,128]{2,1,0:T(8,128)(2,1)S(1)}, u32[]{:S(2)}, u32[]{:S(2)}) async-start(bf16[8,112,128]{2,1,0:T(8,128)(2,1)} %charges.1), calls=%async_computation | async-start | bytes 458752 | tf_op jit(solution)/shard_map/all_to_all | solution.py:1168
  11.8 0.0 copy-start.3
  11.8 1.0 %copy-done.3 = f32[160,512]{1,0:T(8,128)S(1)} copy-done((f32[160,512]{1,0:T(8,128)S(1)}, f32[160,512]{1,0:T(8,128)}, u32[]{:S(2)}) %copy-start.3) | copy-done | bytes 327704
  12.7 0.7 column_tables.1
  13.5 7.3 %all-to-all-done.rows_ref.slab_ref = bf16[8,112,128]{2,1,0:T(8,128)(2,1)S(1)} async-done(((bf16[8,112,128]{2,1,0:T(8,128)(2,1)}), bf16[8,112,128]{2,1,0:T(8,128)(2,1)S(1)}, u32[]{:S(2)}, u32[]{:S(2)}) %all-to-all-start) | async-done | bytes 229408 | tf_op jit(solution)/shard_map/all_to_all | solution.py:1168
  20.8 2.1 %columns.1 = bf16[32,40,128]{2,1,0:T(8,128)(2,1)} custom-call(bf16[8,112,128]{2,1,0:T(8,128)(2,1)S(1)} %all-to-all-done.rows_ref.slab_ref, bf16[512,512]{1,0:T(8,128)(2,1)S(1)} %get-tuple-element.37.even_cos, bf16[512,512]{1,0:T(8,128)(2,1)S(1)} %get-tuple-element.38.even_sin, bf16[512,512]{1,0:T(8,128)(2,1)S(1)} %get-tuple-element.39.odd_cos), custom_call_target="tpu_custom_call" | custom-call | tf_op jit(solution)/shard_map/columns/pallas_call | solution.py:1179
  22.9 3.5 %all-to-all-start.1 = ((bf16[32,40,128]{2,1,0:T(8,128)(2,1)}), bf16[32,40,128]{2,1,0:T(8,128)(2,1)S(1)}, u32[]{:S(2)}, u32[]{:S(2)}) async-start(bf16[32,40,128]{2,1,0:T(8,128)(2,1)} %columns.1), calls=%async_computation.1 | async-start | bytes 655360 | tf_op jit(solution)/shard_map/all_to_all | solution.py:1188
  26.5 0.0 copy-start
  26.5 0.9 %copy-done = f32[2,64,512]{2,1,0:T(8,128)S(1)} copy-done((f32[2,64,512]{2,1,0:T(8,128)S(1)}, f32[2,64,512]{2,1,0:T(8,128)}, u32[]{:S(2)}) %copy-start) | copy-done | bytes 262168
  27.4 2.8 %near.3.refs_1_ = f32[2,64,512]{2,1,0:T(8,128)S(1)} custom-call(f32[2,64,512]{2,1,0:T(8,128)S(1)} %copy-done, bf16[4,64,64,512]{3,2,1,0:T(8,128)(2,1)} %refs_2_.3), custom_call_target="tpu_custom_call" | custom-call | tf_op jit(solution)/shard_map/near/pallas_call | solution.py:1113
  30.2 0.0 copy-done.4
  30.2 4.3 %row_tables.1 = (bf16[512,512]{1,0:T(8,128)(2,1)S(1)}, bf16[512,512]{1,0:T(8,128)(2,1)}, bf16[512,512]{1,0:T(8,128)(2,1)}, bf16[512,512]{1,0:T(8,128)(2,1)}, bf1...) custom-call(f32[64,2048]{1,0:T(8,128)} %green_ref, ...), custom_call_target="tpu_custom_call" | custom-call | tf_op jit(solution)/shard_map/row_tables/pallas_call | solution.py:1191
  34.5 0.0 copy-start.2
  34.5 0.8 %copy-done.2 = bf16[512,512]{1,0:T(8,128)(2,1)} copy-done((bf16[512,512]{1,0:T(8,128)(2,1)}, bf16[512,512]{1,0:T(8,128)(2,1)S(1)}, u32[]{:S(2)}) %copy-start.2) | copy-done | bytes 524312
  35.4 3.1 %all-to-all-done.1.refs_0_.arrived_ref = bf16[32,40,128]{2,1,0:T(8,128)(2,1)S(1)} async-done(((bf16[32,40,128]{2,1,0:T(8,128)(2,1)}), bf16[32,40,128]{2,1,0:T(8,128)(2,1)S(1)}, u32[]{:S(2)}, u32[]{:S(2)}) %all-to-all-start.1) | async-done | bytes 327712 | tf_op jit(solution)/shard_map/all_to_all | solution.py:1188
  38.5 3.8 %rows.1 = bf16[32,40,128]{2,1,0:T(8,128)(2,1)} custom-call(bf16[32,40,128]{2,1,0:T(8,128)(2,1)S(1)} %all-to-all-done.1.refs_0_.arrived_ref, bf16[512,512]{1,0:T(8,128)(2,1)} %copy-done.2, bf16[512,512]{1,0:T(8,128)(2,1)} %get-tuple-element.53.refs_2_, bf16[512,512]{1,0:T(8,128)(2,1)} %get-tuple-element.54.refs_3_, ...), custom_call_target="tpu_custom_call" | custom-call | tf_op jit(solution)/shard_map/rows/pallas_call | solution.py:1198
  42.3 2.7 %all-to-all-start.2 = ((bf16[32,40,128]{2,1,0:T(8,128)(2,1)}), bf16[32,40,128]{2,1,0:T(8,128)(2,1)S(1)}, u32[]{:S(2)}, u32[]{:S(2)}) async-start(bf16[32,40,128]{2,1,0:T(8,128)(2,1)} %rows.1), calls=%async_computation.2 | async-start | bytes 655360 | tf_op jit(solution)/shard_map/all_to_all | solution.py:1211
  45.0 0.0 copy-done.1
  45.0 0.0 copy-done.6
  45.0 0.9 %pick.1.refs_0_ = bf16[3,2,64,512]{3,2,1,0:T(8,128)(2,1)S(1)} custom-call(f32[2,64,512]{2,1,0:T(8,128)S(1)} %copy-done.1, bf16[8,112,128]{2,1,0:T(8,128)(2,1)S(1)} %all-to-all-done.rows_ref.slab_ref, bf16[32,40,128]{2,1,0:T(8,128)(2,1)S(1)} %all-to-all-done.1.refs_0_.arrived_ref, s32[4,512]{1,0:T(4,128)S(1)} %copy-done.6), custom_call_target="tpu_custom_call" | custom-call | tf_op jit(solution)/shard_map/pick/pallas_call | solution.py:1212
  46.0 0.0 copy-start.5
  46.0 3.7 %near.4.refs_1_ = f32[2,64,512]{2,1,0:T(8,128)S(1)} custom-call(bf16[3,2,64,512]{3,2,1,0:T(8,128)(2,1)S(1)} %pick.1.refs_0_, f32[2,64,512]{2,1,0:T(8,128)S(1)} %near.3.refs_1_, bf16[4,64,64,512]{3,2,1,0:T(8,128)(2,1)} %refs_2_.3), custom_call_target="tpu_custom_call" | custom-call | tf_op jit(solution)/shard_map/near/pallas_call | solution.py:1113
  49.7 7.4 %all-to-all-done.2.in_ref = bf16[32,40,128]{2,1,0:T(8,128)(2,1)S(1)} async-done(((bf16[32,40,128]{2,1,0:T(8,128)(2,1)}), bf16[32,40,128]{2,1,0:T(8,128)(2,1)S(1)}, u32[]{:S(2)}, u32[]{:S(2)}) %all-to-all-start.2) | async-done | bytes 327712 | tf_op jit(solution)/shard_map/all_to_all | solution.py:1211
  57.1 1.6 %grid.1 = bf16[8,80,128]{2,1,0:T(8,128)(2,1)} custom-call(bf16[32,40,128]{2,1,0:T(8,128)(2,1)S(1)} %all-to-all-done.2.in_ref, bf16[512,512]{1,0:T(8,128)(2,1)S(1)} %get-tuple-element.37.even_cos, bf16[512,512]{1,0:T(8,128)(2,1)S(1)} %get-tuple-element.38.even_sin, bf16[512,512]{1,0:T(8,128)(2,1)S(1)} %get-tuple-element.39.odd_cos), custom_call_target="tpu_custom_call" | custom-call | tf_op jit(solution)/shard_map/grid/pallas_call | solution.py:1223
  58.7 3.4 %all-to-all-start.3 = ((bf16[8,80,128]{2,1,0:T(8,128)(2,1)}), bf16[8,80,128]{2,1,0:T(8,128)(2,1)S(1)}, u32[]{:S(2)}, u32[]{:S(2)}) async-start(bf16[8,80,128]{2,1,0:T(8,128)(2,1)} %grid.1), calls=%async_computation.3 | async-start | bytes 327680 | tf_op jit(solution)/shard_map/all_to_all | solution.py:1232
  62.1 3.7 %near.5.near_ref = f32[2,64,512]{2,1,0:T(8,128)S(1)} custom-call(bf16[3,2,64,512]{3,2,1,0:T(8,128)(2,1)S(1)} %pick.1.refs_0_, f32[2,64,512]{2,1,0:T(8,128)S(1)} %near.4.refs_1_, bf16[4,64,64,512]{3,2,1,0:T(8,128)(2,1)} %refs_2_.3), custom_call_target="tpu_custom_call" | custom-call | tf_op jit(solution)/shard_map/near/pallas_call | solution.py:1113
  65.7 3.5 %all-to-all-done.3.source_ref = bf16[8,80,128]{2,1,0:T(8,128)(2,1)S(1)} async-done(((bf16[8,80,128]{2,1,0:T(8,128)(2,1)}), bf16[8,80,128]{2,1,0:T(8,128)(2,1)S(1)}, u32[]{:S(2)}, u32[]{:S(2)}) %all-to-all-start.3) | async-done | bytes 163872 | tf_op jit(solution)/shard_map/all_to_all | solution.py:1232
  69.2 0.0 copy-done.5
  69.2 3.7 %far.1 = f32[2,64,512]{2,1,0:T(8,128)} custom-call(bf16[8,80,128]{2,1,0:T(8,128)(2,1)S(1)} %all-to-all-done.3.source_ref, bf16[64,64,512]{2,1,0:T(8,128)(2,1)} %projection_ref.3, s32[2,512]{1,0:T(2,128)S(1)} %copy-done.5, f32[2,64,512]{2,1,0:T(8,128)S(1)} %near.5.near_ref), custom_call_target="tpu_custom_call" | custom-call | tf_op jit(solution)/shard_map/far/pallas_call | solution.py:1235
Async XLA Ops:
  0.0 30.2 %copy-start.4 = (f32[160,512]{1,0:T(8,128)S(1)}, f32[160,512]{1,0:T(8,128)}, u32[]{:S(2)}) copy-start(f32[160,512]{1,0:T(8,128)} %constant.7.clone.position_ref) | copy-start | bytes 983044
  0.0 45.0 %copy-start.1 = (f32[2,64,512]{2,1,0:T(8,128)S(1)}, f32[2,64,512]{2,1,0:T(8,128)}, u32[]{:S(2)}) copy-start(f32[2,64,512]{2,1,0:T(8,128)} %currents_ref.2) | copy-start | bytes 786436
  0.0 45.0 %copy-start.6 = (s32[4,512]{1,0:T(4,128)S(1)}, s32[4,512]{1,0:T(4,128)}, u32[]{:S(2)}) copy-start(s32[4,512]{1,0:T(4,128)} %partners_ref.1) | copy-start | bytes 24580
  5.4 15.4 %all-to-all-start = ((bf16[8,112,128]{2,1,0:T(8,128)(2,1)}), bf16[8,112,128]{2,1,0:T(8,128)(2,1)S(1)}, u32[]{:S(2)}, u32[]{:S(2)}) async-start(bf16[8,112,128]{2,1,0:T(8,128)(2,1)} %charges.1), calls=%async_computation | async-start | bytes 458752 | tf_op jit(solution)/shard_map/all_to_all | solution.py:1168
  11.8 1.0 %copy-start.3 = (f32[160,512]{1,0:T(8,128)S(1)}, f32[160,512]{1,0:T(8,128)}, u32[]{:S(2)}) copy-start(f32[160,512]{1,0:T(8,128)} %constant.6.clone.bases_ref) | copy-start | bytes 983044
  22.9 15.6 %all-to-all-start.1 = ((bf16[32,40,128]{2,1,0:T(8,128)(2,1)}), bf16[32,40,128]{2,1,0:T(8,128)(2,1)S(1)}, u32[]{:S(2)}, u32[]{:S(2)}) async-start(bf16[32,40,128]{2,1,0:T(8,128)(2,1)} %columns.1), calls=%async_computation.1 | async-start | bytes 655360 | tf_op jit(solution)/shard_map/all_to_all | solution.py:1188
  26.5 1.0 %copy-start = (f32[2,64,512]{2,1,0:T(8,128)S(1)}, f32[2,64,512]{2,1,0:T(8,128)}, u32[]{:S(2)}) copy-start(f32[2,64,512]{2,1,0:T(8,128)} %currents_ref.2) | copy-start | bytes 786436
  34.5 0.8 %copy-start.2 = (bf16[512,512]{1,0:T(8,128)(2,1)}, bf16[512,512]{1,0:T(8,128)(2,1)S(1)}, u32[]{:S(2)}) copy-start(bf16[512,512]{1,0:T(8,128)(2,1)S(1)} %get-tuple-element.52.refs_1_) | copy-start | bytes 1572868
  42.3 14.7 %all-to-all-start.2 = ((bf16[32,40,128]{2,1,0:T(8,128)(2,1)}), bf16[32,40,128]{2,1,0:T(8,128)(2,1)S(1)}, u32[]{:S(2)}, u32[]{:S(2)}) async-start(bf16[32,40,128]{2,1,0:T(8,128)(2,1)} %rows.1), calls=%async_computation.2 | async-start | bytes 655360 | tf_op jit(solution)/shard_map/all_to_all | solution.py:1211
  46.0 23.2 %copy-start.5 = (s32[2,512]{1,0:T(2,128)S(1)}, s32[2,512]{1,0:T(2,128)}, u32[]{:S(2)}) copy-start(s32[2,512]{1,0:T(2,128)} %shifts_ref.3) | copy-start | bytes 12292
  58.7 10.5 %all-to-all-start.3 = ((bf16[8,80,128]{2,1,0:T(8,128)(2,1)}), bf16[8,80,128]{2,1,0:T(8,128)(2,1)S(1)}, u32[]{:S(2)}, u32[]{:S(2)}) async-start(bf16[8,80,128]{2,1,0:T(8,128)(2,1)} %grid.1), calls=%async_computation.3 | async-start | bytes 327680 | tf_op jit(solution)/shard_map/all_to_all | solution.py:1232

commit v6 on v5

--- a/solution.py
+++ b/solution.py
@@ -697,7 +697,7 @@
 
 
 def charge_kernel(
-    currents_ref, projection_ref, shifts_ref, out_ref, weights, raw, shifts, current, partial, stencil, sems
+    currents_ref, projection_ref, shifts_ref, out_ref, weights, raw, shifts, current, half, stencil, sems
 ):
     copies = [
         pltpu.make_async_copy(currents_ref, raw, sems.at[STEN]),
@@ -713,28 +713,31 @@
         weight_copy(step).start()
     copies[1].start()
     copies[0].wait()
-    current[...] = raw[...].astype(jnp.bfloat16).astype(jnp.float32)
+    half[...] = raw[...].astype(jnp.bfloat16)
+    current[...] = half[...].astype(jnp.float32)
+    groups = lane_index((SUB, SUB * BASIS)) // BASIS
+    adder = jnp.where(groups == sub_index(groups.shape), 1.0, 0.0).astype(jnp.bfloat16)
 
     def one_row(step, carry):
         weight_copy(step).wait()
-        for t in range(TILES):
-            lanes = slice(LANES * t, LANES * (t + 1))
-            totals = [[None] * RHS for _ in range(STEN)]
-            for b in range(0, BASIS, 16):
-                values = [
-                    [current[q, b + 8 * h : b + 8 * h + 8, lanes] for h in range(2)]
-                    for q in range(RHS)
-                ]
-                for s in range(STEN):
-                    weight = weights[step * STEN + s, b : b + 16, lanes].astype(jnp.float32)
-                    for q in range(RHS):
-                        term = weight[:8] * values[q][0] + weight[8:] * values[q][1]
-                        totals[s][q] = term if totals[s][q] is None else totals[s][q] + term
-            for s in range(STEN):
-                for q in range(RHS):
-                    partial[s, q * TILES + t] = totals[s][q]
-        for s in range(STEN):
-            stencil[step * STEN + s] = sum_rows([partial[s, i] for i in range(SUB)])
+        for s in range(0, STEN, 2):
+            columns = []
+            for h in range(2):
+                weight = weights[step * STEN + s + h]
+                products = [weight * half[q] for q in range(RHS)]
+                columns.append(
+                    jnp.concatenate(
+                        [
+                            products[q][:, LANES * t : LANES * (t + 1)]
+                            for q in range(RHS)
+                            for t in range(TILES)
+                        ],
+                        axis=0,
+                    )
+                )
+            sums = dot(adder, jnp.concatenate(columns, axis=1))
+            stencil[step * STEN + s] = sums[:, :LANES]
+            stencil[step * STEN + s + 1] = sums[:, LANES:]
         return carry
 
     lax.fori_loop(0, STEN, one_row, 0)
@@ -1158,7 +1161,7 @@
             pltpu.VMEM((RHS, BASIS, elements), f32),
             pltpu.VMEM((2, elements), jnp.int32),
             pltpu.VMEM((RHS, BASIS, elements), f32),
-            pltpu.VMEM((STEN, SUB, SUB, LANES), f32),
+            pltpu.VMEM((RHS, BASIS, elements), b16),
             pltpu.VMEM((STEN * STEN, SUB, LANES), f32),
             pltpu.SemaphoreType.DMA((STEN + 2,)),
         ],

time: 73.4 us -> 73.8 us (level)
  no operation moved by 1% of the time
where the time goes in v6:
time: 73.8 us; the launch traced here: 73.2 us
  Pallas kernels  33.1 us (45%)
  waiting for transfers between devices  21.3 us (29%)
  starting transfers between devices  16 us (22%)
  local copies, waits for them, and re-layouts  2.74 us (4%)
    pallas_call x3, Pallas kernels, near_call(): pl.pallas_call(functools.partial(near_kernel, total is not None, slots, s...  10.1 us
    all_to_all x1, waiting for transfers between devices, shards_real(): returned = lax.all_to_all(rows_back, ('row', 'col'), 0, 0, tiled=True)  7.4 us
    all_to_all x1, waiting for transfers between devices, shards_real(): slab = lax.all_to_all(charges, 'col', 0, 0, tiled=True)  7.31 us
    all_to_all x1, starting transfers between devices, shards_real(): slab = lax.all_to_all(charges, 'col', 0, 0, tiled=True)  6.37 us
    pallas_call x1, Pallas kernels, shards_real(): pl.pallas_call(charge_kernel, in_specs=[IN_PLACE] * 3, out_specs=ON_CHIP,...  5.74 us
    pallas_call x1, Pallas kernels, shards_real(): pl.pallas_call(row_table_kernel, out_shape=[table] * 6 + [spread] * 2, co...  4.33 us
    pallas_call x1, Pallas kernels, shards_real(): pl.pallas_call(functools.partial(row_kernel, row_count, col_count), out_s...  3.81 us
    pallas_call x1, Pallas kernels, shards_real(): pl.pallas_call(far_kernel, in_specs=[ON_CHIP, IN_PLACE, IN_PLACE, ON_CHIP...  3.69 us
  transfers between devices with their start and end apart: 4, of which 4 were waited for; matrix products, arithmetic and copies ran while one was open for 0% of the time, Pallas kernels for 22%

profile of v6, /device:TPU:0, one launch (start us, length us, event | category | flops | bytes accessed | tf_op | source)
XLA Modules:
  0.0 73.2 jit_solution(15629341325751002818)
XLA Ops:
  0.0 0.0 copy-start.4
  0.0 0.0 copy-start.1
  0.0 0.0 copy-start.6
  0.0 5.7 %charges.1 = bf16[8,112,128]{2,1,0:T(8,128)(2,1)} custom-call(f32[2,64,512]{2,1,0:T(8,128)} %currents_ref.2, bf16[64,64,512]{2,1,0:T(8,128)(2,1)} %projection_ref.3, s32[2,512]{1,0:T(2,128)} %shifts_ref.3), custom_call_target="tpu_custom_call" | custom-call | tf_op jit(solution)/shard_map/charges/pallas_call | solution.py:1154
  5.8 6.4 %all-to-all-start = ((bf16[8,112,128]{2,1,0:T(8,128)(2,1)}), bf16[8,112,128]{2,1,0:T(8,128)(2,1)S(1)}, u32[]{:S(2)}, u32[]{:S(2)}) async-start(bf16[8,112,128]{2,1,0:T(8,128)(2,1)} %charges.1), calls=%async_computation | async-start | bytes 458752 | tf_op jit(solution)/shard_map/all_to_all | solution.py:1171
  12.1 0.0 copy-start.3
  12.1 1.0 %copy-done.3 = f32[160,512]{1,0:T(8,128)S(1)} copy-done((f32[160,512]{1,0:T(8,128)S(1)}, f32[160,512]{1,0:T(8,128)}, u32[]{:S(2)}) %copy-start.3) | copy-done | bytes 327704
  13.1 0.7 column_tables.1
  13.8 7.3 %all-to-all-done.rows_ref.slab_ref = bf16[8,112,128]{2,1,0:T(8,128)(2,1)S(1)} async-done(((bf16[8,112,128]{2,1,0:T(8,128)(2,1)}), bf16[8,112,128]{2,1,0:T(8,128)(2,1)S(1)}, u32[]{:S(2)}, u32[]{:S(2)}) %all-to-all-start) | async-done | bytes 229408 | tf_op jit(solution)/shard_map/all_to_all | solution.py:1171
  21.1 2.1 %columns.1 = bf16[32,40,128]{2,1,0:T(8,128)(2,1)} custom-call(bf16[8,112,128]{2,1,0:T(8,128)(2,1)S(1)} %all-to-all-done.rows_ref.slab_ref, bf16[512,512]{1,0:T(8,128)(2,1)S(1)} %get-tuple-element.37.even_cos, bf16[512,512]{1,0:T(8,128)(2,1)S(1)} %get-tuple-element.38.even_sin, bf16[512,512]{1,0:T(8,128)(2,1)S(1)} %get-tuple-element.39.odd_cos), custom_call_target="tpu_custom_call" | custom-call | tf_op jit(solution)/shard_map/columns/pallas_call | solution.py:1182
  23.3 3.5 %all-to-all-start.1 = ((bf16[32,40,128]{2,1,0:T(8,128)(2,1)}), bf16[32,40,128]{2,1,0:T(8,128)(2,1)S(1)}, u32[]{:S(2)}, u32[]{:S(2)}) async-start(bf16[32,40,128]{2,1,0:T(8,128)(2,1)} %columns.1), calls=%async_computation.1 | async-start | bytes 655360 | tf_op jit(solution)/shard_map/all_to_all | solution.py:1191
  26.8 0.0 copy-start
  26.8 0.9 %copy-done = f32[2,64,512]{2,1,0:T(8,128)S(1)} copy-done((f32[2,64,512]{2,1,0:T(8,128)S(1)}, f32[2,64,512]{2,1,0:T(8,128)}, u32[]{:S(2)}) %copy-start) | copy-done | bytes 262168
  27.8 2.8 %near.3.refs_1_ = f32[2,64,512]{2,1,0:T(8,128)S(1)} custom-call(f32[2,64,512]{2,1,0:T(8,128)S(1)} %copy-done, bf16[4,64,64,512]{3,2,1,0:T(8,128)(2,1)} %refs_2_.3), custom_call_target="tpu_custom_call" | custom-call | tf_op jit(solution)/shard_map/near/pallas_call | solution.py:1116
  30.6 0.0 copy-done.4
  30.6 4.3 %row_tables.1 = (bf16[512,512]{1,0:T(8,128)(2,1)S(1)}, bf16[512,512]{1,0:T(8,128)(2,1)}, bf16[512,512]{1,0:T(8,128)(2,1)}, bf16[512,512]{1,0:T(8,128)(2,1)}, bf1...) custom-call(f32[64,2048]{1,0:T(8,128)} %green_ref, ...), custom_call_target="tpu_custom_call" | custom-call | tf_op jit(solution)/shard_map/row_tables/pallas_call | solution.py:1194
  34.9 0.0 copy-start.2
  34.9 0.8 %copy-done.2 = bf16[512,512]{1,0:T(8,128)(2,1)} copy-done((bf16[512,512]{1,0:T(8,128)(2,1)}, bf16[512,512]{1,0:T(8,128)(2,1)S(1)}, u32[]{:S(2)}) %copy-start.2) | copy-done | bytes 524312
  35.7 3.1 %all-to-all-done.1.refs_0_.arrived_ref = bf16[32,40,128]{2,1,0:T(8,128)(2,1)S(1)} async-done(((bf16[32,40,128]{2,1,0:T(8,128)(2,1)}), bf16[32,40,128]{2,1,0:T(8,128)(2,1)S(1)}, u32[]{:S(2)}, u32[]{:S(2)}) %all-to-all-start.1) | async-done | bytes 327712 | tf_op jit(solution)/shard_map/all_to_all | solution.py:1191
  38.8 3.8 %rows.1 = bf16[32,40,128]{2,1,0:T(8,128)(2,1)} custom-call(bf16[32,40,128]{2,1,0:T(8,128)(2,1)S(1)} %all-to-all-done.1.refs_0_.arrived_ref, bf16[512,512]{1,0:T(8,128)(2,1)} %copy-done.2, bf16[512,512]{1,0:T(8,128)(2,1)} %get-tuple-element.53.refs_2_, bf16[512,512]{1,0:T(8,128)(2,1)} %get-tuple-element.54.refs_3_, ...), custom_call_target="tpu_custom_call" | custom-call | tf_op jit(solution)/shard_map/rows/pallas_call | solution.py:1201
  42.7 2.7 %all-to-all-start.2 = ((bf16[32,40,128]{2,1,0:T(8,128)(2,1)}), bf16[32,40,128]{2,1,0:T(8,128)(2,1)S(1)}, u32[]{:S(2)}, u32[]{:S(2)}) async-start(bf16[32,40,128]{2,1,0:T(8,128)(2,1)} %rows.1), calls=%async_computation.2 | async-start | bytes 655360 | tf_op jit(solution)/shard_map/all_to_all | solution.py:1214
  45.4 0.0 copy-done.1
  45.4 0.0 copy-done.6
  45.4 0.9 %pick.1.refs_0_ = bf16[3,2,64,512]{3,2,1,0:T(8,128)(2,1)S(1)} custom-call(f32[2,64,512]{2,1,0:T(8,128)S(1)} %copy-done.1, bf16[8,112,128]{2,1,0:T(8,128)(2,1)S(1)} %all-to-all-done.rows_ref.slab_ref, bf16[32,40,128]{2,1,0:T(8,128)(2,1)S(1)} %all-to-all-done.1.refs_0_.arrived_ref, s32[4,512]{1,0:T(4,128)S(1)} %copy-done.6), custom_call_target="tpu_custom_call" | custom-call | tf_op jit(solution)/shard_map/pick/pallas_call | solution.py:1215
  46.3 0.0 copy-start.5
  46.3 3.7 %near.4.refs_1_ = f32[2,64,512]{2,1,0:T(8,128)S(1)} custom-call(bf16[3,2,64,512]{3,2,1,0:T(8,128)(2,1)S(1)} %pick.1.refs_0_, f32[2,64,512]{2,1,0:T(8,128)S(1)} %near.3.refs_1_, bf16[4,64,64,512]{3,2,1,0:T(8,128)(2,1)} %refs_2_.3), custom_call_target="tpu_custom_call" | custom-call | tf_op jit(solution)/shard_map/near/pallas_call | solution.py:1116
  50.0 7.4 %all-to-all-done.2.in_ref = bf16[32,40,128]{2,1,0:T(8,128)(2,1)S(1)} async-done(((bf16[32,40,128]{2,1,0:T(8,128)(2,1)}), bf16[32,40,128]{2,1,0:T(8,128)(2,1)S(1)}, u32[]{:S(2)}, u32[]{:S(2)}) %all-to-all-start.2) | async-done | bytes 327712 | tf_op jit(solution)/shard_map/all_to_all | solution.py:1214
  57.4 1.6 %grid.1 = bf16[8,80,128]{2,1,0:T(8,128)(2,1)} custom-call(bf16[32,40,128]{2,1,0:T(8,128)(2,1)S(1)} %all-to-all-done.2.in_ref, bf16[512,512]{1,0:T(8,128)(2,1)S(1)} %get-tuple-element.37.even_cos, bf16[512,512]{1,0:T(8,128)(2,1)S(1)} %get-tuple-element.38.even_sin, bf16[512,512]{1,0:T(8,128)(2,1)S(1)} %get-tuple-element.39.odd_cos), custom_call_target="tpu_custom_call" | custom-call | tf_op jit(solution)/shard_map/grid/pallas_call | solution.py:1226
  59.0 3.4 %all-to-all-start.3 = ((bf16[8,80,128]{2,1,0:T(8,128)(2,1)}), bf16[8,80,128]{2,1,0:T(8,128)(2,1)S(1)}, u32[]{:S(2)}, u32[]{:S(2)}) async-start(bf16[8,80,128]{2,1,0:T(8,128)(2,1)} %grid.1), calls=%async_computation.3 | async-start | bytes 327680 | tf_op jit(solution)/shard_map/all_to_all | solution.py:1235
  62.4 3.7 %near.5.near_ref = f32[2,64,512]{2,1,0:T(8,128)S(1)} custom-call(bf16[3,2,64,512]{3,2,1,0:T(8,128)(2,1)S(1)} %pick.1.refs_0_, f32[2,64,512]{2,1,0:T(8,128)S(1)} %near.4.refs_1_, bf16[4,64,64,512]{3,2,1,0:T(8,128)(2,1)} %refs_2_.3), custom_call_target="tpu_custom_call" | custom-call | tf_op jit(solution)/shard_map/near/pallas_call | solution.py:1116
  66.1 3.5 %all-to-all-done.3.source_ref = bf16[8,80,128]{2,1,0:T(8,128)(2,1)S(1)} async-done(((bf16[8,80,128]{2,1,0:T(8,128)(2,1)}), bf16[8,80,128]{2,1,0:T(8,128)(2,1)S(1)}, u32[]{:S(2)}, u32[]{:S(2)}) %all-to-all-start.3) | async-done | bytes 163872 | tf_op jit(solution)/shard_map/all_to_all | solution.py:1235
  69.5 0.0 copy-done.5
  69.5 3.7 %far.1 = f32[2,64,512]{2,1,0:T(8,128)} custom-call(bf16[8,80,128]{2,1,0:T(8,128)(2,1)S(1)} %all-to-all-done.3.source_ref, bf16[64,64,512]{2,1,0:T(8,128)(2,1)} %projection_ref.3, s32[2,512]{1,0:T(2,128)S(1)} %copy-done.5, f32[2,64,512]{2,1,0:T(8,128)S(1)} %near.5.near_ref), custom_call_target="tpu_custom_call" | custom-call | tf_op jit(solution)/shard_map/far/pallas_call | solution.py:1238
Async XLA Ops:
  0.0 30.6 %copy-start.4 = (f32[160,512]{1,0:T(8,128)S(1)}, f32[160,512]{1,0:T(8,128)}, u32[]{:S(2)}) copy-start(f32[160,512]{1,0:T(8,128)} %constant.7.clone.position_ref) | copy-start | bytes 983044
  0.0 45.4 %copy-start.1 = (f32[2,64,512]{2,1,0:T(8,128)S(1)}, f32[2,64,512]{2,1,0:T(8,128)}, u32[]{:S(2)}) copy-start(f32[2,64,512]{2,1,0:T(8,128)} %currents_ref.2) | copy-start | bytes 786436
  0.0 45.4 %copy-start.6 = (s32[4,512]{1,0:T(4,128)S(1)}, s32[4,512]{1,0:T(4,128)}, u32[]{:S(2)}) copy-start(s32[4,512]{1,0:T(4,128)} %partners_ref.1) | copy-start | bytes 24580
  5.8 15.4 %all-to-all-start = ((bf16[8,112,128]{2,1,0:T(8,128)(2,1)}), bf16[8,112,128]{2,1,0:T(8,128)(2,1)S(1)}, u32[]{:S(2)}, u32[]{:S(2)}) async-start(bf16[8,112,128]{2,1,0:T(8,128)(2,1)} %charges.1), calls=%async_computation | async-start | bytes 458752 | tf_op jit(solution)/shard_map/all_to_all | solution.py:1171
  12.1 1.0 %copy-start.3 = (f32[160,512]{1,0:T(8,128)S(1)}, f32[160,512]{1,0:T(8,128)}, u32[]{:S(2)}) copy-start(f32[160,512]{1,0:T(8,128)} %constant.6.clone.bases_ref) | copy-start | bytes 983044
  23.3 15.6 %all-to-all-start.1 = ((bf16[32,40,128]{2,1,0:T(8,128)(2,1)}), bf16[32,40,128]{2,1,0:T(8,128)(2,1)S(1)}, u32[]{:S(2)}, u32[]{:S(2)}) async-start(bf16[32,40,128]{2,1,0:T(8,128)(2,1)} %columns.1), calls=%async_computation.1 | async-start | bytes 655360 | tf_op jit(solution)/shard_map/all_to_all | solution.py:1191
  26.8 1.0 %copy-start = (f32[2,64,512]{2,1,0:T(8,128)S(1)}, f32[2,64,512]{2,1,0:T(8,128)}, u32[]{:S(2)}) copy-start(f32[2,64,512]{2,1,0:T(8,128)} %currents_ref.2) | copy-start | bytes 786436
  34.9 0.8 %copy-start.2 = (bf16[512,512]{1,0:T(8,128)(2,1)}, bf16[512,512]{1,0:T(8,128)(2,1)S(1)}, u32[]{:S(2)}) copy-start(bf16[512,512]{1,0:T(8,128)(2,1)S(1)} %get-tuple-element.52.refs_1_) | copy-start | bytes 1572868
  42.7 14.7 %all-to-all-start.2 = ((bf16[32,40,128]{2,1,0:T(8,128)(2,1)}), bf16[32,40,128]{2,1,0:T(8,128)(2,1)S(1)}, u32[]{:S(2)}, u32[]{:S(2)}) async-start(bf16[32,40,128]{2,1,0:T(8,128)(2,1)} %rows.1), calls=%async_computation.2 | async-start | bytes 655360 | tf_op jit(solution)/shard_map/all_to_all | solution.py:1214
  46.3 23.2 %copy-start.5 = (s32[2,512]{1,0:T(2,128)S(1)}, s32[2,512]{1,0:T(2,128)}, u32[]{:S(2)}) copy-start(s32[2,512]{1,0:T(2,128)} %shifts_ref.3) | copy-start | bytes 12292
  59.0 10.5 %all-to-all-start.3 = ((bf16[8,80,128]{2,1,0:T(8,128)(2,1)}), bf16[8,80,128]{2,1,0:T(8,128)(2,1)S(1)}, u32[]{:S(2)}, u32[]{:S(2)}) async-start(bf16[8,80,128]{2,1,0:T(8,128)(2,1)} %grid.1), calls=%async_computation.3 | async-start | bytes 327680 | tf_op jit(solution)/shard_map/all_to_all | solution.py:1235

commit v7 on v5

--- a/solution.py
+++ b/solution.py
@@ -836,30 +836,18 @@
                 device += 1
 
 
-def row_kernel(row_count, col_count, *refs):
-    sources, out_ref, held, sems = refs[:9], refs[9], refs[10:19], refs[19]
-    loads = [
-        pltpu.make_async_copy(source, target, sems.at[n])
-        for n, (source, target) in enumerate(zip(sources, held))
-    ]
-    for load in loads:
-        load.start()
-    in_ref, even_cos, even_sin, odd_cos, back_cos, back_sin, back_odd, sum_ref, diff_ref = held
-    loads[0].wait()
+def row_kernel(row_count, col_count, in_ref, even_cos, even_sin, odd_cos, back_cos, back_sin, back_odd,
+               sum_ref, diff_ref, out_ref):
     even, odd = add_outer_rows(
         lambda i, j: in_ref[i * col_count + j].astype(jnp.float32), row_count, col_count
     )
     flip = jnp.where((sub_index(odd.shape) & 4) == 0, 1.0, -1.0)
     both = jnp.concatenate([odd, odd * flip], axis=1).astype(jnp.bfloat16)
     even = even.astype(jnp.bfloat16)
-    for n in range(1, 4):
-        loads[n].wait()
     a = [dot(even_cos[...], even), dot(even_sin[...], even)]
     both = dot(odd_cos[...], both)
     b = [both[:, :LANES], both[:, LANES:]]
     quarter = odd.shape[0]
-    for n in range(4, 9):
-        loads[n].wait()
 
     def pieces(left, right):
         for k in range(2):
@@ -1198,12 +1186,8 @@
     rows_back = pl.pallas_call(
         functools.partial(row_kernel, row_count, col_count),
         out_shape=struct((devices, 40, LANES), b16),
-        in_specs=[ON_CHIP] + [IN_PLACE] * 8,
+        in_specs=[ON_CHIP] * 9,
         out_specs=ON_CHIP,
-        scratch_shapes=[pltpu.VMEM((devices, 40, LANES), b16)]
-        + [pltpu.VMEM((quarter, quarter), b16)] * 6
-        + [pltpu.VMEM((2 * quarter, LANES), f32)] * 2
-        + [pltpu.SemaphoreType.DMA((9,))],
         compiler_params=FULL_PARAMS,
         name="rows",
     )(arrived, *row_tables)

time: 73.4 us -> 73.7 us (level)
  no operation moved by 1% of the time
where the time goes in v7:
time: 73.7 us; the launch traced here: 73.2 us
  Pallas kernels  33 us (45%)
  waiting for transfers between devices  21.3 us (29%)
  starting transfers between devices  16 us (22%)
  local copies, waits for them, and re-layouts  2.74 us (4%)
    pallas_call x3, Pallas kernels, near_call(): pl.pallas_call(functools.partial(near_kernel, total is not None, slots, s...  10.1 us
    all_to_all x1, waiting for transfers between devices, shards_real(): returned = lax.all_to_all(rows_back, ('row', 'col'), 0, 0, tiled=True)  7.4 us
    all_to_all x1, waiting for transfers between devices, shards_real(): slab = lax.all_to_all(charges, 'col', 0, 0, tiled=True)  7.31 us
    all_to_all x1, starting transfers between devices, shards_real(): slab = lax.all_to_all(charges, 'col', 0, 0, tiled=True)  6.37 us
    pallas_call x1, Pallas kernels, shards_real(): pl.pallas_call(charge_kernel, in_specs=[IN_PLACE] * 3, out_specs=ON_CHIP,...  5.39 us
    pallas_call x1, Pallas kernels, shards_real(): pl.pallas_call(row_table_kernel, out_shape=[table] * 6 + [spread] * 2, co...  4.33 us
    pallas_call x1, Pallas kernels, shards_real(): pl.pallas_call(functools.partial(row_kernel, row_count, col_count), out_s...  4.12 us
    pallas_call x1, Pallas kernels, shards_real(): pl.pallas_call(far_kernel, in_specs=[ON_CHIP, IN_PLACE, IN_PLACE, ON_CHIP...  3.69 us
  transfers between devices with their start and end apart: 4, of which 4 were waited for; matrix products, arithmetic and copies ran while one was open for 0% of the time, Pallas kernels for 22%

profile of v7, /device:TPU:0, one launch (start us, length us, event | category | flops | bytes accessed | tf_op | source)
XLA Modules:
  0.0 73.2 jit_solution(3894692527755105696)
XLA Ops:
  0.0 0.0 copy-start.4
  0.0 0.0 copy-start.1
  0.0 0.0 copy-start.6
  0.0 5.4 %charges.1 = bf16[8,112,128]{2,1,0:T(8,128)(2,1)} custom-call(f32[2,64,512]{2,1,0:T(8,128)} %currents_ref.2, bf16[64,64,512]{2,1,0:T(8,128)(2,1)} %projection_ref.3, s32[2,512]{1,0:T(2,128)} %shifts_ref.3), custom_call_target="tpu_custom_call" | custom-call | tf_op jit(solution)/shard_map/charges/pallas_call | solution.py:1139
  5.4 6.4 %all-to-all-start = ((bf16[8,112,128]{2,1,0:T(8,128)(2,1)}), bf16[8,112,128]{2,1,0:T(8,128)(2,1)S(1)}, u32[]{:S(2)}, u32[]{:S(2)}) async-start(bf16[8,112,128]{2,1,0:T(8,128)(2,1)} %charges.1), calls=%async_computation | async-start | bytes 458752 | tf_op jit(solution)/shard_map/all_to_all | solution.py:1156
  11.8 0.0 copy-start.3
  11.8 1.0 %copy-done.3 = f32[160,512]{1,0:T(8,128)S(1)} copy-done((f32[160,512]{1,0:T(8,128)S(1)}, f32[160,512]{1,0:T(8,128)}, u32[]{:S(2)}) %copy-start.3) | copy-done | bytes 327704
  12.7 0.7 column_tables.1
  13.5 7.3 %all-to-all-done.rows_ref.slab_ref = bf16[8,112,128]{2,1,0:T(8,128)(2,1)S(1)} async-done(((bf16[8,112,128]{2,1,0:T(8,128)(2,1)}), bf16[8,112,128]{2,1,0:T(8,128)(2,1)S(1)}, u32[]{:S(2)}, u32[]{:S(2)}) %all-to-all-start) | async-done | bytes 229408 | tf_op jit(solution)/shard_map/all_to_all | solution.py:1156
  20.8 2.1 %columns.1 = bf16[32,40,128]{2,1,0:T(8,128)(2,1)} custom-call(bf16[8,112,128]{2,1,0:T(8,128)(2,1)S(1)} %all-to-all-done.rows_ref.slab_ref, bf16[512,512]{1,0:T(8,128)(2,1)S(1)} %get-tuple-element.37.even_cos, bf16[512,512]{1,0:T(8,128)(2,1)S(1)} %get-tuple-element.38.even_sin, bf16[512,512]{1,0:T(8,128)(2,1)S(1)} %get-tuple-element.39.odd_cos), custom_call_target="tpu_custom_call" | custom-call | tf_op jit(solution)/shard_map/columns/pallas_call | solution.py:1167
  22.9 3.5 %all-to-all-start.1 = ((bf16[32,40,128]{2,1,0:T(8,128)(2,1)}), bf16[32,40,128]{2,1,0:T(8,128)(2,1)S(1)}, u32[]{:S(2)}, u32[]{:S(2)}) async-start(bf16[32,40,128]{2,1,0:T(8,128)(2,1)} %columns.1), calls=%async_computation.1 | async-start | bytes 655360 | tf_op jit(solution)/shard_map/all_to_all | solution.py:1176
  26.5 0.0 copy-start
  26.5 0.9 %copy-done = f32[2,64,512]{2,1,0:T(8,128)S(1)} copy-done((f32[2,64,512]{2,1,0:T(8,128)S(1)}, f32[2,64,512]{2,1,0:T(8,128)}, u32[]{:S(2)}) %copy-start) | copy-done | bytes 262168
  27.4 2.8 %near.3.refs_1_ = f32[2,64,512]{2,1,0:T(8,128)S(1)} custom-call(f32[2,64,512]{2,1,0:T(8,128)S(1)} %copy-done, bf16[4,64,64,512]{3,2,1,0:T(8,128)(2,1)} %refs_2_.3), custom_call_target="tpu_custom_call" | custom-call | tf_op jit(solution)/shard_map/near/pallas_call | solution.py:1101
  30.2 0.0 copy-done.4
  30.2 4.3 %row_tables.1 = (bf16[512,512]{1,0:T(8,128)(2,1)S(1)}, bf16[512,512]{1,0:T(8,128)(2,1)}, bf16[512,512]{1,0:T(8,128)(2,1)}, bf16[512,512]{1,0:T(8,128)(2,1)}, bf1...) custom-call(f32[64,2048]{1,0:T(8,128)} %green_ref, ...), custom_call_target="tpu_custom_call" | custom-call | tf_op jit(solution)/shard_map/row_tables/pallas_call | solution.py:1179
  34.5 0.0 copy-start.2
  34.5 0.8 %copy-done.2 = bf16[512,512]{1,0:T(8,128)(2,1)} copy-done((bf16[512,512]{1,0:T(8,128)(2,1)}, bf16[512,512]{1,0:T(8,128)(2,1)S(1)}, u32[]{:S(2)}) %copy-start.2) | copy-done | bytes 524312
  35.4 3.1 %all-to-all-done.1.in_ref.arrived_ref = bf16[32,40,128]{2,1,0:T(8,128)(2,1)S(1)} async-done(((bf16[32,40,128]{2,1,0:T(8,128)(2,1)}), bf16[32,40,128]{2,1,0:T(8,128)(2,1)S(1)}, u32[]{:S(2)}, u32[]{:S(2)}) %all-to-all-start.1) | async-done | bytes 327712 | tf_op jit(solution)/shard_map/all_to_all | solution.py:1176
  38.5 4.1 %rows.1 = bf16[32,40,128]{2,1,0:T(8,128)(2,1)} custom-call(bf16[32,40,128]{2,1,0:T(8,128)(2,1)S(1)} %all-to-all-done.1.in_ref.arrived_ref, bf16[512,512]{1,0:T(8,128)(2,1)} %copy-done.2, bf16[512,512]{1,0:T(8,128)(2,1)} %get-tuple-element.53.even_sin, bf16[512,512]{1,0:T(8,128)(2,1)} %get-tuple-element.54.odd_cos, ...), custom_call_target="tpu_custom_call" | custom-call | tf_op jit(solution)/shard_map/rows/pallas_call | solution.py:1186
  42.6 2.7 %all-to-all-start.2 = ((bf16[32,40,128]{2,1,0:T(8,128)(2,1)}), bf16[32,40,128]{2,1,0:T(8,128)(2,1)S(1)}, u32[]{:S(2)}, u32[]{:S(2)}) async-start(bf16[32,40,128]{2,1,0:T(8,128)(2,1)} %rows.1), calls=%async_computation.2 | async-start | bytes 655360 | tf_op jit(solution)/shard_map/all_to_all | solution.py:1195
  45.3 0.0 copy-done.1
  45.3 0.0 copy-done.6
  45.3 0.9 %pick.1.refs_0_ = bf16[3,2,64,512]{3,2,1,0:T(8,128)(2,1)S(1)} custom-call(f32[2,64,512]{2,1,0:T(8,128)S(1)} %copy-done.1, bf16[8,112,128]{2,1,0:T(8,128)(2,1)S(1)} %all-to-all-done.rows_ref.slab_ref, bf16[32,40,128]{2,1,0:T(8,128)(2,1)S(1)} %all-to-all-done.1.in_ref.arrived_ref, s32[4,512]{1,0:T(4,128)S(1)} %copy-done.6), custom_call_target="tpu_custom_call" | custom-call | tf_op jit(solution)/shard_map/pick/pallas_call | solution.py:1196
  46.3 0.0 copy-start.5
  46.3 3.7 %near.4.refs_1_ = f32[2,64,512]{2,1,0:T(8,128)S(1)} custom-call(bf16[3,2,64,512]{3,2,1,0:T(8,128)(2,1)S(1)} %pick.1.refs_0_, f32[2,64,512]{2,1,0:T(8,128)S(1)} %near.3.refs_1_, bf16[4,64,64,512]{3,2,1,0:T(8,128)(2,1)} %refs_2_.3), custom_call_target="tpu_custom_call" | custom-call | tf_op jit(solution)/shard_map/near/pallas_call | solution.py:1101
  49.9 7.4 %all-to-all-done.2.in_ref = bf16[32,40,128]{2,1,0:T(8,128)(2,1)S(1)} async-done(((bf16[32,40,128]{2,1,0:T(8,128)(2,1)}), bf16[32,40,128]{2,1,0:T(8,128)(2,1)S(1)}, u32[]{:S(2)}, u32[]{:S(2)}) %all-to-all-start.2) | async-done | bytes 327712 | tf_op jit(solution)/shard_map/all_to_all | solution.py:1195
  57.3 1.6 %grid.1 = bf16[8,80,128]{2,1,0:T(8,128)(2,1)} custom-call(bf16[32,40,128]{2,1,0:T(8,128)(2,1)S(1)} %all-to-all-done.2.in_ref, bf16[512,512]{1,0:T(8,128)(2,1)S(1)} %get-tuple-element.37.even_cos, bf16[512,512]{1,0:T(8,128)(2,1)S(1)} %get-tuple-element.38.even_sin, bf16[512,512]{1,0:T(8,128)(2,1)S(1)} %get-tuple-element.39.odd_cos), custom_call_target="tpu_custom_call" | custom-call | tf_op jit(solution)/shard_map/grid/pallas_call | solution.py:1207
  59.0 3.4 %all-to-all-start.3 = ((bf16[8,80,128]{2,1,0:T(8,128)(2,1)}), bf16[8,80,128]{2,1,0:T(8,128)(2,1)S(1)}, u32[]{:S(2)}, u32[]{:S(2)}) async-start(bf16[8,80,128]{2,1,0:T(8,128)(2,1)} %grid.1), calls=%async_computation.3 | async-start | bytes 327680 | tf_op jit(solution)/shard_map/all_to_all | solution.py:1216
  62.4 3.7 %near.5.near_ref = f32[2,64,512]{2,1,0:T(8,128)S(1)} custom-call(bf16[3,2,64,512]{3,2,1,0:T(8,128)(2,1)S(1)} %pick.1.refs_0_, f32[2,64,512]{2,1,0:T(8,128)S(1)} %near.4.refs_1_, bf16[4,64,64,512]{3,2,1,0:T(8,128)(2,1)} %refs_2_.3), custom_call_target="tpu_custom_call" | custom-call | tf_op jit(solution)/shard_map/near/pallas_call | solution.py:1101
  66.0 3.5 %all-to-all-done.3.source_ref = bf16[8,80,128]{2,1,0:T(8,128)(2,1)S(1)} async-done(((bf16[8,80,128]{2,1,0:T(8,128)(2,1)}), bf16[8,80,128]{2,1,0:T(8,128)(2,1)S(1)}, u32[]{:S(2)}, u32[]{:S(2)}) %all-to-all-start.3) | async-done | bytes 163872 | tf_op jit(solution)/shard_map/all_to_all | solution.py:1216
  69.5 0.0 copy-done.5
  69.5 3.7 %far.1 = f32[2,64,512]{2,1,0:T(8,128)} custom-call(bf16[8,80,128]{2,1,0:T(8,128)(2,1)S(1)} %all-to-all-done.3.source_ref, bf16[64,64,512]{2,1,0:T(8,128)(2,1)} %projection_ref.3, s32[2,512]{1,0:T(2,128)S(1)} %copy-done.5, f32[2,64,512]{2,1,0:T(8,128)S(1)} %near.5.near_ref), custom_call_target="tpu_custom_call" | custom-call | tf_op jit(solution)/shard_map/far/pallas_call | solution.py:1219
Async XLA Ops:
  0.0 30.2 %copy-start.4 = (f32[160,512]{1,0:T(8,128)S(1)}, f32[160,512]{1,0:T(8,128)}, u32[]{:S(2)}) copy-start(f32[160,512]{1,0:T(8,128)} %constant.7.clone.position_ref) | copy-start | bytes 983044
  0.0 45.3 %copy-start.1 = (f32[2,64,512]{2,1,0:T(8,128)S(1)}, f32[2,64,512]{2,1,0:T(8,128)}, u32[]{:S(2)}) copy-start(f32[2,64,512]{2,1,0:T(8,128)} %currents_ref.2) | copy-start | bytes 786436
  0.0 45.3 %copy-start.6 = (s32[4,512]{1,0:T(4,128)S(1)}, s32[4,512]{1,0:T(4,128)}, u32[]{:S(2)}) copy-start(s32[4,512]{1,0:T(4,128)} %partners_ref.1) | copy-start | bytes 24580
  5.4 15.4 %all-to-all-start = ((bf16[8,112,128]{2,1,0:T(8,128)(2,1)}), bf16[8,112,128]{2,1,0:T(8,128)(2,1)S(1)}, u32[]{:S(2)}, u32[]{:S(2)}) async-start(bf16[8,112,128]{2,1,0:T(8,128)(2,1)} %charges.1), calls=%async_computation | async-start | bytes 458752 | tf_op jit(solution)/shard_map/all_to_all | solution.py:1156
  11.8 1.0 %copy-start.3 = (f32[160,512]{1,0:T(8,128)S(1)}, f32[160,512]{1,0:T(8,128)}, u32[]{:S(2)}) copy-start(f32[160,512]{1,0:T(8,128)} %constant.6.clone.bases_ref) | copy-start | bytes 983044
  22.9 15.6 %all-to-all-start.1 = ((bf16[32,40,128]{2,1,0:T(8,128)(2,1)}), bf16[32,40,128]{2,1,0:T(8,128)(2,1)S(1)}, u32[]{:S(2)}, u32[]{:S(2)}) async-start(bf16[32,40,128]{2,1,0:T(8,128)(2,1)} %columns.1), calls=%async_computation.1 | async-start | bytes 655360 | tf_op jit(solution)/shard_map/all_to_all | solution.py:1176
  26.5 1.0 %copy-start = (f32[2,64,512]{2,1,0:T(8,128)S(1)}, f32[2,64,512]{2,1,0:T(8,128)}, u32[]{:S(2)}) copy-start(f32[2,64,512]{2,1,0:T(8,128)} %currents_ref.2) | copy-start | bytes 786436
  34.5 0.8 %copy-start.2 = (bf16[512,512]{1,0:T(8,128)(2,1)}, bf16[512,512]{1,0:T(8,128)(2,1)S(1)}, u32[]{:S(2)}) copy-start(bf16[512,512]{1,0:T(8,128)(2,1)S(1)} %get-tuple-element.52.even_cos) | copy-start | bytes 1572868
  42.6 14.7 %all-to-all-start.2 = ((bf16[32,40,128]{2,1,0:T(8,128)(2,1)}), bf16[32,40,128]{2,1,0:T(8,128)(2,1)S(1)}, u32[]{:S(2)}, u32[]{:S(2)}) async-start(bf16[32,40,128]{2,1,0:T(8,128)(2,1)} %rows.1), calls=%async_computation.2 | async-start | bytes 655360 | tf_op jit(solution)/shard_map/all_to_all | solution.py:1195
  46.3 23.2 %copy-start.5 = (s32[2,512]{1,0:T(2,128)S(1)}, s32[2,512]{1,0:T(2,128)}, u32[]{:S(2)}) copy-start(s32[2,512]{1,0:T(2,128)} %shifts_ref.3) | copy-start | bytes 12292
  59.0 10.5 %all-to-all-start.3 = ((bf16[8,80,128]{2,1,0:T(8,128)(2,1)}), bf16[8,80,128]{2,1,0:T(8,128)(2,1)S(1)}, u32[]{:S(2)}, u32[]{:S(2)}) async-start(bf16[8,80,128]{2,1,0:T(8,128)(2,1)} %grid.1), calls=%async_computation.3 | async-start | bytes 327680 | tf_op jit(solution)/shard_map/all_to_all | solution.py:1216
